TPU v7x, 128 devices: a whole 4x4x4 slice. The times are simulated.
128 devices in a mesh: section: 4 (over z_hi, core), dp: 32 (over z_lo, y, x).
Axes of the slice: x: 4, y: 4, z: 4 (z_hi: 2, z_lo: 2; z = z_hi * 2 + z_lo), core: 2. Of those that a mesh axis runs over, the one named last changes fastest.
Arguments:
- value_weight: bfloat16 [4, 8192, 1024], P('section', 'dp'), may hold values from -0.0625 to 0.0625
- norm_gain: bfloat16 [4, 8192], P('section'), may hold values from 0.25 to 1.75
- mask_logits: bfloat16 [4, 6, 2048, 1024], P('section', None, 'dp'), may hold values from -5 to 5
- gumbel_noise: bfloat16 [4, 6, 2048, 1024], P('section', None, 'dp'), may hold values from -2.23 to 9.22, as said below
- stream_in: bfloat16 [2, 2048, 8192], P(None, 'dp'), may hold values from -6 to 6
- stream_grad: bfloat16 [2, 2048, 8192], P(None, 'dp'), may hold values from -6 to 6
Outputs:
- logit_grad: bfloat16 [4, 6, 2048, 1024], P('section', None, 'dp')
Inputs may be any that keep to these rules, and one draw needn't show every extreme that they name: `gumbel_noise`: gumbel noise, minus the log of minus the log of a uniform number.
All inputs are finite; a program needn't handle non-finite values.
Results may differ from a plain program's by a relative error of at most 0.029.
Values may be sent and summed in bfloat16 or wider, within the bound.
No kernel may reach another device: no remote copies, remote signals or barrier semaphores. Data moves between devices by JAX's collectives and lax.ppermute only.
A program may use at most 128 MiB of HBM per device.

v0:
```python
import functools

import jax
import jax.numpy as jnp
from jax import lax
from jax.experimental import pallas as pl
from jax.experimental.pallas import tpu as pltpu
from jax.sharding import Mesh
from jax.sharding import PartitionSpec as P


VHEADS = 8
sharpness_divisor = 0.6666667
epsilon = 1e-05
BF = jnp.bfloat16
F32 = jnp.float32
CHUNKS = 2
INTERPRET = False
KEEPS = ((0, 1), (0, 2), (0, 3), (1, 2), (1, 3), (2, 3))
LAYER = ("zh", "co")


def shape(dims, dtype):
    return jax.ShapeDtypeStruct(dims, dtype)


def call(kernel, out, **rest):
    params = pltpu.CompilerParams(vmem_limit_bytes=20 << 20)
    return pl.pallas_call(kernel, out_shape=out, interpret=INTERPRET, compiler_params=params, **rest)


def tiles(width, most=128):
    step = min(width, most)
    return [slice(i, i + step) for i in range(0, width, step)]


def by_tile(rows, width, most=128):
    cols = tiles(width, min(most, 128))
    return pltpu.VMEM((len(cols), rows, cols[0].stop), F32)


def mask_kernel(at, logits, noise, weight, gain, probs, scaled, q0, q1, q2, q3, rows):
    for i, s in enumerate(tiles(weight.shape[1])):
        expo = [
            jnp.exp((logits[k, :, s].astype(F32) + noise[k, :, s].astype(F32)) * (1.0 / sharpness_divisor))
            for k in range(6)
        ]
        inverse = 1.0 / (((expo[0] + expo[1]) + (expo[2] + expo[3])) + (expo[4] + expo[5]))
        p = [e * inverse for e in expo]
        for k in range(6):
            probs[k, :, s] = p[k]
        for r in range(4):
            kept = [p[k] for k in range(6) if r in KEEPS[k]]
            rows.at[i][pl.ds(r, kept[0].shape[0], stride=4), :] = kept[0] + kept[1] + kept[2]
        value = weight[:, s].astype(F32) * rows[i] * gain[...]
        scaled[:, s] = value.astype(BF)
        rows[i] = value
        quarter = q0.shape[0]
        for k, q in enumerate((q0, q1, q2, q3)):
            begin = pl.multiple_of(lax.rem(at[0] + k, 4) * quarter, quarter)
            one = rows.at[i][pl.ds(begin, quarter), :]
            two = rows.at[i][pl.ds(begin + 4 * quarter, quarter), :]
            q[:, s] = (one + two).astype(BF)


def masked_weights(at, logits, noise, weight, gain):
    n, kv = weight.shape
    return call(
        mask_kernel,
        (shape(logits.shape, F32), shape((n, kv), BF)) + (shape((n // 8, kv), BF),) * 4,
        in_specs=[pl.BlockSpec(memory_space=pltpu.SMEM)] + [pl.BlockSpec(memory_space=pltpu.VMEM)] * 4,
        scratch_shapes=[by_tile(n, kv)],
    )(at, logits, noise, weight, gain)


def final_kernel(probs, weight, gain, *refs):
    parts, out, rows = refs[:-2], refs[-2], refs[-1]
    kv = weight.shape[1]
    wide = parts[0].shape[1]
    for i, s in enumerate(tiles(kv, min(wide, 128))):
        j, at = divmod(s.start, wide)
        inner = slice(at, at + s.stop - s.start)
        mine = parts[j * 4 : j * 4 + 4]
        total = (mine[0][:, inner].astype(F32) + mine[1][:, inner].astype(F32)) + (
            mine[2][:, inner].astype(F32) + mine[3][:, inner].astype(F32)
        )
        rows[i] = total * gain[...] * weight[:, s].astype(F32) * (1.0 / sharpness_divisor)
        d = [rows.at[i][pl.ds(r, probs.shape[1], stride=4), :] for r in range(4)]
        p = [probs[k, :, s] for k in range(6)]
        dprob = [d[a] + d[b] for a, b in KEEPS]
        mean = p[0] * dprob[0]
        for k in range(1, 6):
            mean = mean + p[k] * dprob[k]
        for k in range(6):
            out[k, :, s] = (p[k] * (dprob[k] - mean)).astype(BF)


def logit_gradient(probs, weight, gain, parts):
    return call(
        final_kernel,
        shape(probs.shape, BF),
        scratch_shapes=[by_tile(*weight.shape, most=parts[0].shape[1])],
    )(probs, weight, gain, *parts)


def sums_kernel(repeat, head, core, tokens, grads, y0, spread, g4, mine):
    t = tokens[0]
    mine[0] = t
    pieces = [t[:, r * head : (r + 1) * head].astype(F32) for r in range(repeat)]
    total = functools.reduce(lambda a, b: a + b, pieces)
    mean = total * (1.0 / repeat)
    squares = functools.reduce(lambda a, b: a + b, [(p - mean) * (p - mean) for p in pieces])
    y0[...] = total

    @pl.when(pl.program_id(0) == 0)
    def _():
        spread[...] = squares

    @pl.when(pl.program_id(0) != 0)
    def _():
        spread[...] += squares

    g = grads[0]
    g4[...] = functools.reduce(
        lambda a, b: a + b, [g[:, r * head : (r + 1) * head].astype(F32) for r in range(repeat)]
    )


def token_sums(core, tokens, grads, head):
    rows, width = tokens.shape[1:]
    span = width // VHEADS
    block = pl.BlockSpec((1, rows, span), lambda h, core: (core[0], 0, h))
    narrow = pl.BlockSpec((rows, head), lambda h, core: (0, h))
    return call(
        functools.partial(sums_kernel, span // head, head),
        (
            shape((rows, VHEADS * head), F32),
            shape((rows, head), F32),
            shape((rows, VHEADS * head), F32),
            shape((VHEADS, rows, span), tokens.dtype),
        ),
        grid_spec=pltpu.PrefetchScalarGridSpec(
            num_scalar_prefetch=1,
            grid=(VHEADS,),
            in_specs=[block, block],
            out_specs=(
                narrow,
                pl.BlockSpec((rows, head), lambda h, core: (0, 0)),
                narrow,
                pl.BlockSpec((1, rows, span), lambda h, core: (h, 0, 0)),
            ),
        ),
    )(core, tokens, grads)


def values_kernel(at, core, own, other, w0, w1, w3, top, bottom, u):
    part = w0.shape[0]
    mine = core[0] == pl.program_id(0) // 2
    total = None
    opposite = jnp.concatenate([top[...], bottom[...]], 0)
    for k, w in enumerate((w0, w1, opposite, w3)):
        cols = pl.ds(pl.multiple_of(lax.rem(at[0] - k + 4, 4) * part, part), part)
        tokens = jnp.where(mine, own[:, cols], other[:, cols])
        term = jnp.dot(tokens, w[...], preferred_element_type=F32)
        total = term if total is None else total + term
    u[...] = total.astype(BF)


def turn_over_kernel(core, own, other, turned):
    turned[...] = jnp.where(core[0] == pl.program_id(0) // 2, own[...], other[...]).T


def partial_values(at, core, own, other, blocks):
    count, span = own.shape
    kv = blocks[0].shape[1]
    step = count // 2
    tokens = pl.BlockSpec((step, span), lambda i, at, core: (i % 2, 0))
    return call(
        values_kernel,
        shape((2 * count, kv), BF),
        grid_spec=pltpu.PrefetchScalarGridSpec(
            num_scalar_prefetch=2,
            grid=(4,),
            in_specs=[tokens, tokens]
            + [pl.BlockSpec(b.shape, lambda i, at, core: (0, 0)) for b in blocks],
            out_specs=pl.BlockSpec((step, kv), lambda i, at, core: (i, 0)),
        ),
    )(at, core, own, other, *blocks)


def turn_over(core, own, other):
    count, span = own.shape
    step = count // 2
    tokens = pl.BlockSpec((step, span), lambda i, core: (i % 2, 0))
    return call(
        turn_over_kernel,
        shape((span, 2 * count), BF),
        grid_spec=pltpu.PrefetchScalarGridSpec(
            num_scalar_prefetch=1,
            grid=(4,),
            in_specs=[tokens, tokens],
            out_specs=pl.BlockSpec((span, step), lambda i, core: (0, i)),
        ),
    )(core, own, other)


def short_kernel(q0, q1, q2, q3, out):
    total = (q0[...].astype(F32) + q1[...].astype(F32)) + (q2[...].astype(F32) + q3[...].astype(F32))
    out[...] = jnp.broadcast_to(total.astype(BF), out.shape)


def short_weights(quarters):
    return call(short_kernel, shape((VHEADS, *quarters[0].shape), BF))(*quarters)


def square_kernel(at, n0, n1, n2, n3, out):
    heads, quarter = n0.shape[:2]
    for k, n in enumerate((n0, n1, n2, n3)):
        source = lax.rem(at[0] - k + 4, 4)
        for h in range(heads):
            begin = pl.multiple_of(h * 4 * quarter + source * quarter, quarter)
            out[pl.ds(begin, quarter), :] = n[h]


def square_weights(at, blocks):
    kv = blocks[0].shape[2]
    return call(
        square_kernel,
        shape((kv, kv), BF),
        in_specs=[pl.BlockSpec(memory_space=pltpu.SMEM)] + [pl.BlockSpec(memory_space=pltpu.VMEM)] * 4,
    )(at, *blocks)


def scale_of(sums, spread, repeat, width):
    mean = jnp.sum(spread, -1, keepdims=True) + jnp.sum(sums * sums, -1, keepdims=True) * (1.0 / repeat)
    return lax.rsqrt(mean * (1.0 / width) + epsilon)


def by_layer(core, layer, own, other, acc, v, dims):
    @pl.when(core == layer)
    def _():
        acc[...] = lax.dot_general(v, own[...], (dims, ((), ())), preferred_element_type=F32)

    @pl.when(core != layer)
    def _():
        acc[...] = lax.dot_general(v, other[...], (dims, ((), ())), preferred_element_type=F32)

    return acc[...]


AHEAD = ((1,), (0,))
BEHIND = ((1,), (1,))


def first_kernel(repeat, width, at, own, other, parts, y0, spread, u, c_out, acc):
    count = parts.shape[0] // 2
    for layer in range(2):
        total = parts[layer * count].astype(F32)
        for i in range(1, count):
            total = total + parts[layer * count + i].astype(F32)
        u[layer] = total
    c = scale_of(y0[...], spread[...], repeat, width) * u[0]
    sums = y0[...] + repeat * c
    value = u[1] + by_layer(at[0], 1, own, other, acc, c.astype(BF), AHEAD)
    c_out[...] = (c + scale_of(sums, spread[...], repeat, width) * value).astype(BF)


def lower_of(width, at, layer, own, other, acc, g, sums, sigma, value):
    vg = g.astype(BF)
    du = by_layer(at[0], layer, own, other, acc, vg, BEHIND)
    dot = jnp.sum(vg.astype(F32) * value, -1, keepdims=True) * (1.0 / width)
    return g + sigma * du - sigma * sigma * dot * sums


def turn_kernel(repeat, width, at, own, other, u, y0, spread, c_in, g4, value, sums, sigma, mid, g_out, acc):
    c = c_in[...]
    base = c.astype(F32)
    for layer in range(2):
        sums[layer] = y0[...] + repeat * base
        s = scale_of(sums[layer], spread[...], repeat, width)
        sigma[layer] = jnp.broadcast_to(s, sigma.shape[1:])
        value[layer] = s * (u[layer] + by_layer(at[0], layer, own, other, acc, c, AHEAD))
        if layer == 0:
            base = base + value[0]
            c = base.astype(BF)
            mid[...] = c
    g = g4[...]
    for layer in (1, 0):
        g = lower_of(width, at, layer, own, other, acc, g, sums[layer], sigma[layer][:, :1], value[layer])
    g_out[...] = g.astype(BF)


def send_kernel(width, kc, at, own, other, g4, g_in, value, sums, sigma, c_in, mid, *outs):
    outs, acc = outs[:-1], outs[-1]
    head = c_in.shape[1] // VHEADS
    g = jnp.where(at[1] == 1, g4[...], g_in[...].astype(F32))
    for layer in (1, 0):
        s = sigma[layer][:, :1]
        sv = (g.astype(BF).astype(F32) * s).astype(BF)
        c = (c_in, mid)[layer]
        for i in range(VHEADS):
            for j, out in enumerate(outs):
                out[layer * VHEADS + i, :, :kc] = sv[:, j * kc : (j + 1) * kc]
            outs[0][layer * VHEADS + i, :, kc:] = c[:, i * head : (i + 1) * head]
        if layer == 1:
            g = lower_of(width, at, 1, own, other, acc, g, sums[1], s, value[1])


def chain_call(kernel, out, at, *args):
    rows, kv = args[2].shape[-2:]
    return call(
        kernel,
        out,
        in_specs=[pl.BlockSpec(memory_space=pltpu.SMEM)] + [pl.BlockSpec(memory_space=pltpu.VMEM)] * len(args),
        scratch_shapes=[pltpu.VMEM((rows, kv), F32)],
    )(at, *args)


def wgrad_kernel(kc, at, turned, right, *outs):
    count = turned.shape[1]
    r = right[...].reshape(count, right.shape[2])
    part = outs[0].shape[0]
    if r.shape[1] > kc:
        c = r[:, kc:].astype(F32).T
        add = jnp.concatenate([c] * (part // c.shape[0]), 0)
    for k in range(4):
        rows = pl.ds(pl.multiple_of(lax.rem(at[0] + k, 4) * part, part), part)
        x = turned[rows, :]
        if r.shape[1] > kc:
            x = (x.astype(F32) + add).astype(BF)
            outs[4][rows, :] = x
        outs[k][...] = jnp.dot(x, r[:, :kc], preferred_element_type=F32).astype(BF)


def wgrad(at, turned, right, kc):
    span, count = turned.shape
    out = [shape((span // 4, kc), BF)] * 4
    if right.shape[2] > kc:
        out.append(shape((span, count), BF))
    return call(
        functools.partial(wgrad_kernel, kc),
        out,
        in_specs=[pl.BlockSpec(memory_space=pltpu.SMEM)] + [pl.BlockSpec(memory_space=pltpu.VMEM)] * 2,
    )(at, turned, right)


def along_x(v, k):
    return v if k == 0 else lax.ppermute(v, "x", [(i, (i + k) % 4) for i in range(4)])


def group(v, axes=("zl", "y")):
    return lax.all_to_all(v, axes, 0, 0, tiled=True)


def per_device(value_weight, norm_gain, mask_logits, gumbel_noise, stream_in, stream_grad):
    zh, co, zl, y, x = (lax.axis_index(n) for n in ("zh", "co", "zl", "y", "x"))
    _, rows, width = stream_in.shape
    kv = value_weight.shape[2]
    head = kv // VHEADS
    repeat = width // kv
    part = value_weight.shape[1]
    span = width // VHEADS
    kc = kv // CHUNKS
    own = zl * 16 + y * 4 + x
    at, core = x.reshape(1), co.reshape(1)
    weight = value_weight[0]
    gain = lax.dynamic_slice_in_dim(norm_gain[0].astype(F32), own * part, part, 0)[:, None]

    probs, scaled, *quarters = masked_weights(at, mask_logits[0], gumbel_noise[0], weight, gain)
    y0, spread, g4, mine = token_sums(core, stream_in, stream_grad, head)
    quarters = [along_x(quarters[k], k) for k in range(4)]
    short = short_weights(quarters)

    mine, scaled = lax.optimization_barrier((mine, scaled))
    before, after = along_x(scaled, 1), along_x(scaled, 3)
    blocks = [scaled, before, after, along_x(before[: part // 2], 1), along_x(after[part // 2 :], 3)]
    got = group(mine)
    swapped = lax.ppermute(got, "co", [(0, 1), (1, 0)])
    got, swapped = got.reshape(-1, span), swapped.reshape(-1, span)
    held = group(short)

    u = partial_values(at, core, got, swapped, blocks)
    u, held = lax.optimization_barrier((u, held))
    parts = group(u.reshape(2 * VHEADS, rows, kv), ("co", "zl", "y"))
    square = [along_x(held, k) for k in range(4)]
    turned = turn_over(core, got, swapped)
    n = square_weights(at, square)
    n_other = lax.ppermute(n, "co", [(0, 1), (1, 0)])

    where = jnp.stack([co, zh])
    two = shape((2, rows, kv), F32)
    half = shape((rows, kv), BF)
    u, c = chain_call(functools.partial(first_kernel, repeat, width), (two, half), where, n, n_other, parts, y0, spread)
    c_in = lax.ppermute(c, "zh", [(0, 1)])
    value, sums, sigma, mid, g = chain_call(
        functools.partial(turn_kernel, repeat, width),
        (two, two, shape((2, rows, head), F32), half, half),
        where, n, n_other, u, y0, spread, c_in, g4,
    )
    g_in = lax.ppermute(g, "zh", [(1, 0)])
    sends = chain_call(
        functools.partial(send_kernel, width, kc),
        tuple(shape((2 * VHEADS, rows, kc + (head if j == 0 else 0)), BF) for j in range(CHUNKS)),
        where, n, n_other, g4, g_in, value, sums, sigma, c_in, mid,
    )

    pieces = []
    for j in range(CHUNKS):
        right = group(sends[j], ("co", "zl", "y"))
        right, *pieces = lax.optimization_barrier((right, *pieces))
        term = wgrad(at, turned, right, kc)
        if j == 0:
            turned = term[4]
        pieces += [along_x(term[k], k) for k in range(4)]
    return logit_gradient(probs, weight, gain, pieces)[None]


def solution(mesh):
    fine = Mesh(mesh.devices.reshape(2, 2, 2, 4, 4), ("zh", "co", "zl", "y", "x"))
    dp = ("zl", "y", "x")

    return jax.shard_map(
        per_device,
        mesh=fine,
        in_specs=(
            P(LAYER, dp, None),
            P(LAYER, None),
            P(LAYER, None, dp, None),
            P(LAYER, None, dp, None),
            P(None, dp, None),
            P(None, dp, None),
        ),
        out_specs=P(LAYER, None, dp, None),
        check_vma=False,
    )
```

profile of v0, /device:TPU:0, one launch (start us, length us, event | category | flops | bytes accessed | tf_op | source)
XLA Modules:
  0.0 235.0 jit_solution(14036323684590793726)
XLA Ops:
  8.5 21.4 %all_to_all.25 = bf16[8,64,1024]{2,1,0:T(8,128)(2,1)S(1)} all-to-all(bf16[8,64,1024]{2,1,0:T(8,128)(2,1)S(1)} %get-tuple-element.45), channel_id=1, replica_groups=mesh['zh'=2,'co'=2,'zl'=2,'y'=4,'x'=4] {'zl','y'}, dimensions={0} | all-to-all | bytes 2097152 | tf_op jit(solution)/shard_map/all_to_all | solution.py:352
  33.5 3.9 %collective-permute-start.6 = (bf16[32,1024]{1,0:T(8,128)(2,1)S(1)}, bf16[32,1024]{1,0:T(8,128)(2,1)S(1)}, u32[]{:S(2)}, u32[]{:S(2)}) collective-permute-start(bf16[32,1024]{1,0:T(8,128)(2,1)S(1)} %get-tuple-element.49), channel_id=1, source_target_pairs={{0,2},{1,3},{2,0},{3,1},{4,6},{5,7},{6,4},{7,5},{8,10},{9,11},{10,... | collective-permute-start | bytes 196616 | tf_op jit(solution)/shard_map/ppermute | solution.py:348
  37.4 13.5 %collective-permute-done.5.q1 = bf16[32,1024]{1,0:T(8,128)(2,1)S(1)} collective-permute-done((bf16[32,1024]{1,0:T(8,128)(2,1)S(1)}, bf16[32,1024]{1,0:T(8,128)(2,1)S(1)}, u32[]{:S(2)}, u32[]{:S(2)}) %collective-permute-start.5) | collective-permute-done | bytes 65568 | tf_op jit(solution)/shard_map/ppermute | solution.py:348
  50.9 4.3 %collective-permute-done.7.q3 = bf16[32,1024]{1,0:T(8,128)(2,1)S(1)} collective-permute-done((bf16[32,1024]{1,0:T(8,128)(2,1)S(1)}, bf16[32,1024]{1,0:T(8,128)(2,1)S(1)}, u32[]{:S(2)}, u32[]{:S(2)}) %collective-permute-start.7) | collective-permute-done | bytes 65568 | tf_op jit(solution)/shard_map/ppermute | solution.py:348
  56.0 3.5 %all-to-all-start.1 = ((bf16[8,32,1024]{2,1,0:T(8,128)(2,1)}), bf16[8,32,1024]{2,1,0:T(8,128)(2,1)S(1)}, u32[]{:S(2)}, u32[]{:S(2)}) async-start(bf16[8,32,1024]{2,1,0:T(8,128)(2,1)} %shard_map.67), calls=%async_computation.1 | async-start | bytes 1048576 | tf_op jit(solution)/shard_map/all_to_all | solution.py:352
  62.7 3.4 %collective-permute-done.4.bottom = bf16[128,1024]{1,0:T(8,128)(2,1)S(1)} collective-permute-done((bf16[128,1024]{1,0:T(8,128)(2,1)S(1)}, bf16[128,1024]{1,0:T(8,128)(2,1)S(1)}, u32[]{:S(2)}, u32[]{:S(2)}) %collective-permute-start.4) | collective-permute-done | bytes 262176 | tf_op jit(solution)/shard_map/ppermute | solution.py:348
  66.1 3.5 %collective-permute-done.3.top = bf16[128,1024]{1,0:T(8,128)(2,1)S(1)} collective-permute-done((bf16[128,1024]{1,0:T(8,128)(2,1)S(1)}, bf16[128,1024]{1,0:T(8,128)(2,1)S(1)}, u32[]{:S(2)}, u32[]{:S(2)}) %collective-permute-start.3) | collective-permute-done | bytes 262176 | tf_op jit(solution)/shard_map/ppermute | solution.py:348
  69.6 4.5 %shard_map.66 = bf16[1024,1024]{1,0:T(8,128)(2,1)S(1)} custom-call(s32[1]{0:T(128)} %bitcast.at, s32[1]{0:T(128)} %bitcast.5.core, bf16[512,1024]{1,0:T(8,128)(2,1)S(1)} %bitcast.12, bf16[512,1024]{1,0:T(8,128)(2,1)S(1)} %bitcast.15, bf16[256,1024]{1,0:T(8,128)(2,1)} %get-tuple-element.46.w0, bf16[256,1024]{1,0:T(8,128)(2,1)} %collective-permute-done.1.w1, ...), custom_call_target="tpu_custom_call" | custom-call | tf_op jit(solution)/shard_map/pallas_call | solution.py:178
  78.3 12.0 %collective-permute-done.10.n3 = bf16[8,32,1024]{2,1,0:T(8,128)(2,1)S(1)} collective-permute-done((bf16[8,32,1024]{2,1,0:T(8,128)(2,1)S(1)}, bf16[8,32,1024]{2,1,0:T(8,128)(2,1)S(1)}, u32[]{:S(2)}, u32[]{:S(2)}) %collective-permute-start.10) | collective-permute-done | bytes 524320 | tf_op jit(solution)/shard_map/ppermute | solution.py:348
  91.7 7.7 %collective-permute-done.8.n1 = bf16[8,32,1024]{2,1,0:T(8,128)(2,1)S(1)} collective-permute-done((bf16[8,32,1024]{2,1,0:T(8,128)(2,1)S(1)}, bf16[8,32,1024]{2,1,0:T(8,128)(2,1)S(1)}, u32[]{:S(2)}, u32[]{:S(2)}) %collective-permute-start.8) | collective-permute-done | bytes 524320 | tf_op jit(solution)/shard_map/ppermute | solution.py:348
  100.7 5.2 %all-to-all-start.2 = ((bf16[16,64,1024]{2,1,0:T(8,128)(2,1)}), bf16[16,64,1024]{2,1,0:T(8,128)(2,1)}, u32[]{:S(2)}, u32[]{:S(2)}) async-start(bf16[16,64,1024]{2,1,0:T(8,128)(2,1)} %bitcast.14), calls=%async_computation.2 | async-start | bytes 4194304 | tf_op jit(solution)/shard_map/all_to_all | solution.py:352
  106.0 29.8 %all-to-all-done.2.parts = bf16[16,64,1024]{2,1,0:T(8,128)(2,1)} async-done(((bf16[16,64,1024]{2,1,0:T(8,128)(2,1)}), bf16[16,64,1024]{2,1,0:T(8,128)(2,1)}, u32[]{:S(2)}, u32[]{:S(2)}) %all-to-all-start.2) | async-done | bytes 2097184 | tf_op jit(solution)/shard_map/all_to_all | solution.py:352
  137.5 3.2 %shard_map.69 = (f32[2,64,1024]{2,1,0:T(8,128)S(1)}, bf16[64,1024]{1,0:T(8,128)(2,1)S(1)}) custom-call(s32[2]{0:T(128)S(1)} %pad_add_fusion.at, bf16[1024,1024]{1,0:T(8,128)(2,1)S(1)} %shard_map.68.own, bf16[1024,1024]{1,0:T(8,128)(2,1)} %collective-permute-done.11.other, bf16[16,64,1024]{2,1,0:T(8,128)(2,1)} %all-to-all-done.2.parts, ...), custom_call_target="tpu_custom_call" | custom-call | tf_op jit(solution)/shard_map/pallas_call | solution.py:311
  140.8 5.5 %collective-permute-start.12 = (bf16[64,1024]{1,0:T(8,128)(2,1)S(1)}, bf16[64,1024]{1,0:T(8,128)(2,1)S(1)}, u32[]{:S(2)}, u32[]{:S(2)}) collective-permute-start(bf16[64,1024]{1,0:T(8,128)(2,1)S(1)} %get-tuple-element.57), channel_id=1, source_target_pairs={{0,64},{1,65},{2,66},{3,67},{4,68},{5,69},{6,70},{7,71},{8,72},{9,... | collective-permute-start | bytes 393224 | tf_op jit(solution)/shard_map/ppermute | solution.py:394
  146.3 3.3 %collective-permute-done.12.c_in = bf16[64,1024]{1,0:T(8,128)(2,1)S(1)} collective-permute-done((bf16[64,1024]{1,0:T(8,128)(2,1)S(1)}, bf16[64,1024]{1,0:T(8,128)(2,1)S(1)}, u32[]{:S(2)}, u32[]{:S(2)}) %collective-permute-start.12) | collective-permute-done | bytes 131104 | tf_op jit(solution)/shard_map/ppermute | solution.py:394
  149.6 4.9 %shard_map.70 = (f32[2,64,1024]{2,1,0:T(8,128)S(1)}, f32[2,64,1024]{2,1,0:T(8,128)S(1)}, f32[2,64,128]{2,1,0:T(8,128)S(1)}, bf16[64,1024]{1,0:T(8,128)(2,1)S(1)}, bf16[64,1024]{1,0:T(8,128)(2,1)S(1)}) custom-call(s32[2]{0:T(128)S(1)} %pad_add_fusion.at, bf16[1024,1024]{1,0:T(8,128)(2,1)S(1)} %shard_map.68.own, ...), custom_call_target="tpu_custom_call" | custom-call | tf_op jit(solution)/shard_map/pallas_call | solution.py:311
  155.7 7.1 %collective-permute-done.13.g_in = bf16[64,1024]{1,0:T(8,128)(2,1)S(1)} collective-permute-done((bf16[64,1024]{1,0:T(8,128)(2,1)S(1)}, bf16[64,1024]{1,0:T(8,128)(2,1)S(1)}, u32[]{:S(2)}, u32[]{:S(2)}) %collective-permute-start.13) | collective-permute-done | bytes 131104 | tf_op jit(solution)/shard_map/ppermute | solution.py:400
  162.9 2.9 %shard_map.71 = (bf16[16,64,640]{2,1,0:T(8,128)(2,1)S(1)}, bf16[16,64,512]{2,1,0:T(8,128)(2,1)S(1)}) custom-call(s32[2]{0:T(128)S(1)} %pad_add_fusion.at, bf16[1024,1024]{1,0:T(8,128)(2,1)S(1)} %shard_map.68.own, bf16[1024,1024]{1,0:T(8,128)(2,1)} %collective-permute-done.11.other, f32[64,1024]{1,0:T(8,128)S(1)} %get-tuple-element.52.g4, ...), custom_call_target="tpu_custom_call" | custom-call | tf_op jit(solution)/shard_map/pallas_call | solution.py:311
  165.8 21.9 %all_to_all.26.right = bf16[16,64,640]{2,1,0:T(8,128)(2,1)S(1)} all-to-all(bf16[16,64,640]{2,1,0:T(8,128)(2,1)S(1)} %get-tuple-element.64), channel_id=1, replica_groups=mesh['zh'=2,'co'=2,'zl'=2,'y'=4,'x'=4] {'co','zl','y'}, dimensions={0} | all-to-all | bytes 2621440 | tf_op jit(solution)/shard_map/all_to_all | solution.py:352
  187.7 4.3 %all-to-all-start.3 = ((bf16[16,64,512]{2,1,0:T(8,128)(2,1)}), bf16[16,64,512]{2,1,0:T(8,128)(2,1)}, u32[]{:S(2)}, u32[]{:S(2)}) async-start(bf16[16,64,512]{2,1,0:T(8,128)(2,1)} %copy-done.13), calls=%async_computation.3 | async-start | bytes 2097152 | tf_op jit(solution)/shard_map/all_to_all | solution.py:352
  199.9 8.4 %all-to-all-done.3.right = bf16[16,64,512]{2,1,0:T(8,128)(2,1)} async-done(((bf16[16,64,512]{2,1,0:T(8,128)(2,1)}), bf16[16,64,512]{2,1,0:T(8,128)(2,1)}, u32[]{:S(2)}, u32[]{:S(2)}) %all-to-all-start.3) | async-done | bytes 1048608 | tf_op jit(solution)/shard_map/all_to_all | solution.py:352
  216.7 3.3 %collective-permute-start.18 = (bf16[256,512]{1,0:T(8,128)(2,1)S(1)}, bf16[256,512]{1,0:T(8,128)(2,1)S(1)}, u32[]{:S(2)}, u32[]{:S(2)}) collective-permute-start(bf16[256,512]{1,0:T(8,128)(2,1)S(1)} %get-tuple-element.77), channel_id=1, source_target_pairs={{0,2},{1,3},{2,0},{3,1},{4,6},{5,7},{6,4},{7,5},{8,10},{9,11},{10,... | collective-permute-start | bytes 786440 | tf_op jit(solution)/shard_map/ppermute | solution.py:348
  220.0 5.0 %collective-permute-done.17.refs_5_ = bf16[256,512]{1,0:T(8,128)(2,1)S(1)} collective-permute-done((bf16[256,512]{1,0:T(8,128)(2,1)S(1)}, bf16[256,512]{1,0:T(8,128)(2,1)S(1)}, u32[]{:S(2)}, u32[]{:S(2)}) %collective-permute-start.17) | collective-permute-done | bytes 262176 | tf_op jit(solution)/shard_map/ppermute | solution.py:348
  225.0 6.8 %collective-permute-done.18.refs_6_ = bf16[256,512]{1,0:T(8,128)(2,1)S(1)} collective-permute-done((bf16[256,512]{1,0:T(8,128)(2,1)S(1)}, bf16[256,512]{1,0:T(8,128)(2,1)S(1)}, u32[]{:S(2)}, u32[]{:S(2)}) %collective-permute-start.18) | collective-permute-done | bytes 262176 | tf_op jit(solution)/shard_map/ppermute | solution.py:348
  (83 shorter events, 45.4 us)
Async XLA Ops:
  29.9 39.7 %collective-permute-start = (bf16[8,64,1024]{2,1,0:T(8,128)(2,1)S(1)}, bf16[8,64,1024]{2,1,0:T(8,128)(2,1)S(1)}, u32[]{:S(2)}, u32[]{:S(2)}) collective-permute-start(bf16[8,64,1024]{2,1,0:T(8,128)(2,1)S(1)} %all_to_all.25), channel_id=1, source_target_pairs={{0,32},{32,0},{1,33},{33,1},{2,34},{34,2},{3,35},{35,3},{4,36},{36... | collective-permute-start | bytes 3145736 | tf_op jit(solution)/shard_map/ppermute | solution.py:378
  29.9 29.6 %collective-permute-start.2 = (bf16[256,1024]{1,0:T(8,128)(2,1)}, bf16[256,1024]{1,0:T(8,128)(2,1)S(1)}, u32[]{:S(2)}, u32[]{:S(2)}) collective-permute-start(bf16[256,1024]{1,0:T(8,128)(2,1)} %get-tuple-element.46.w0), channel_id=1, source_target_pairs={{0,3},{1,0},{2,1},{3,2},{4,7},{5,4},{6,5},{7,6},{8,11},{9,8},{10,9... | collective-permute-start | bytes 1572872 | tf_op jit(solution)/shard_map/ppermute | solution.py:348
  32.7 28.1 %collective-permute-start.1 = (bf16[256,1024]{1,0:T(8,128)(2,1)}, bf16[256,1024]{1,0:T(8,128)(2,1)}, u32[]{:S(2)}, u32[]{:S(2)}) collective-permute-start(bf16[256,1024]{1,0:T(8,128)(2,1)} %get-tuple-element.46.w0), channel_id=1, source_target_pairs={{0,1},{1,2},{2,3},{3,0},{4,5},{5,6},{6,7},{7,4},{8,9},{9,10},{10,1... | collective-permute-start | bytes 1572872 | tf_op jit(solution)/shard_map/ppermute | solution.py:348
  32.7 18.2 %collective-permute-start.5 = (bf16[32,1024]{1,0:T(8,128)(2,1)S(1)}, bf16[32,1024]{1,0:T(8,128)(2,1)S(1)}, u32[]{:S(2)}, u32[]{:S(2)}) collective-permute-start(bf16[32,1024]{1,0:T(8,128)(2,1)S(1)} %get-tuple-element.48), channel_id=1, source_target_pairs={{0,1},{1,2},{2,3},{3,0},{4,5},{5,6},{6,7},{7,4},{8,9},{9,10},{10,1... | collective-permute-start | bytes 196616 | tf_op jit(solution)/shard_map/ppermute | solution.py:348
  33.5 17.5 %collective-permute-start.6 = (bf16[32,1024]{1,0:T(8,128)(2,1)S(1)}, bf16[32,1024]{1,0:T(8,128)(2,1)S(1)}, u32[]{:S(2)}, u32[]{:S(2)}) collective-permute-start(bf16[32,1024]{1,0:T(8,128)(2,1)S(1)} %get-tuple-element.49), channel_id=1, source_target_pairs={{0,2},{1,3},{2,0},{3,1},{4,6},{5,7},{6,4},{7,5},{8,10},{9,11},{10,... | collective-permute-start | bytes 196616 | tf_op jit(solution)/shard_map/ppermute | solution.py:348
  50.9 4.3 %collective-permute-start.7 = (bf16[32,1024]{1,0:T(8,128)(2,1)S(1)}, bf16[32,1024]{1,0:T(8,128)(2,1)S(1)}, u32[]{:S(2)}, u32[]{:S(2)}) collective-permute-start(bf16[32,1024]{1,0:T(8,128)(2,1)S(1)} %get-tuple-element.50), channel_id=1, source_target_pairs={{0,3},{1,0},{2,1},{3,2},{4,7},{5,4},{6,5},{7,6},{8,11},{9,8},{10,9... | collective-permute-start | bytes 196616 | tf_op jit(solution)/shard_map/ppermute | solution.py:348
  56.0 19.4 %all-to-all-start.1 = ((bf16[8,32,1024]{2,1,0:T(8,128)(2,1)}), bf16[8,32,1024]{2,1,0:T(8,128)(2,1)S(1)}, u32[]{:S(2)}, u32[]{:S(2)}) async-start(bf16[8,32,1024]{2,1,0:T(8,128)(2,1)} %shard_map.67), calls=%async_computation.1 | async-start | bytes 1048576 | tf_op jit(solution)/shard_map/all_to_all | solution.py:352
  59.6 6.5 %collective-permute-start.4 = (bf16[128,1024]{1,0:T(8,128)(2,1)S(1)}, bf16[128,1024]{1,0:T(8,128)(2,1)S(1)}, u32[]{:S(2)}, u32[]{:S(2)}) collective-permute-start(bf16[128,1024]{1,0:T(8,128)(2,1)S(1)} %slice.9), channel_id=1, source_target_pairs={{0,3},{1,0},{2,1},{3,2},{4,7},{5,4},{6,5},{7,6},{8,11},{9,8},{10,9... | collective-permute-start | bytes 786440 | tf_op jit(solution)/shard_map/ppermute | solution.py:348
  61.8 7.7 %collective-permute-start.3 = (bf16[128,1024]{1,0:T(8,128)(2,1)S(1)}, bf16[128,1024]{1,0:T(8,128)(2,1)S(1)}, u32[]{:S(2)}, u32[]{:S(2)}) collective-permute-start(bf16[128,1024]{1,0:T(8,128)(2,1)S(1)} %slice.8), channel_id=1, source_target_pairs={{0,1},{1,2},{2,3},{3,0},{4,5},{5,6},{6,7},{7,4},{8,9},{9,10},{10,1... | collective-permute-start | bytes 786440 | tf_op jit(solution)/shard_map/ppermute | solution.py:348
  75.4 14.8 %collective-permute-start.10 = (bf16[8,32,1024]{2,1,0:T(8,128)(2,1)S(1)}, bf16[8,32,1024]{2,1,0:T(8,128)(2,1)S(1)}, u32[]{:S(2)}, u32[]{:S(2)}) collective-permute-start(bf16[8,32,1024]{2,1,0:T(8,128)(2,1)S(1)} %all-to-all-done.1.n0), channel_id=1, source_target_pairs={{0,3},{1,0},{2,1},{3,2},{4,7},{5,4},{6,5},{7,6},{8,11},{9,8},{10,9... | collective-permute-start | bytes 1572872 | tf_op jit(solution)/shard_map/ppermute | solution.py:348
  75.4 16.3 %collective-permute-start.9 = (bf16[8,32,1024]{2,1,0:T(8,128)(2,1)S(1)}, bf16[8,32,1024]{2,1,0:T(8,128)(2,1)S(1)}, u32[]{:S(2)}, u32[]{:S(2)}) collective-permute-start(bf16[8,32,1024]{2,1,0:T(8,128)(2,1)S(1)} %all-to-all-done.1.n0), channel_id=1, source_target_pairs={{0,2},{1,3},{2,0},{3,1},{4,6},{5,7},{6,4},{7,5},{8,10},{9,11},{10,... | collective-permute-start | bytes 1572872 | tf_op jit(solution)/shard_map/ppermute | solution.py:348
  77.0 22.3 %collective-permute-start.8 = (bf16[8,32,1024]{2,1,0:T(8,128)(2,1)S(1)}, bf16[8,32,1024]{2,1,0:T(8,128)(2,1)S(1)}, u32[]{:S(2)}, u32[]{:S(2)}) collective-permute-start(bf16[8,32,1024]{2,1,0:T(8,128)(2,1)S(1)} %all-to-all-done.1.n0), channel_id=1, source_target_pairs={{0,1},{1,2},{2,3},{3,0},{4,5},{5,6},{6,7},{7,4},{8,9},{9,10},{10,1... | collective-permute-start | bytes 1572872 | tf_op jit(solution)/shard_map/ppermute | solution.py:348
  100.6 35.2 %collective-permute-start.11 = (bf16[1024,1024]{1,0:T(8,128)(2,1)S(1)}, bf16[1024,1024]{1,0:T(8,128)(2,1)}, u32[]{:S(2)}, u32[]{:S(2)}) collective-permute-start(bf16[1024,1024]{1,0:T(8,128)(2,1)S(1)} %shard_map.68.own), channel_id=1, source_target_pairs={{0,32},{32,0},{1,33},{33,1},{2,34},{34,2},{3,35},{35,3},{4,36},{36... | collective-permute-start | bytes 6291464 | tf_op jit(solution)/shard_map/ppermute | solution.py:388
  100.7 35.1 %all-to-all-start.2 = ((bf16[16,64,1024]{2,1,0:T(8,128)(2,1)}), bf16[16,64,1024]{2,1,0:T(8,128)(2,1)}, u32[]{:S(2)}, u32[]{:S(2)}) async-start(bf16[16,64,1024]{2,1,0:T(8,128)(2,1)} %bitcast.14), calls=%async_computation.2 | async-start | bytes 4194304 | tf_op jit(solution)/shard_map/all_to_all | solution.py:352
  140.8 8.8 %collective-permute-start.12 = (bf16[64,1024]{1,0:T(8,128)(2,1)S(1)}, bf16[64,1024]{1,0:T(8,128)(2,1)S(1)}, u32[]{:S(2)}, u32[]{:S(2)}) collective-permute-start(bf16[64,1024]{1,0:T(8,128)(2,1)S(1)} %get-tuple-element.57), channel_id=1, source_target_pairs={{0,64},{1,65},{2,66},{3,67},{4,68},{5,69},{6,70},{7,71},{8,72},{9,... | collective-permute-start | bytes 393224 | tf_op jit(solution)/shard_map/ppermute | solution.py:394
  154.4 8.4 %collective-permute-start.13 = (bf16[64,1024]{1,0:T(8,128)(2,1)S(1)}, bf16[64,1024]{1,0:T(8,128)(2,1)S(1)}, u32[]{:S(2)}, u32[]{:S(2)}) collective-permute-start(bf16[64,1024]{1,0:T(8,128)(2,1)S(1)} %get-tuple-element.58), channel_id=1, source_target_pairs={{64,0},{65,1},{66,2},{67,3},{68,4},{69,5},{70,6},{71,7},{72,8},{73... | collective-permute-start | bytes 393224 | tf_op jit(solution)/shard_map/ppermute | solution.py:400
  187.7 20.6 %all-to-all-start.3 = ((bf16[16,64,512]{2,1,0:T(8,128)(2,1)}), bf16[16,64,512]{2,1,0:T(8,128)(2,1)}, u32[]{:S(2)}, u32[]{:S(2)}) async-start(bf16[16,64,512]{2,1,0:T(8,128)(2,1)} %copy-done.13), calls=%async_computation.3 | async-start | bytes 2097152 | tf_op jit(solution)/shard_map/all_to_all | solution.py:352
  195.8 36.0 %copy-start.4 = (bf16[1,256,1024]{2,1,0:T(8,128)(2,1)S(1)}, bf16[1,256,1024]{2,1,0:T(8,128)(2,1)}, u32[]{:S(2)}) copy-start(bf16[1,256,1024]{2,1,0:T(8,128)(2,1)} %param.6) | copy-start | bytes 1572868
  195.8 15.3 %collective-permute-start.14 = (bf16[256,512]{1,0:T(8,128)(2,1)S(1)}, bf16[256,512]{1,0:T(8,128)(2,1)S(1)}, u32[]{:S(2)}, u32[]{:S(2)}) collective-permute-start(bf16[256,512]{1,0:T(8,128)(2,1)S(1)} %get-tuple-element.66), channel_id=1, source_target_pairs={{0,1},{1,2},{2,3},{3,0},{4,5},{5,6},{6,7},{7,4},{8,9},{9,10},{10,1... | collective-permute-start | bytes 786440 | tf_op jit(solution)/shard_map/ppermute | solution.py:348
  195.8 15.3 %collective-permute-start.15 = (bf16[256,512]{1,0:T(8,128)(2,1)S(1)}, bf16[256,512]{1,0:T(8,128)(2,1)S(1)}, u32[]{:S(2)}, u32[]{:S(2)}) collective-permute-start(bf16[256,512]{1,0:T(8,128)(2,1)S(1)} %get-tuple-element.67), channel_id=1, source_target_pairs={{0,2},{1,3},{2,0},{3,1},{4,6},{5,7},{6,4},{7,5},{8,10},{9,11},{10,... | collective-permute-start | bytes 786440 | tf_op jit(solution)/shard_map/ppermute | solution.py:348
  198.5 13.3 %collective-permute-start.16 = (bf16[256,512]{1,0:T(8,128)(2,1)S(1)}, bf16[256,512]{1,0:T(8,128)(2,1)S(1)}, u32[]{:S(2)}, u32[]{:S(2)}) collective-permute-start(bf16[256,512]{1,0:T(8,128)(2,1)S(1)} %get-tuple-element.68), channel_id=1, source_target_pairs={{0,3},{1,0},{2,1},{3,2},{4,7},{5,4},{6,5},{7,6},{8,11},{9,8},{10,9... | collective-permute-start | bytes 786440 | tf_op jit(solution)/shard_map/ppermute | solution.py:348
  215.8 9.2 %collective-permute-start.17 = (bf16[256,512]{1,0:T(8,128)(2,1)S(1)}, bf16[256,512]{1,0:T(8,128)(2,1)S(1)}, u32[]{:S(2)}, u32[]{:S(2)}) collective-permute-start(bf16[256,512]{1,0:T(8,128)(2,1)S(1)} %get-tuple-element.76), channel_id=1, source_target_pairs={{0,1},{1,2},{2,3},{3,0},{4,5},{5,6},{6,7},{7,4},{8,9},{9,10},{10,1... | collective-permute-start | bytes 786440 | tf_op jit(solution)/shard_map/ppermute | solution.py:348
  216.7 15.1 %collective-permute-start.18 = (bf16[256,512]{1,0:T(8,128)(2,1)S(1)}, bf16[256,512]{1,0:T(8,128)(2,1)S(1)}, u32[]{:S(2)}, u32[]{:S(2)}) collective-permute-start(bf16[256,512]{1,0:T(8,128)(2,1)S(1)} %get-tuple-element.77), channel_id=1, source_target_pairs={{0,2},{1,3},{2,0},{3,1},{4,6},{5,7},{6,4},{7,5},{8,10},{9,11},{10,... | collective-permute-start | bytes 786440 | tf_op jit(solution)/shard_map/ppermute | solution.py:348
  220.0 11.8 %collective-permute-start.19 = (bf16[256,512]{1,0:T(8,128)(2,1)S(1)}, bf16[256,512]{1,0:T(8,128)(2,1)S(1)}, u32[]{:S(2)}, u32[]{:S(2)}) collective-permute-start(bf16[256,512]{1,0:T(8,128)(2,1)S(1)} %get-tuple-element.78), channel_id=1, source_target_pairs={{0,3},{1,0},{2,1},{3,2},{4,7},{5,4},{6,5},{7,6},{8,11},{9,8},{10,9... | collective-permute-start | bytes 786440 | tf_op jit(solution)/shard_map/ppermute | solution.py:348
  (20 other events, 131.8 us)
where the time goes:
time: 236 us; the launch traced here: 235 us
  waiting for transfers between devices  110 us (47%)
  blocking collectives  43.3 us (18%)
  starting transfers between devices  39.9 us (17%)
  Pallas kernels  25.9 us (11%)
  local copies, waits for them, and re-layouts  15.2 us (6%)
    ppermute x16, waiting for transfers between devices, along_x(): lax.ppermute(v, 'x', [(i, (i + k) % 4) for i in range(4)])  61.1 us
    all_to_all x2, blocking collectives, group(): return lax.all_to_all(v, axes, 0, 0, tiled=True)  43.3 us
    all_to_all x3, waiting for transfers between devices, group(): return lax.all_to_all(v, axes, 0, 0, tiled=True)  38.3 us
    ppermute x16, starting transfers between devices, along_x(): lax.ppermute(v, 'x', [(i, (i + k) % 4) for i in range(4)])  19.9 us
    unnamed x42, local copies, waits for them, and re-layouts  14.1 us
    all_to_all x3, starting transfers between devices, group(): return lax.all_to_all(v, axes, 0, 0, tiled=True)  13 us
    pallas_call x3, Pallas kernels, chain_call(): call(kernel, out, in_specs=[pl.BlockSpec(memory_space=pltpu.SMEM)] + [pl....  11 us
    ppermute x1, waiting for transfers between devices, per_device(): g_in = lax.ppermute(g, 'zh', [(1, 0)])  7.15 us
  transfers between devices with their start and end apart: 23, of which 15 were waited for; matrix products, arithmetic and copies ran while one was open for 0% of the time, Pallas kernels for 3%

commit v1 on v0

v1 whole, which is shorter than its diff:
```python
import functools

import jax
import jax.numpy as jnp
from jax import lax
from jax.experimental import pallas as pl
from jax.experimental.pallas import tpu as pltpu
from jax.sharding import Mesh
from jax.sharding import PartitionSpec as P


VHEADS = 8
sharpness_divisor = 0.6666667
epsilon = 1e-05
BF = jnp.bfloat16
F32 = jnp.float32
INTERPRET = False
KEEPS = ((0, 1), (0, 2), (0, 3), (1, 2), (1, 3), (2, 3))
LAYER = ("zh", "co")


def shape(dims, dtype):
    return jax.ShapeDtypeStruct(dims, dtype)


def call(kernel, out, **rest):
    params = pltpu.CompilerParams(vmem_limit_bytes=20 << 20)
    return pl.pallas_call(kernel, out_shape=out, interpret=INTERPRET, compiler_params=params, **rest)


def tiles(width, most=128):
    step = min(width, most)
    return [slice(i, i + step) for i in range(0, width, step)]


def by_tile(rows, width, most=128):
    cols = tiles(width, min(most, 128))
    return pltpu.VMEM((len(cols), rows, cols[0].stop), F32)


def pattern_probs(logits, noise, s):
    expo = [
        jnp.exp((logits[k, :, s].astype(F32) + noise[k, :, s].astype(F32)) * (1.0 / sharpness_divisor))
        for k in range(6)
    ]
    inverse = 1.0 / (((expo[0] + expo[1]) + (expo[2] + expo[3])) + (expo[4] + expo[5]))
    return [e * inverse for e in expo]


def mask_kernel(at, logits, noise, weight, gain, scaled, q0, q1, q2, q3, rows):
    for i, s in enumerate(tiles(weight.shape[1])):
        p = pattern_probs(logits, noise, s)
        for r in range(4):
            kept = [p[k] for k in range(6) if r in KEEPS[k]]
            rows.at[i][pl.ds(r, kept[0].shape[0], stride=4), :] = kept[0] + kept[1] + kept[2]
        value = weight[:, s].astype(F32) * rows[i] * gain[...]
        scaled[:, s] = value.astype(BF)
        rows[i] = value
        quarter = q0.shape[0]
        for k, q in enumerate((q0, q1, q2, q3)):
            begin = pl.multiple_of(lax.rem(at[0] + k, 4) * quarter, quarter)
            one = rows.at[i][pl.ds(begin, quarter), :]
            two = rows.at[i][pl.ds(begin + 4 * quarter, quarter), :]
            q[:, s] = (one + two).astype(BF)


def masked_weights(at, logits, noise, weight, gain):
    n, kv = weight.shape
    return call(
        mask_kernel,
        (shape((n, kv), BF),) + (shape((n // 8, kv), BF),) * 4,
        in_specs=[pl.BlockSpec(memory_space=pltpu.SMEM)] + [pl.BlockSpec(memory_space=pltpu.VMEM)] * 4,
        scratch_shapes=[by_tile(n, kv)],
    )(at, logits, noise, weight, gain)


def final_kernel(logits, noise, weight, gain, *refs):
    parts, out, rows = refs[:-2], refs[-2], refs[-1]
    tile = rows.shape[2]
    where = [(j, at) for j in range(len(parts) // 4) for at in range(0, parts[j * 4].shape[1], tile)]
    for i, (j, at) in enumerate(where):
        s, inner = slice(i * tile, (i + 1) * tile), slice(at, at + tile)
        mine = parts[j * 4 : j * 4 + 4]
        total = (mine[0][:, inner].astype(F32) + mine[1][:, inner].astype(F32)) + (
            mine[2][:, inner].astype(F32) + mine[3][:, inner].astype(F32)
        )
        rows[i] = total * gain[...] * weight[:, s].astype(F32) * (1.0 / sharpness_divisor)
        d = [rows.at[i][pl.ds(r, logits.shape[1], stride=4), :] for r in range(4)]
        p = pattern_probs(logits, noise, s)
        dprob = [d[a] + d[b] for a, b in KEEPS]
        mean = p[0] * dprob[0]
        for k in range(1, 6):
            mean = mean + p[k] * dprob[k]
        for k in range(6):
            out[k, :, s] = (p[k] * (dprob[k] - mean)).astype(BF)


def logit_gradient(logits, noise, weight, gain, parts):
    return call(
        final_kernel,
        shape(logits.shape, BF),
        scratch_shapes=[by_tile(*weight.shape, most=weight.shape[1] // 8)],
    )(logits, noise, weight, gain, *parts)


def run_copies(copies, sems):
    copies = [pltpu.make_async_copy(src, dst, sems.at[i]) for i, (src, dst) in enumerate(copies)]
    for copy in copies:
        copy.start()
    for copy in copies:
        copy.wait()


def wide(index, part):
    return pl.ds(pl.multiple_of(index * part, part), part)


def place(core, zl, g, h):
    return zl * 16 + jnp.where(core == 0, g * 4 + h, h * 4 + g)


def heads_kernel(at, tokens, near, far, sems):
    zl, g, h, core = (at[i] for i in range(4))
    rows, width = tokens.shape[1:]
    part = width // 32
    copies = []
    for k in range(4):
        for i in range(4):
            source = wide(place(core, zl, lax.rem(g + k, 4), i), part)
            for m in range(2):
                copies.append((
                    tokens.at[core if m == 0 else 1 - core, :, source],
                    near.at[k, pl.ds(m * rows, rows), pl.ds(i * part, part)],
                ))
            source = wide(place(1 - core, 1 - zl, lax.rem(h + k, 4), i), part)
            copies.append((tokens.at[core, :, source], far.at[k, :, pl.ds(i * part, part)]))
    run_copies(copies, sems)


def token_blocks(at, tokens):
    rows, width = tokens.shape[1:]
    block = pl.BlockSpec(memory_space=pl.ANY)
    return call(
        heads_kernel,
        (shape((4, 2 * rows, width // 8), BF), shape((4, rows, width // 8), BF)),
        in_specs=[pl.BlockSpec(memory_space=pltpu.SMEM), block],
        out_specs=(block, block),
        scratch_shapes=[pltpu.SemaphoreType.DMA((48,))],
    )(at, tokens)


def pair_kernel(at, mine, other, o0, o1, o2, o3, sems):
    g, h = at[1], at[2]
    rows = mine.shape[1]
    part = mine.shape[2] // 4
    copies = []
    for k, out in enumerate((o0, o1, o2, o3)):
        for i in range(4):
            source = mine.at[lax.rem(i - h + 4, 4), :, wide(lax.rem(g + k, 4), part)]
            copies.append((source, out.at[pl.ds(0, rows), pl.ds(i * part, part)]))
        copies.append((other.at[k], out.at[pl.ds(rows, rows), :]))
    run_copies(copies, sems)


def pair_blocks(at, mine, other):
    rows, span = mine.shape[1:]
    block = pl.BlockSpec(memory_space=pl.ANY)
    return call(
        pair_kernel,
        (shape((2 * rows, span), BF),) * 4,
        in_specs=[pl.BlockSpec(memory_space=pltpu.SMEM), block, block],
        out_specs=(block,) * 4,
        scratch_shapes=[pltpu.SemaphoreType.DMA((20,))],
    )(at, mine, other)


def sums_kernel(repeat, head, core, tokens, grads, y0, spread, g4):
    t = tokens[0]
    pieces = [t[:, r * head : (r + 1) * head].astype(F32) for r in range(repeat)]
    total = functools.reduce(lambda a, b: a + b, pieces)
    mean = total * (1.0 / repeat)
    squares = functools.reduce(lambda a, b: a + b, [(p - mean) * (p - mean) for p in pieces])
    y0[...] = total

    @pl.when(pl.program_id(0) == 0)
    def _():
        spread[...] = squares

    @pl.when(pl.program_id(0) != 0)
    def _():
        spread[...] += squares

    g = grads[0]
    g4[...] = functools.reduce(
        lambda a, b: a + b, [g[:, r * head : (r + 1) * head].astype(F32) for r in range(repeat)]
    )


def token_sums(core, tokens, grads, head):
    rows, width = tokens.shape[1:]
    span = width // VHEADS
    block = pl.BlockSpec((1, rows, span), lambda h, core: (core[0], 0, h))
    narrow = pl.BlockSpec((rows, head), lambda h, core: (0, h))
    return call(
        functools.partial(sums_kernel, span // head, head),
        (
            shape((rows, VHEADS * head), F32),
            shape((rows, head), F32),
            shape((rows, VHEADS * head), F32),
        ),
        grid_spec=pltpu.PrefetchScalarGridSpec(
            num_scalar_prefetch=1,
            grid=(VHEADS,),
            in_specs=[block, block],
            out_specs=(
                narrow,
                pl.BlockSpec((rows, head), lambda h, core: (0, 0)),
                narrow,
            ),
        ),
    )(core, tokens, grads)


def small(count):
    vmem = pl.BlockSpec(memory_space=pltpu.VMEM)
    return dict(in_specs=[pl.BlockSpec(memory_space=pltpu.SMEM)] + [vmem] * count)


def values_kernel(at, *refs):
    tokens, w, outs = refs[:8], refs[8:12], refs[12:]
    part = w[0].shape[0]
    rows = tokens[0].shape[0]
    for k in range(4):
        total = None
        for j in range(4):
            cols = wide(lax.rem(at[2] - j + 4, 4), part)
            lhs = jnp.concatenate([tokens[k][:, cols], tokens[4 + k][:, cols]], 0)
            term = jnp.dot(lhs, w[j][...], preferred_element_type=F32)
            total = term if total is None else total + term
        outs[k][0] = total[:rows].astype(BF)
        outs[k][1] = total[rows:].astype(BF)


def partial_values(at, near, far, blocks):
    rows = near[0].shape[0]
    out = [shape((2, rows, blocks[0].shape[1]), BF)] * 4
    return call(values_kernel, out, **small(12))(at, *near, *far, *blocks)


def gathered_kernel(m0, m1, m2, m3, own, give, far_keep, far_give):
    rows = own.shape[0]
    for z in range(2):
        total = (m0[z].astype(F32) + m1[z].astype(F32)) + (m2[z].astype(F32) + m3[z].astype(F32))
        if z == 0:
            own[...] = total[:rows]
            give[...] = total[rows:].astype(BF)
        else:
            far_keep[...] = total[:rows].astype(BF)
            far_give[...] = total[rows:].astype(BF)


def turn_over_kernel(at, *refs):
    tokens, cs, out = refs[:8], refs[8:12], refs[12]
    rows = tokens[0].shape[0]
    head = cs[0].shape[2] // 4
    for k in range(4):
        for z in range(2):
            add = []
            for i in range(4):
                which = jnp.where(at[3] == 0, at[1], i)
                c = cs[k][z, :, wide(which, head)].astype(F32)
                add += [c, c]
            x = tokens[z * 4 + k][...].astype(F32) + jnp.concatenate(add, 1)
            begin = (k * 2 + z) * rows
            out[:, begin : begin + rows] = x.astype(BF).T


def turn_over(at, near, far, cs):
    rows, span = near[0].shape
    return call(turn_over_kernel, shape((span, 8 * rows), BF), **small(12))(at, *near, *far, *cs)


def short_kernel(q0, q1, q2, q3, out):
    total = (q0[...].astype(F32) + q1[...].astype(F32)) + (q2[...].astype(F32) + q3[...].astype(F32))
    out[...] = total.astype(BF)


def square_kernel(at, n0, n1, n2, n3, out):
    quarter = n0.shape[2]
    zl, g, h, core = (at[i] for i in range(4))
    for j, n in enumerate((n0, n1, n2, n3)):
        for k in range(4):
            for z in range(2):
                there = zl if z == 0 else 1 - zl
                at_row = place(core, there, lax.rem(g - k + 4, 4), lax.rem(h - j + 4, 4))
                out[wide(at_row, quarter), :] = n[k, z]


def scale_of(sums, spread, repeat, width):
    mean = jnp.sum(spread, -1, keepdims=True) + jnp.sum(sums * sums, -1, keepdims=True) * (1.0 / repeat)
    return lax.rsqrt(mean * (1.0 / width) + epsilon)


def by_layer(core, layer, own, other, acc, v, dims):
    @pl.when(core == layer)
    def _():
        acc[...] = lax.dot_general(v, own[...], (dims, ((), ())), preferred_element_type=F32)

    @pl.when(core != layer)
    def _():
        acc[...] = lax.dot_general(v, other[...], (dims, ((), ())), preferred_element_type=F32)

    return acc[...]


AHEAD = ((1,), (0,))
BEHIND = ((1,), (1,))


def first_kernel(repeat, width, at, own, other, mine, theirs, far_mine, far_theirs, y0, spread, u, c_out, acc):
    one = mine[...] + far_mine[...].astype(F32)
    two = theirs[...].astype(F32) + far_theirs[...].astype(F32)
    u[0] = jnp.where(at[3] == 0, one, two)
    u[1] = jnp.where(at[3] == 0, two, one)
    c = scale_of(y0[...], spread[...], repeat, width) * u[0]
    sums = y0[...] + repeat * c
    value = u[1] + by_layer(at[3], 1, own, other, acc, c.astype(BF), AHEAD)
    c_out[...] = (c + scale_of(sums, spread[...], repeat, width) * value).astype(BF)


def lower_of(width, at, layer, own, other, acc, g, sums, sigma, value):
    vg = g.astype(BF)
    du = by_layer(at[3], layer, own, other, acc, vg, BEHIND)
    dot = jnp.sum(vg.astype(F32) * value, -1, keepdims=True) * (1.0 / width)
    return g + sigma * du - sigma * sigma * dot * sums


def pick(at, a, b):
    first = at[3] == 0
    return jnp.where(first, a, b), jnp.where(first, b, a)


def turn_kernel(
    repeat, width, at, own, other, u, y0, spread, c_in, g4,
    value, sums, sigma, keep, give, far_keep, far_give, g_out, acc,
):
    c = c_in[...]
    base = c.astype(F32)
    inputs = []
    for layer in range(2):
        inputs.append(base)
        sums[layer] = y0[...] + repeat * base
        s = scale_of(sums[layer], spread[...], repeat, width)
        sigma[layer] = jnp.broadcast_to(s, sigma.shape[1:])
        value[layer] = s * (u[layer] + by_layer(at[3], layer, own, other, acc, c, AHEAD))
        base = base + value[layer]
        c = base.astype(BF)
    half = keep.shape[1]
    mine, theirs = pick(at, *inputs)
    low = at[0] == 0
    for c, here, there in ((mine, keep, far_keep), (theirs, give, far_give)):
        c = c.astype(BF).astype(F32)
        here[...] = jnp.where(low, c[:, :half], c[:, half:]).astype(BF)
        there[...] = jnp.where(low, c[:, half:], c[:, :half]).astype(BF)
    g = g4[...]
    for layer in (1, 0):
        g = lower_of(width, at, layer, own, other, acc, g, sums[layer], sigma[layer][:, :1], value[layer])
    g_out[...] = g.astype(BF)


def send_kernel(width, at, own, other, g4, g_in, value, sums, sigma, keep, give, acc):
    g = jnp.where(at[4] == 1, g4[...], g_in[...].astype(F32))
    out = [None, None]
    for layer in (1, 0):
        s = sigma[layer][:, :1]
        out[layer] = g.astype(BF).astype(F32) * s
        if layer == 1:
            g = lower_of(width, at, 1, own, other, acc, g, sums[1], s, value[1])
    mine, theirs = pick(at, *out)
    keep[...] = mine.astype(BF)
    give[...] = theirs.astype(BF)


def chain_call(kernel, out, at, *args):
    rows, kv = args[2].shape[-2:]
    return call(
        kernel,
        out,
        in_specs=[pl.BlockSpec(memory_space=pltpu.SMEM)] + [pl.BlockSpec(memory_space=pltpu.VMEM)] * len(args),
        scratch_shapes=[pltpu.VMEM((rows, kv), F32)],
    )(at, *args)


def wgrad_kernel(at, turned, r0, r1, r2, r3, *outs):
    right = jnp.concatenate([r[z] for r in (r0, r1, r2, r3) for z in range(2)], 0)
    part = outs[0].shape[0]
    for j in range(4):
        rows = wide(lax.rem(at[2] + j, 4), part)
        outs[j][...] = jnp.dot(turned[rows, :], right, preferred_element_type=F32).astype(BF)


AXES = ("zh", "co", "zl", "y", "x")


def move(v, where):
    flat = lambda d: (((d[0] * 2 + d[1]) * 2 + d[2]) * 4 + d[3] % 4) * 4 + d[4] % 4
    every = [(a, b, c, d, e) for a in range(2) for b in range(2) for c in range(2) for d in range(4) for e in range(4)]
    pairs = [(flat(d), flat(where(*d))) for d in every if where(*d) is not None]
    return lax.ppermute(v, AXES, pairs)


def ring(v, k, on_y):
    if k % 4 == 0:
        return v
    return move(v, lambda a, b, c, y, x: (a, b, c, y + k, x) if b == on_y else (a, b, c, y, x + k))


def to_g(v, k):
    return ring(v, k, 0)


def to_h(v, k):
    return ring(v, k, 1)


def along_x(v, k):
    return v if k == 0 else move(v, lambda a, b, c, y, x: (a, b, c, y, x + k))


def to_z(v):
    return move(v, lambda a, b, c, y, x: (a, b, 1 - c, y, x))


def to_core(v):
    return move(v, lambda a, b, c, y, x: (a, 1 - b, c, y, x))


def to_z_core(v):
    return move(v, lambda a, b, c, y, x: (a, 1 - b, 1 - c, y, x))


def up(v):
    return move(v, lambda a, b, c, y, x: (1, b, c, y, x) if a == 0 else None)


def down(v):
    return move(v, lambda a, b, c, y, x: (0, b, c, y, x) if a == 1 else None)


def per_device(value_weight, norm_gain, mask_logits, gumbel_noise, stream_in, stream_grad):
    zh, co, zl, y, x = (lax.axis_index(n) for n in AXES)
    _, rows, width = stream_in.shape
    kv = value_weight.shape[2]
    head = kv // VHEADS
    repeat = width // kv
    part = value_weight.shape[1]
    own = zl * 16 + y * 4 + x
    first = co == 0
    at = jnp.stack([zl, jnp.where(first, y, x), jnp.where(first, x, y), co, zh])
    weight = value_weight[0]
    gain = lax.dynamic_slice_in_dim(norm_gain[0].astype(F32), own * part, part, 0)[:, None]
    wide32 = shape((rows, kv), F32)
    half = shape((rows, kv), BF)

    near, far = token_blocks(at, stream_in)
    far = to_z(far)
    near = [to_g(near[k], k) for k in range(4)]
    scaled, *quarters = masked_weights(x.reshape(1), mask_logits[0], gumbel_noise[0], weight, gain)
    quarters = [along_x(quarters[k], k) for k in range(4)]
    blocks = [to_h(scaled, k) for k in range(4)]
    swapped = to_core(far)
    far = pair_blocks(at, far, swapped)
    far = [to_g(far[k], k) for k in range(4)]

    short = call(short_kernel, shape(quarters[0].shape, BF))(*quarters)
    short = jnp.stack([short, to_z(short)])
    short = jnp.stack([to_g(short, k) for k in range(4)])
    square = [to_h(short, k) for k in range(4)]
    n = call(square_kernel, shape((kv, kv), BF), **small(4))(at, *square)
    n_other = to_core(n)

    u = partial_values(at, near, far, blocks)
    u = [to_g(u[k], -k) for k in range(4)]
    mine, give, far_keep, far_give = call(gathered_kernel, (wide32, half, half, half))(*u)
    far_mine = to_z(far_keep)
    far_theirs = to_z_core(far_give)
    theirs = to_core(give)
    y0, spread, g4 = token_sums(at[3:4], stream_in, stream_grad, head)

    two = shape((2, rows, kv), F32)
    u, c = chain_call(
        functools.partial(first_kernel, repeat, width),
        (two, half),
        at, n, n_other, mine, theirs, far_mine, far_theirs, y0, spread,
    )
    c_in = up(c)
    quarter = shape((rows, kv // 2), BF)
    value, sums, sigma, keep, give, far_keep, far_give, g = chain_call(
        functools.partial(turn_kernel, repeat, width),
        (two, two, shape((2, rows, head), F32)) + (quarter,) * 4 + (half,),
        at, n, n_other, u, y0, spread, c_in, g4,
    )
    g_in = down(g)
    cs = jnp.stack([
        jnp.concatenate([keep, to_core(give)]), jnp.concatenate([to_z(far_keep), to_z_core(far_give)])
    ])
    cs = [to_g(cs, k) for k in range(4)]
    keep, give = chain_call(
        functools.partial(send_kernel, width), (half, half),
        at, n, n_other, g4, g_in, value, sums, sigma,
    )
    right = jnp.stack([jnp.concatenate([keep, to_core(give)]), jnp.concatenate([to_z(keep), to_z_core(give)])])
    right = [to_g(right, k) for k in range(4)]
    turned = turn_over(at, near, far, cs)
    term = call(wgrad_kernel, [shape((part, kv), BF)] * 4, **small(5))(at, turned, *right)
    term = [to_h(term[k], k) for k in range(4)]
    return logit_gradient(mask_logits[0], gumbel_noise[0], weight, gain, term)[None]


def solution(mesh):
    fine = Mesh(mesh.devices.reshape(2, 2, 2, 4, 4), ("zh", "co", "zl", "y", "x"))
    dp = ("zl", "y", "x")

    return jax.shard_map(
        per_device,
        mesh=fine,
        in_specs=(
            P(LAYER, dp, None),
            P(LAYER, None),
            P(LAYER, None, dp, None),
            P(LAYER, None, dp, None),
            P(None, dp, None),
            P(None, dp, None),
        ),
        out_specs=P(LAYER, None, dp, None),
        check_vma=False,
    )
```

time: 236 us -> 197 us (0.83)
  blocking collectives: 43.3 us -> 0 us
  starting transfers between devices: 39.9 us -> 63.4 us
  local copies, waits for them, and re-layouts: 15.2 us -> 3.64 us
  waiting for transfers between devices: 110 us -> 106 us
  Pallas kernels: 25.9 us -> 22.8 us
    all_to_all x2 -> x0, blocking collectives: 43.3 us -> none  [group(): return lax.all_to_all(v, axes, 0, 0, tiled=True)]
    all_to_all x3 -> x0, waiting for transfers between devices: 38.3 us -> none  [group(): return lax.all_to_all(v, axes, 0, 0, tiled=True)]
    ppermute x20 -> x45, starting transfers between devices: 26.8 us -> 63.4 us  [move(): return lax.ppermute(v, AXES, pairs)]
    ppermute x20 -> x45, waiting for transfers between devices: 71.5 us -> 106 us  [move(): return lax.ppermute(v, AXES, pairs)]
    all_to_all x3 -> x0, starting transfers between devices: 13 us -> none  [group(): return lax.all_to_all(v, axes, 0, 0, tiled=True)]
    unnamed x42 -> x16, local copies, waits for them, and re-layouts: 14.1 us -> 3.33 us
    pallas_call x3, Pallas kernels: 11 us -> 6.78 us  [chain_call(): call(kernel, out, in_specs=[pl.BlockSpec(memory_space=pltpu.SMEM)] + [pl....]
    pallas_call x8 -> x10, Pallas kernels: 13.8 us -> 15 us  [the longest x1 2.89 us: per_device(): call(wgrad_kernel, [shape((part, kv), BF)] * 4, **small(5))]
  transfers between devices with their start and end apart: 23 -> 45, of which waited for: 15 -> 25; matrix products, arithmetic and copies ran while one was open for 0% -> 0% of each run, Pallas kernels for 3% -> 6%
where the time goes in v1:
time: 197 us
  waiting for transfers between devices  106 us (54%)
  starting transfers between devices  63.4 us (32%)
  Pallas kernels  22.8 us (12%)
  local copies, waits for them, and re-layouts  3.64 us (2%)
    ppermute x45, waiting for transfers between devices, move(): return lax.ppermute(v, AXES, pairs)  106 us
    ppermute x45, starting transfers between devices, move(): return lax.ppermute(v, AXES, pairs)  63.4 us
    pallas_call x3, Pallas kernels, chain_call(): call(kernel, out, in_specs=[pl.BlockSpec(memory_space=pltpu.SMEM)] + [pl....  6.78 us
  transfers between devices with their start and end apart: 45, of which 25 were waited for; matrix products, arithmetic and copies ran while one was open for 0% of the time, Pallas kernels for 6%

profile of v1, /device:TPU:0, one launch (start us, length us, event | category | flops | bytes accessed | tf_op | source)
XLA Modules:
  0.0 197.0 jit_solution(10796914833093648718)
XLA Ops:
  18.3 3.3 %collective-permute-start.13 = (bf16[2,32,1024]{2,1,0:T(8,128)(2,1)S(1)}, bf16[2,32,1024]{2,1,0:T(8,128)(2,1)S(1)}, u32[]{:S(2)}, u32[]{:S(2)}) collective-permute-start(bf16[2,32,1024]{2,1,0:T(8,128)(2,1)S(1)} %get-tuple-element.86), channel_id=1, source_target_pairs={{0,8},{1,9},{2,10},{3,11},{4,12},{5,13},{6,14},{7,15},{8,0},{9,1},... | collective-permute-start | bytes 393224 | tf_op jit(solution)/shard_map/ppermute | solution.py:409
  24.8 2.9 %collective-permute-done.12 = bf16[2,32,1024]{2,1,0:T(8,128)(2,1)S(1)} collective-permute-done((bf16[2,32,1024]{2,1,0:T(8,128)(2,1)S(1)}, bf16[2,32,1024]{2,1,0:T(8,128)(2,1)S(1)}, u32[]{:S(2)}, u32[]{:S(2)}) %collective-permute-start.12) | collective-permute-done | bytes 131104 | tf_op jit(solution)/shard_map/ppermute | solution.py:409
  36.0 7.8 %collective-permute-done.17.n3 = bf16[4,2,32,1024]{3,2,1,0:T(8,128)(2,1)} collective-permute-done((bf16[4,2,32,1024]{3,2,1,0:T(8,128)(2,1)S(1)}, bf16[4,2,32,1024]{3,2,1,0:T(8,128)(2,1)}, u32[]{:S(2)}, u32[]{:S(2)}) %collective-permute-start.17) | collective-permute-done | bytes 524320 | tf_op jit(solution)/shard_map/ppermute | solution.py:409
  43.8 3.8 %collective-permute-done.15.n1 = bf16[4,2,32,1024]{3,2,1,0:T(8,128)(2,1)} collective-permute-done((bf16[4,2,32,1024]{3,2,1,0:T(8,128)(2,1)S(1)}, bf16[4,2,32,1024]{3,2,1,0:T(8,128)(2,1)}, u32[]{:S(2)}, u32[]{:S(2)}) %collective-permute-start.15) | collective-permute-done | bytes 524320 | tf_op jit(solution)/shard_map/ppermute | solution.py:409
  49.9 3.7 %collective-permute-start.2 = (bf16[128,1024]{1,0:T(8,128)(2,1)S(1)}, bf16[128,1024]{1,0:T(8,128)(2,1)S(1)}, u32[]{:S(2)}, u32[]{:S(2)}) collective-permute-start(bf16[128,1024]{1,0:T(8,128)(2,1)S(1)} %get-tuple-element.81), channel_id=1, source_target_pairs={{0,12},{1,13},{2,14},{3,15},{4,0},{5,1},{6,2},{7,3},{8,4},{9,5},{1... | collective-permute-start | bytes 786440 | tf_op jit(solution)/shard_map/ppermute | solution.py:409
  54.5 7.5 %collective-permute-done.2.refs_3_ = bf16[128,1024]{1,0:T(8,128)(2,1)S(1)} collective-permute-done((bf16[128,1024]{1,0:T(8,128)(2,1)S(1)}, bf16[128,1024]{1,0:T(8,128)(2,1)S(1)}, u32[]{:S(2)}, u32[]{:S(2)}) %collective-permute-start.2) | collective-permute-done | bytes 262176 | tf_op jit(solution)/shard_map/ppermute | solution.py:409
  63.3 3.9 %collective-permute-start = (bf16[128,1024]{1,0:T(8,128)(2,1)S(1)}, bf16[128,1024]{1,0:T(8,128)(2,1)S(1)}, u32[]{:S(2)}, u32[]{:S(2)}) collective-permute-start(bf16[128,1024]{1,0:T(8,128)(2,1)S(1)} %get-tuple-element.83), channel_id=1, source_target_pairs={{0,4},{1,5},{2,6},{3,7},{4,8},{5,9},{6,10},{7,11},{8,12},{9,13},{1... | collective-permute-start | bytes 786440 | tf_op jit(solution)/shard_map/ppermute | solution.py:409
  68.8 5.8 %collective-permute-done.refs_1_ = bf16[128,1024]{1,0:T(8,128)(2,1)S(1)} collective-permute-done((bf16[128,1024]{1,0:T(8,128)(2,1)S(1)}, bf16[128,1024]{1,0:T(8,128)(2,1)S(1)}, u32[]{:S(2)}, u32[]{:S(2)}) %collective-permute-start) | collective-permute-done | bytes 262176 | tf_op jit(solution)/shard_map/ppermute | solution.py:409
  74.6 3.3 %collective-permute-start.6 = (bf16[128,1024]{1,0:T(8,128)(2,1)S(1)}, bf16[128,1024]{1,0:T(8,128)(2,1)S(1)}, u32[]{:S(2)}, u32[]{:S(2)}) collective-permute-start(bf16[128,1024]{1,0:T(8,128)(2,1)S(1)} %get-tuple-element.47), channel_id=1, source_target_pairs={{0,8},{1,9},{2,10},{3,11},{4,12},{5,13},{6,14},{7,15},{8,0},{9,1},... | collective-permute-start | bytes 786440 | tf_op jit(solution)/shard_map/ppermute | solution.py:409
  79.8 4.0 %collective-permute-done.19.refs_9_ = bf16[256,1024]{1,0:T(8,128)(2,1)S(1)} collective-permute-done((bf16[256,1024]{1,0:T(8,128)(2,1)S(1)}, bf16[256,1024]{1,0:T(8,128)(2,1)S(1)}, u32[]{:S(2)}, u32[]{:S(2)}) %collective-permute-start.19) | collective-permute-done | bytes 524320 | tf_op jit(solution)/shard_map/ppermute | solution.py:409
  92.5 11.4 %collective-permute-done.22.m1 = bf16[2,128,1024]{2,1,0:T(8,128)(2,1)S(1)} collective-permute-done((bf16[2,128,1024]{2,1,0:T(8,128)(2,1)S(1)}, bf16[2,128,1024]{2,1,0:T(8,128)(2,1)S(1)}, u32[]{:S(2)}, u32[]{:S(2)}) %collective-permute-start.22) | collective-permute-done | bytes 524320 | tf_op jit(solution)/shard_map/ppermute | solution.py:409
  103.9 3.7 %collective-permute-done.24.m3 = bf16[2,128,1024]{2,1,0:T(8,128)(2,1)S(1)} collective-permute-done((bf16[2,128,1024]{2,1,0:T(8,128)(2,1)S(1)}, bf16[2,128,1024]{2,1,0:T(8,128)(2,1)S(1)}, u32[]{:S(2)}, u32[]{:S(2)}) %collective-permute-start.24) | collective-permute-done | bytes 524320 | tf_op jit(solution)/shard_map/ppermute | solution.py:409
  111.0 3.4 %collective-permute-done.26.far_mine = bf16[64,1024]{1,0:T(8,128)(2,1)S(1)} collective-permute-done((bf16[64,1024]{1,0:T(8,128)(2,1)S(1)}, bf16[64,1024]{1,0:T(8,128)(2,1)S(1)}, u32[]{:S(2)}, u32[]{:S(2)}) %collective-permute-start.26) | collective-permute-done | bytes 131104 | tf_op jit(solution)/shard_map/ppermute | solution.py:409
  117.7 5.4 %collective-permute-start.28 = (bf16[64,1024]{1,0:T(8,128)(2,1)S(1)}, bf16[64,1024]{1,0:T(8,128)(2,1)S(1)}, u32[]{:S(2)}, u32[]{:S(2)}) collective-permute-start(bf16[64,1024]{1,0:T(8,128)(2,1)S(1)} %get-tuple-element.65), channel_id=1, source_target_pairs={{0,64},{1,65},{2,66},{3,67},{4,68},{5,69},{6,70},{7,71},{8,72},{9,... | collective-permute-start | bytes 393224 | tf_op jit(solution)/shard_map/ppermute | solution.py:409
  123.2 3.3 %collective-permute-done.28.c_in = bf16[64,1024]{1,0:T(8,128)(2,1)S(1)} collective-permute-done((bf16[64,1024]{1,0:T(8,128)(2,1)S(1)}, bf16[64,1024]{1,0:T(8,128)(2,1)S(1)}, u32[]{:S(2)}, u32[]{:S(2)}) %collective-permute-start.28) | collective-permute-done | bytes 131104 | tf_op jit(solution)/shard_map/ppermute | solution.py:409
  126.4 3.9 %shard_map.73 = (f32[2,64,1024]{2,1,0:T(8,128)S(1)}, f32[2,64,1024]{2,1,0:T(8,128)S(1)}, f32[2,64,128]{2,1,0:T(8,128)S(1)}, bf16[64,512]{1,0:T(8,128)(2,1)S(1)},...) custom-call(s32[5]{0:T(128)S(1)} %stack.65.at, ...), custom_call_target="tpu_custom_call" | custom-call | tf_op jit(solution)/shard_map/pallas_call | solution.py:386
  133.7 6.5 %collective-permute-done.35.g_in = bf16[64,1024]{1,0:T(8,128)(2,1)S(1)} collective-permute-done((bf16[64,1024]{1,0:T(8,128)(2,1)S(1)}, bf16[64,1024]{1,0:T(8,128)(2,1)S(1)}, u32[]{:S(2)}, u32[]{:S(2)}) %collective-permute-start.35) | collective-permute-done | bytes 131104 | tf_op jit(solution)/shard_map/ppermute | solution.py:409
  145.2 5.5 %collective-permute-done.37 = bf16[64,1024]{1,0:T(8,128)(2,1)S(1)} collective-permute-done((bf16[64,1024]{1,0:T(8,128)(2,1)S(1)}, bf16[64,1024]{1,0:T(8,128)(2,1)S(1)}, u32[]{:S(2)}, u32[]{:S(2)}) %collective-permute-start.37) | collective-permute-done | bytes 131104 | tf_op jit(solution)/shard_map/ppermute | solution.py:409
  152.8 4.1 %collective-permute-start.33 = (bf16[2,128,512]{2,1,0:T(8,128)(2,1)S(1)}, bf16[2,128,512]{2,1,0:T(8,128)(2,1)S(1)}, u32[]{:S(2)}, u32[]{:S(2)}) collective-permute-start(bf16[2,128,512]{2,1,0:T(8,128)(2,1)S(1)} %pad_maximum_fusion.2.refs_8_), channel_id=1, source_target_pairs={{0,8},{1,9},{2,10},{3,11},{4,12},{5,13},{6,14},{7,15},{8,0},{9,1},... | collective-permute-start | bytes 786440 | tf_op jit(solution)/shard_map/ppermute | solution.py:409
  157.0 14.0 %collective-permute-done.33.refs_10_ = bf16[2,128,512]{2,1,0:T(8,128)(2,1)S(1)} collective-permute-done((bf16[2,128,512]{2,1,0:T(8,128)(2,1)S(1)}, bf16[2,128,512]{2,1,0:T(8,128)(2,1)S(1)}, u32[]{:S(2)}, u32[]{:S(2)}) %collective-permute-start.33) | collective-permute-done | bytes 262176 | tf_op jit(solution)/shard_map/ppermute | solution.py:409
  174.9 2.9 %shard_map.76 = (bf16[256,1024]{1,0:T(8,128)(2,1)S(1)}, bf16[256,1024]{1,0:T(8,128)(2,1)S(1)}, bf16[256,1024]{1,0:T(8,128)(2,1)S(1)}, bf16[256,1024]{1,0:T(8,128)(2,1)S(1)}) custom-call(s32[5]{0:T(128)S(1)} %stack.65.at, bf16[1024,1024]{1,0:T(8,128)(2,1)S(1)} %shard_map.74.turned, bf16[2,128,1024]{2,1,0:T(8,128)(2,1)S(1)} %pad_maximum_fusion.1.r0, ...), custom_call_target="tpu_custom_call" | custom-call | tf_op jit(solution)/shard_map/pallas_call | solution.py:515
  177.9 3.2 %collective-permute-start.43 = (bf16[256,1024]{1,0:T(8,128)(2,1)S(1)}, bf16[256,1024]{1,0:T(8,128)(2,1)S(1)}, u32[]{:S(2)}, u32[]{:S(2)}) collective-permute-start(bf16[256,1024]{1,0:T(8,128)(2,1)S(1)} %get-tuple-element.79), channel_id=1, source_target_pairs={{0,2},{1,3},{2,0},{3,1},{4,6},{5,7},{6,4},{7,5},{8,10},{9,11},{10,... | collective-permute-start | bytes 1572872 | tf_op jit(solution)/shard_map/ppermute | solution.py:409
  182.7 5.6 %collective-permute-done.42.refs_1_ = bf16[256,1024]{1,0:T(8,128)(2,1)S(1)} collective-permute-done((bf16[256,1024]{1,0:T(8,128)(2,1)S(1)}, bf16[256,1024]{1,0:T(8,128)(2,1)S(1)}, u32[]{:S(2)}, u32[]{:S(2)}) %collective-permute-start.42) | collective-permute-done | bytes 524320 | tf_op jit(solution)/shard_map/ppermute | solution.py:409
  188.3 5.6 %collective-permute-done.43.refs_2_ = bf16[256,1024]{1,0:T(8,128)(2,1)S(1)} collective-permute-done((bf16[256,1024]{1,0:T(8,128)(2,1)S(1)}, bf16[256,1024]{1,0:T(8,128)(2,1)S(1)}, u32[]{:S(2)}, u32[]{:S(2)}) %collective-permute-start.43) | collective-permute-done | bytes 524320 | tf_op jit(solution)/shard_map/ppermute | solution.py:409
  (108 shorter events, 72.2 us)
Async XLA Ops:
  28.7 15.1 %collective-permute-start.17 = (bf16[4,2,32,1024]{3,2,1,0:T(8,128)(2,1)S(1)}, bf16[4,2,32,1024]{3,2,1,0:T(8,128)(2,1)}, u32[]{:S(2)}, u32[]{:S(2)}) collective-permute-start(bf16[4,2,32,1024]{3,2,1,0:T(8,128)(2,1)S(1)} %pad_maximum_fusion.n0), channel_id=1, source_target_pairs={{0,3},{1,0},{2,1},{3,2},{4,7},{5,4},{6,5},{7,6},{8,11},{9,8},{10,9... | collective-permute-start | bytes 1572872 | tf_op jit(solution)/shard_map/ppermute | solution.py:409
  31.4 12.4 %collective-permute-start.16 = (bf16[4,2,32,1024]{3,2,1,0:T(8,128)(2,1)S(1)}, bf16[4,2,32,1024]{3,2,1,0:T(8,128)(2,1)}, u32[]{:S(2)}, u32[]{:S(2)}) collective-permute-start(bf16[4,2,32,1024]{3,2,1,0:T(8,128)(2,1)S(1)} %pad_maximum_fusion.n0), channel_id=1, source_target_pairs={{0,2},{1,3},{2,0},{3,1},{4,6},{5,7},{6,4},{7,5},{8,10},{9,11},{10,... | collective-permute-start | bytes 1572872 | tf_op jit(solution)/shard_map/ppermute | solution.py:409
  31.4 16.1 %collective-permute-start.15 = (bf16[4,2,32,1024]{3,2,1,0:T(8,128)(2,1)S(1)}, bf16[4,2,32,1024]{3,2,1,0:T(8,128)(2,1)}, u32[]{:S(2)}, u32[]{:S(2)}) collective-permute-start(bf16[4,2,32,1024]{3,2,1,0:T(8,128)(2,1)S(1)} %pad_maximum_fusion.n0), channel_id=1, source_target_pairs={{0,1},{1,2},{2,3},{3,0},{4,5},{5,6},{6,7},{7,4},{8,9},{9,10},{10,1... | collective-permute-start | bytes 1572872 | tf_op jit(solution)/shard_map/ppermute | solution.py:409
  34.0 15.2 %collective-permute-start.3 = (bf16[4,64,1024]{2,1,0:T(8,128)(2,1)S(1)}, bf16[4,64,1024]{2,1,0:T(8,128)(2,1)S(1)}, u32[]{:S(2)}, u32[]{:S(2)}) collective-permute-start(bf16[4,64,1024]{2,1,0:T(8,128)(2,1)S(1)} %get-tuple-element.44), channel_id=1, source_target_pairs={{0,16},{1,17},{2,18},{3,19},{4,20},{5,21},{6,22},{7,23},{8,24},{9,... | collective-permute-start | bytes 1572872 | tf_op jit(solution)/shard_map/ppermute | solution.py:409
  49.1 67.3 %collective-permute-start.18 = (bf16[1024,1024]{1,0:T(8,128)(2,1)S(1)}, bf16[1024,1024]{1,0:T(8,128)(2,1)S(1)}, u32[]{:S(2)}, u32[]{:S(2)}) collective-permute-start(bf16[1024,1024]{1,0:T(8,128)(2,1)S(1)} %shard_map.68.own), channel_id=1, source_target_pairs={{0,32},{1,33},{2,34},{3,35},{4,36},{5,37},{6,38},{7,39},{8,40},{9,... | collective-permute-start | bytes 6291464 | tf_op jit(solution)/shard_map/ppermute | solution.py:409
  49.3 17.9 %collective-permute-start.4 = (bf16[4,64,1024]{2,1,0:T(8,128)(2,1)S(1)}, bf16[4,64,1024]{2,1,0:T(8,128)(2,1)S(1)}, u32[]{:S(2)}, u32[]{:S(2)}) collective-permute-start(bf16[4,64,1024]{2,1,0:T(8,128)(2,1)S(1)} %collective-permute-done.3.mine), channel_id=1, source_target_pairs={{0,32},{1,33},{2,34},{3,35},{4,36},{5,37},{6,38},{7,39},{8,40},{9,... | collective-permute-start | bytes 1572872 | tf_op jit(solution)/shard_map/ppermute | solution.py:409
  49.9 12.1 %collective-permute-start.2 = (bf16[128,1024]{1,0:T(8,128)(2,1)S(1)}, bf16[128,1024]{1,0:T(8,128)(2,1)S(1)}, u32[]{:S(2)}, u32[]{:S(2)}) collective-permute-start(bf16[128,1024]{1,0:T(8,128)(2,1)S(1)} %get-tuple-element.81), channel_id=1, source_target_pairs={{0,12},{1,13},{2,14},{3,15},{4,0},{5,1},{6,2},{7,3},{8,4},{9,5},{1... | collective-permute-start | bytes 786440 | tf_op jit(solution)/shard_map/ppermute | solution.py:409
  53.6 21.0 %collective-permute-start.21 = (bf16[256,1024]{1,0:T(8,128)(2,1)S(1)}, bf16[256,1024]{1,0:T(8,128)(2,1)S(1)}, u32[]{:S(2)}, u32[]{:S(2)}) collective-permute-start(bf16[256,1024]{1,0:T(8,128)(2,1)S(1)} %get-tuple-element.53.refs_8_), channel_id=1, source_target_pairs={{0,3},{1,0},{2,1},{3,2},{4,7},{5,4},{6,5},{7,6},{8,11},{9,8},{10,9... | collective-permute-start | bytes 1572872 | tf_op jit(solution)/shard_map/ppermute | solution.py:409
  62.0 15.9 %collective-permute-start.20 = (bf16[256,1024]{1,0:T(8,128)(2,1)S(1)}, bf16[256,1024]{1,0:T(8,128)(2,1)S(1)}, u32[]{:S(2)}, u32[]{:S(2)}) collective-permute-start(bf16[256,1024]{1,0:T(8,128)(2,1)S(1)} %get-tuple-element.53.refs_8_), channel_id=1, source_target_pairs={{0,2},{1,3},{2,0},{3,1},{4,6},{5,7},{6,4},{7,5},{8,10},{9,11},{10,... | collective-permute-start | bytes 1572872 | tf_op jit(solution)/shard_map/ppermute | solution.py:409
  63.3 11.3 %collective-permute-start = (bf16[128,1024]{1,0:T(8,128)(2,1)S(1)}, bf16[128,1024]{1,0:T(8,128)(2,1)S(1)}, u32[]{:S(2)}, u32[]{:S(2)}) collective-permute-start(bf16[128,1024]{1,0:T(8,128)(2,1)S(1)} %get-tuple-element.83), channel_id=1, source_target_pairs={{0,4},{1,5},{2,6},{3,7},{4,8},{5,9},{6,10},{7,11},{8,12},{9,13},{1... | collective-permute-start | bytes 786440 | tf_op jit(solution)/shard_map/ppermute | solution.py:409
  67.2 16.7 %collective-permute-start.19 = (bf16[256,1024]{1,0:T(8,128)(2,1)S(1)}, bf16[256,1024]{1,0:T(8,128)(2,1)S(1)}, u32[]{:S(2)}, u32[]{:S(2)}) collective-permute-start(bf16[256,1024]{1,0:T(8,128)(2,1)S(1)} %get-tuple-element.53.refs_8_), channel_id=1, source_target_pairs={{0,1},{1,2},{2,3},{3,0},{4,5},{5,6},{6,7},{7,4},{8,9},{9,10},{10,1... | collective-permute-start | bytes 1572872 | tf_op jit(solution)/shard_map/ppermute | solution.py:409
  74.6 10.5 %collective-permute-start.6 = (bf16[128,1024]{1,0:T(8,128)(2,1)S(1)}, bf16[128,1024]{1,0:T(8,128)(2,1)S(1)}, u32[]{:S(2)}, u32[]{:S(2)}) collective-permute-start(bf16[128,1024]{1,0:T(8,128)(2,1)S(1)} %get-tuple-element.47), channel_id=1, source_target_pairs={{0,8},{1,9},{2,10},{3,11},{4,12},{5,13},{6,14},{7,15},{8,0},{9,1},... | collective-permute-start | bytes 786440 | tf_op jit(solution)/shard_map/ppermute | solution.py:409
  88.7 15.2 %collective-permute-start.22 = (bf16[2,128,1024]{2,1,0:T(8,128)(2,1)S(1)}, bf16[2,128,1024]{2,1,0:T(8,128)(2,1)S(1)}, u32[]{:S(2)}, u32[]{:S(2)}) collective-permute-start(bf16[2,128,1024]{2,1,0:T(8,128)(2,1)S(1)} %get-tuple-element.55), channel_id=1, source_target_pairs={{0,12},{1,13},{2,14},{3,15},{4,0},{5,1},{6,2},{7,3},{8,4},{9,5},{1... | collective-permute-start | bytes 1572872 | tf_op jit(solution)/shard_map/ppermute | solution.py:409
  91.6 12.4 %collective-permute-start.23 = (bf16[2,128,1024]{2,1,0:T(8,128)(2,1)S(1)}, bf16[2,128,1024]{2,1,0:T(8,128)(2,1)S(1)}, u32[]{:S(2)}, u32[]{:S(2)}) collective-permute-start(bf16[2,128,1024]{2,1,0:T(8,128)(2,1)S(1)} %get-tuple-element.56), channel_id=1, source_target_pairs={{0,8},{1,9},{2,10},{3,11},{4,12},{5,13},{6,14},{7,15},{8,0},{9,1},... | collective-permute-start | bytes 1572872 | tf_op jit(solution)/shard_map/ppermute | solution.py:409
  91.6 16.0 %collective-permute-start.24 = (bf16[2,128,1024]{2,1,0:T(8,128)(2,1)S(1)}, bf16[2,128,1024]{2,1,0:T(8,128)(2,1)S(1)}, u32[]{:S(2)}, u32[]{:S(2)}) collective-permute-start(bf16[2,128,1024]{2,1,0:T(8,128)(2,1)S(1)} %get-tuple-element.57), channel_id=1, source_target_pairs={{0,4},{1,5},{2,6},{3,7},{4,8},{5,9},{6,10},{7,11},{8,12},{9,13},{1... | collective-permute-start | bytes 1572872 | tf_op jit(solution)/shard_map/ppermute | solution.py:409
  144.2 12.8 %collective-permute-start.34 = (bf16[2,128,512]{2,1,0:T(8,128)(2,1)S(1)}, bf16[2,128,512]{2,1,0:T(8,128)(2,1)S(1)}, u32[]{:S(2)}, u32[]{:S(2)}) collective-permute-start(bf16[2,128,512]{2,1,0:T(8,128)(2,1)S(1)} %pad_maximum_fusion.2.refs_8_), channel_id=1, source_target_pairs={{0,12},{1,13},{2,14},{3,15},{4,0},{5,1},{6,2},{7,3},{8,4},{9,5},{1... | collective-permute-start | bytes 786440 | tf_op jit(solution)/shard_map/ppermute | solution.py:409
  150.7 24.2 %collective-permute-start.41 = (bf16[2,128,1024]{2,1,0:T(8,128)(2,1)S(1)}, bf16[2,128,1024]{2,1,0:T(8,128)(2,1)S(1)}, u32[]{:S(2)}, u32[]{:S(2)}) collective-permute-start(bf16[2,128,1024]{2,1,0:T(8,128)(2,1)S(1)} %pad_maximum_fusion.1.r0), channel_id=1, source_target_pairs={{0,12},{1,13},{2,14},{3,15},{4,0},{5,1},{6,2},{7,3},{8,4},{9,5},{1... | collective-permute-start | bytes 1572872 | tf_op jit(solution)/shard_map/ppermute | solution.py:409
  151.7 23.2 %collective-permute-start.40 = (bf16[2,128,1024]{2,1,0:T(8,128)(2,1)S(1)}, bf16[2,128,1024]{2,1,0:T(8,128)(2,1)S(1)}, u32[]{:S(2)}, u32[]{:S(2)}) collective-permute-start(bf16[2,128,1024]{2,1,0:T(8,128)(2,1)S(1)} %pad_maximum_fusion.1.r0), channel_id=1, source_target_pairs={{0,8},{1,9},{2,10},{3,11},{4,12},{5,13},{6,14},{7,15},{8,0},{9,1},... | collective-permute-start | bytes 1572872 | tf_op jit(solution)/shard_map/ppermute | solution.py:409
  151.7 23.2 %collective-permute-start.39 = (bf16[2,128,1024]{2,1,0:T(8,128)(2,1)S(1)}, bf16[2,128,1024]{2,1,0:T(8,128)(2,1)S(1)}, u32[]{:S(2)}, u32[]{:S(2)}) collective-permute-start(bf16[2,128,1024]{2,1,0:T(8,128)(2,1)S(1)} %pad_maximum_fusion.1.r0), channel_id=1, source_target_pairs={{0,4},{1,5},{2,6},{3,7},{4,8},{5,9},{6,10},{7,11},{8,12},{9,13},{1... | collective-permute-start | bytes 1572872 | tf_op jit(solution)/shard_map/ppermute | solution.py:409
  152.8 18.1 %collective-permute-start.33 = (bf16[2,128,512]{2,1,0:T(8,128)(2,1)S(1)}, bf16[2,128,512]{2,1,0:T(8,128)(2,1)S(1)}, u32[]{:S(2)}, u32[]{:S(2)}) collective-permute-start(bf16[2,128,512]{2,1,0:T(8,128)(2,1)S(1)} %pad_maximum_fusion.2.refs_8_), channel_id=1, source_target_pairs={{0,8},{1,9},{2,10},{3,11},{4,12},{5,13},{6,14},{7,15},{8,0},{9,1},... | collective-permute-start | bytes 786440 | tf_op jit(solution)/shard_map/ppermute | solution.py:409
  157.0 16.6 %collective-permute-start.32 = (bf16[2,128,512]{2,1,0:T(8,128)(2,1)S(1)}, bf16[2,128,512]{2,1,0:T(8,128)(2,1)S(1)}, u32[]{:S(2)}, u32[]{:S(2)}) collective-permute-start(bf16[2,128,512]{2,1,0:T(8,128)(2,1)S(1)} %pad_maximum_fusion.2.refs_8_), channel_id=1, source_target_pairs={{0,4},{1,5},{2,6},{3,7},{4,8},{5,9},{6,10},{7,11},{8,12},{9,13},{1... | collective-permute-start | bytes 786440 | tf_op jit(solution)/shard_map/ppermute | solution.py:409
  177.8 10.5 %collective-permute-start.42 = (bf16[256,1024]{1,0:T(8,128)(2,1)S(1)}, bf16[256,1024]{1,0:T(8,128)(2,1)S(1)}, u32[]{:S(2)}, u32[]{:S(2)}) collective-permute-start(bf16[256,1024]{1,0:T(8,128)(2,1)S(1)} %get-tuple-element.78), channel_id=1, source_target_pairs={{0,1},{1,2},{2,3},{3,0},{4,5},{5,6},{6,7},{7,4},{8,9},{9,10},{10,1... | collective-permute-start | bytes 1572872 | tf_op jit(solution)/shard_map/ppermute | solution.py:409
  177.9 16.0 %collective-permute-start.43 = (bf16[256,1024]{1,0:T(8,128)(2,1)S(1)}, bf16[256,1024]{1,0:T(8,128)(2,1)S(1)}, u32[]{:S(2)}, u32[]{:S(2)}) collective-permute-start(bf16[256,1024]{1,0:T(8,128)(2,1)S(1)} %get-tuple-element.79), channel_id=1, source_target_pairs={{0,2},{1,3},{2,0},{3,1},{4,6},{5,7},{6,4},{7,5},{8,10},{9,11},{10,... | collective-permute-start | bytes 1572872 | tf_op jit(solution)/shard_map/ppermute | solution.py:409
  181.1 13.7 %collective-permute-start.44 = (bf16[256,1024]{1,0:T(8,128)(2,1)S(1)}, bf16[256,1024]{1,0:T(8,128)(2,1)S(1)}, u32[]{:S(2)}, u32[]{:S(2)}) collective-permute-start(bf16[256,1024]{1,0:T(8,128)(2,1)S(1)} %get-tuple-element.80), channel_id=1, source_target_pairs={{0,3},{1,0},{2,1},{3,2},{4,7},{5,4},{6,5},{7,6},{8,11},{9,8},{10,9... | collective-permute-start | bytes 1572872 | tf_op jit(solution)/shard_map/ppermute | solution.py:409
  (29 other events, 260.0 us)

commit v2 on v1

--- a/solution.py
+++ b/solution.py
@@ -15,6 +15,7 @@
 BF = jnp.bfloat16
 F32 = jnp.float32
 INTERPRET = False
+HBM = pltpu.HBM
 KEEPS = ((0, 1), (0, 2), (0, 3), (1, 2), (1, 3), (2, 3))
 LAYER = ("zh", "co")
 
@@ -119,59 +120,50 @@
     return zl * 16 + jnp.where(core == 0, g * 4 + h, h * 4 + g)
 
 
-def heads_kernel(at, tokens, near, far, sems):
-    zl, g, h, core = (at[i] for i in range(4))
+def slice_kernel(at, tokens, out, sem):
+    width = out.shape[1]
+    source = wide(1 - at[0], width)
+    copy = pltpu.make_async_copy(tokens.at[at[3], :, source], out, sem)
+    copy.start()
+    copy.wait()
+
+
+def far_half(at, tokens):
+    rows, width = tokens.shape[1:]
+    return call(
+        slice_kernel,
+        shape((rows, width // 2), BF),
+        in_specs=[pl.BlockSpec(memory_space=pltpu.SMEM), pl.BlockSpec(memory_space=HBM)],
+        out_specs=pl.BlockSpec(memory_space=pltpu.VMEM),
+        scratch_shapes=[pltpu.SemaphoreType.DMA],
+    )(at, tokens)
+
+
+def blocks_kernel(at, tokens, mine, other, o0, o1, o2, o3, sems):
+    zl, g, core = at[0], at[1], at[3]
     rows, width = tokens.shape[1:]
     part = width // 32
     copies = []
-    for k in range(4):
+    for k, out in enumerate((o0, o1, o2, o3)):
         for i in range(4):
-            source = wide(place(core, zl, lax.rem(g + k, 4), i), part)
-            for m in range(2):
-                copies.append((
-                    tokens.at[core if m == 0 else 1 - core, :, source],
-                    near.at[k, pl.ds(m * rows, rows), pl.ds(i * part, part)],
-                ))
-            source = wide(place(1 - core, 1 - zl, lax.rem(h + k, 4), i), part)
-            copies.append((tokens.at[core, :, source], far.at[k, :, pl.ds(i * part, part)]))
+            near = wide(place(core, zl, lax.rem(g + k, 4), i), part)
+            far = wide(place(core, 0, lax.rem(g + k, 4), i), part)
+            sources = (tokens.at[core, :, near], tokens.at[1 - core, :, near], mine.at[:, far], other.at[:, far])
+            for r, source in enumerate(sources):
+                copies.append((source, out.at[pl.ds(r * rows, rows), pl.ds(i * part, part)]))
     run_copies(copies, sems)
 
 
-def token_blocks(at, tokens):
+def token_blocks(at, tokens, mine, other):
     rows, width = tokens.shape[1:]
     block = pl.BlockSpec(memory_space=pl.ANY)
     return call(
-        heads_kernel,
-        (shape((4, 2 * rows, width // 8), BF), shape((4, rows, width // 8), BF)),
-        in_specs=[pl.BlockSpec(memory_space=pltpu.SMEM), block],
-        out_specs=(block, block),
-        scratch_shapes=[pltpu.SemaphoreType.DMA((48,))],
-    )(at, tokens)
-
-
-def pair_kernel(at, mine, other, o0, o1, o2, o3, sems):
-    g, h = at[1], at[2]
-    rows = mine.shape[1]
-    part = mine.shape[2] // 4
-    copies = []
-    for k, out in enumerate((o0, o1, o2, o3)):
-        for i in range(4):
-            source = mine.at[lax.rem(i - h + 4, 4), :, wide(lax.rem(g + k, 4), part)]
-            copies.append((source, out.at[pl.ds(0, rows), pl.ds(i * part, part)]))
-        copies.append((other.at[k], out.at[pl.ds(rows, rows), :]))
-    run_copies(copies, sems)
-
-
-def pair_blocks(at, mine, other):
-    rows, span = mine.shape[1:]
-    block = pl.BlockSpec(memory_space=pl.ANY)
-    return call(
-        pair_kernel,
-        (shape((2 * rows, span), BF),) * 4,
-        in_specs=[pl.BlockSpec(memory_space=pltpu.SMEM), block, block],
+        blocks_kernel,
+        (shape((4 * rows, width // 8), BF),) * 4,
+        in_specs=[pl.BlockSpec(memory_space=pltpu.SMEM), pl.BlockSpec(memory_space=HBM), block, block],
         out_specs=(block,) * 4,
-        scratch_shapes=[pltpu.SemaphoreType.DMA((20,))],
-    )(at, mine, other)
+        scratch_shapes=[pltpu.SemaphoreType.DMA((64,))],
+    )(at, tokens, mine, other)
 
 
 def sums_kernel(repeat, head, core, tokens, grads, y0, spread, g4):
@@ -226,42 +218,37 @@
     return dict(in_specs=[pl.BlockSpec(memory_space=pltpu.SMEM)] + [vmem] * count)
 
 
-def values_kernel(at, *refs):
-    tokens, w, outs = refs[:8], refs[8:12], refs[12:]
+def values_kernel(far, at, *refs):
+    tokens, w, outs = refs[:4], refs[4:8], refs[8:]
     part = w[0].shape[0]
-    rows = tokens[0].shape[0]
-    for k in range(4):
+    rows = outs[0].shape[0]
+    mine = slice(rows, 2 * rows) if far else slice(0, rows)
+    for k in range(0, 4, 2):
         total = None
         for j in range(4):
             cols = wide(lax.rem(at[2] - j + 4, 4), part)
-            lhs = jnp.concatenate([tokens[k][:, cols], tokens[4 + k][:, cols]], 0)
+            lhs = jnp.concatenate([tokens[k][mine, cols], tokens[k + 1][mine, cols]], 0)
             term = jnp.dot(lhs, w[j][...], preferred_element_type=F32)
             total = term if total is None else total + term
-        outs[k][0] = total[:rows].astype(BF)
-        outs[k][1] = total[rows:].astype(BF)
-
-
-def partial_values(at, near, far, blocks):
-    rows = near[0].shape[0]
-    out = [shape((2, rows, blocks[0].shape[1]), BF)] * 4
-    return call(values_kernel, out, **small(12))(at, *near, *far, *blocks)
-
-
-def gathered_kernel(m0, m1, m2, m3, own, give, far_keep, far_give):
-    rows = own.shape[0]
-    for z in range(2):
-        total = (m0[z].astype(F32) + m1[z].astype(F32)) + (m2[z].astype(F32) + m3[z].astype(F32))
-        if z == 0:
-            own[...] = total[:rows]
-            give[...] = total[rows:].astype(BF)
-        else:
-            far_keep[...] = total[:rows].astype(BF)
-            far_give[...] = total[rows:].astype(BF)
+        outs[k][...] = total[:rows].astype(BF)
+        outs[k + 1][...] = total[rows:].astype(BF)
+
+
+def partial_values(at, tokens, blocks, far):
+    out = [shape((tokens[0].shape[0] // 2, blocks[0].shape[1]), BF)] * 4
+    return call(functools.partial(values_kernel, far), out, **small(8))(at, *tokens, *blocks)
+
+
+def gathered_kernel(m0, m1, m2, m3, keep, give):
+    rows = keep.shape[0]
+    for i, out in enumerate((keep, give)):
+        p = [m[i * rows : (i + 1) * rows, :].astype(F32) for m in (m0, m1, m2, m3)]
+        out[...] = ((p[0] + p[1]) + (p[2] + p[3])).astype(out.dtype)
 
 
 def turn_over_kernel(at, *refs):
-    tokens, cs, out = refs[:8], refs[8:12], refs[12]
-    rows = tokens[0].shape[0]
+    tokens, cs, out = refs[:4], refs[4:8], refs[8]
+    rows = tokens[0].shape[0] // 2
     head = cs[0].shape[2] // 4
     for k in range(4):
         for z in range(2):
@@ -270,14 +257,14 @@
                 which = jnp.where(at[3] == 0, at[1], i)
                 c = cs[k][z, :, wide(which, head)].astype(F32)
                 add += [c, c]
-            x = tokens[z * 4 + k][...].astype(F32) + jnp.concatenate(add, 1)
+            x = tokens[k][z * rows : (z + 1) * rows, :].astype(F32) + jnp.concatenate(add, 1)
             begin = (k * 2 + z) * rows
             out[:, begin : begin + rows] = x.astype(BF).T
 
 
-def turn_over(at, near, far, cs):
-    rows, span = near[0].shape
-    return call(turn_over_kernel, shape((span, 8 * rows), BF), **small(12))(at, *near, *far, *cs)
+def turn_over(at, tokens, cs):
+    rows, span = tokens[0].shape
+    return call(turn_over_kernel, shape((span, 4 * rows), BF), **small(8))(at, *tokens, *cs)
 
 
 def short_kernel(q0, q1, q2, q3, out):
@@ -285,9 +272,11 @@
     out[...] = total.astype(BF)
 
 
-def square_kernel(at, n0, n1, n2, n3, out):
+def square_kernel(swapped, at, n0, n1, n2, n3, out):
     quarter = n0.shape[2]
     zl, g, h, core = (at[i] for i in range(4))
+    if swapped:
+        g, h, core = h, g, 1 - core
     for j, n in enumerate((n0, n1, n2, n3)):
         for k in range(4):
             for z in range(2):
@@ -391,12 +380,20 @@
     )(at, *args)
 
 
-def wgrad_kernel(at, turned, r0, r1, r2, r3, *outs):
-    right = jnp.concatenate([r[z] for r in (r0, r1, r2, r3) for z in range(2)], 0)
+def wgrad_first_kernel(at, turned, *refs):
+    near, far, out, right = refs[:4], refs[4:8], refs[8], refs[9]
+    for k in range(4):
+        for z, r in enumerate((near[k], far[k])):
+            begin = (k * 2 + z) * r.shape[0]
+            right[begin : begin + r.shape[0], :] = r[...]
+    wgrad_kernel((2,), at, turned, right, out)
+
+
+def wgrad_kernel(ahead, at, turned, right, *outs):
     part = outs[0].shape[0]
-    for j in range(4):
+    for j, out in zip(ahead, outs):
         rows = wide(lax.rem(at[2] + j, 4), part)
-        outs[j][...] = jnp.dot(turned[rows, :], right, preferred_element_type=F32).astype(BF)
+        out[...] = jnp.dot(turned[rows, :], right[...], preferred_element_type=F32).astype(BF)
 
 
 AXES = ("zh", "co", "zl", "y", "x")
@@ -421,6 +418,10 @@
 
 def to_h(v, k):
     return ring(v, k, 1)
+
+
+def ring_all(vs, way):
+    return [vs[0] if k == 0 else to_g(vs[k], way * k) for k in range(4)]
 
 
 def along_x(v, k):
@@ -462,28 +463,31 @@
     wide32 = shape((rows, kv), F32)
     half = shape((rows, kv), BF)
 
-    near, far = token_blocks(at, stream_in)
+    stream = stream_in if INTERPRET else pltpu.with_memory_space_constraint(stream_in, HBM)
+    far = far_half(at, stream)
     far = to_z(far)
-    near = [to_g(near[k], k) for k in range(4)]
     scaled, *quarters = masked_weights(x.reshape(1), mask_logits[0], gumbel_noise[0], weight, gain)
+    blocks = [to_h(scaled, k) for k in range(4)]
     quarters = [along_x(quarters[k], k) for k in range(4)]
-    blocks = [to_h(scaled, k) for k in range(4)]
     swapped = to_core(far)
-    far = pair_blocks(at, far, swapped)
-    far = [to_g(far[k], k) for k in range(4)]
-
+    tokens = token_blocks(at, stream, far, swapped)
+    tokens = [to_g(tokens[k], k) for k in range(4)]
     short = call(short_kernel, shape(quarters[0].shape, BF))(*quarters)
     short = jnp.stack([short, to_z(short)])
     short = jnp.stack([to_g(short, k) for k in range(4)])
     square = [to_h(short, k) for k in range(4)]
-    n = call(square_kernel, shape((kv, kv), BF), **small(4))(at, *square)
-    n_other = to_core(n)
-
-    u = partial_values(at, near, far, blocks)
-    u = [to_g(u[k], -k) for k in range(4)]
-    mine, give, far_keep, far_give = call(gathered_kernel, (wide32, half, half, half))(*u)
+    swapped = [to_core(v) for v in square]
+    n = call(functools.partial(square_kernel, 0), shape((kv, kv), BF), **small(4))(at, *square)
+    n_other = call(functools.partial(square_kernel, 1), shape((kv, kv), BF), **small(4))(at, *swapped)
+
+    u_far = partial_values(at, tokens, blocks, True)
+    u_far = ring_all(u_far, -1)
+    u_near = partial_values(at, tokens, blocks, False)
+    u_near = ring_all(u_near, -1)
+    far_keep, far_give = call(gathered_kernel, (half, half))(*u_far)
     far_mine = to_z(far_keep)
     far_theirs = to_z_core(far_give)
+    mine, give = call(gathered_kernel, (wide32, half))(*u_near)
     theirs = to_core(give)
     y0, spread, g4 = token_sums(at[3:4], stream_in, stream_grad, head)
 
@@ -509,12 +513,18 @@
         functools.partial(send_kernel, width), (half, half),
         at, n, n_other, g4, g_in, value, sums, sigma,
     )
-    right = jnp.stack([jnp.concatenate([keep, to_core(give)]), jnp.concatenate([to_z(keep), to_z_core(give)])])
-    right = [to_g(right, k) for k in range(4)]
-    turned = turn_over(at, near, far, cs)
-    term = call(wgrad_kernel, [shape((part, kv), BF)] * 4, **small(5))(at, turned, *right)
-    term = [to_h(term[k], k) for k in range(4)]
-    return logit_gradient(mask_logits[0], gumbel_noise[0], weight, gain, term)[None]
+    near = to_core(give)
+    far, far_give = to_z(keep), to_z_core(give)
+    near = ring_all([jnp.concatenate([keep, near])] * 4, 1)
+    far = ring_all([jnp.concatenate([far, far_give])] * 4, 1)
+    turned = turn_over(at, tokens, cs)
+    block = shape((part, kv), BF)
+    t2, right = call(wgrad_first_kernel, [block, shape(turned.shape, BF)], **small(9))(at, turned, *near, *far)
+    t2 = to_h(t2, 2)
+    t1, t3 = call(functools.partial(wgrad_kernel, (1, 3)), [block] * 2, **small(2))(at, turned, right)
+    t1, t3 = to_h(t1, 1), to_h(t3, 3)
+    (t0,) = call(functools.partial(wgrad_kernel, (0,)), [block], **small(2))(at, turned, right)
+    return logit_gradient(mask_logits[0], gumbel_noise[0], weight, gain, [t0, t1, t2, t3])[None]
 
 
 def solution(mesh):

time: 197 us -> 183 us (0.929)
  waiting for transfers between devices: 106 us -> 86.4 us
  starting transfers between devices: 63.4 us -> 69.2 us
  local copies, waits for them, and re-layouts: 3.64 us -> 0.28 us
  Pallas kernels: 22.8 us -> 25.7 us
    ppermute x45 -> x51, waiting for transfers between devices: 106 us -> 86.4 us  [move(): return lax.ppermute(v, AXES, pairs)]
    ppermute x45 -> x51, starting transfers between devices: 63.4 us -> 69.2 us  [move(): return lax.ppermute(v, AXES, pairs)]
    unnamed x16 -> x12, local copies, waits for them, and re-layouts: 3.33 us -> 0.04 us
    pallas_call x7 -> x12, Pallas kernels: 11.9 us -> 14.8 us  [the longest x2 3.57 us: partial_values(): call(functools.partial(values_kernel, far), out, **small(8))]
  transfers between devices with their start and end apart: 45 -> 51, of which waited for: 25 -> 28; matrix products, arithmetic and copies ran while one was open for 0% -> 1% of each run, Pallas kernels for 6% -> 7%
where the time goes in v2:
time: 183 us
  waiting for transfers between devices  86.4 us (47%)
  starting transfers between devices  69.2 us (38%)
  Pallas kernels  25.7 us (14%)
    ppermute x51, waiting for transfers between devices, move(): return lax.ppermute(v, AXES, pairs)  86.4 us
    ppermute x51, starting transfers between devices, move(): return lax.ppermute(v, AXES, pairs)  69.2 us
    pallas_call x3, Pallas kernels, chain_call(): call(kernel, out, in_specs=[pl.BlockSpec(memory_space=pltpu.SMEM)] + [pl....  6.8 us
  transfers between devices with their start and end apart: 51, of which 28 were waited for; matrix products, arithmetic and copies ran while one was open for 1% of the time, Pallas kernels for 7%

profile of v2, /device:TPU:0, one launch (start us, length us, event | category | flops | bytes accessed | tf_op | source)
XLA Modules:
  0.0 182.7 jit_solution(5308511694244396199)
XLA Ops:
  3.8 11.9 %collective-permute-done.mine = bf16[64,4096]{1,0:T(8,128)(2,1)S(1)} collective-permute-done((bf16[64,4096]{1,0:T(8,128)(2,1)S(1)}, bf16[64,4096]{1,0:T(8,128)(2,1)S(1)}, u32[]{:S(2)}, u32[]{:S(2)}) %collective-permute-start) | collective-permute-done | bytes 524320 | tf_op jit(solution)/shard_map/ppermute | solution.py:406
  19.0 2.7 %collective-permute-start.6 = (bf16[32,1024]{1,0:T(8,128)(2,1)S(1)}, bf16[32,1024]{1,0:T(8,128)(2,1)S(1)}, u32[]{:S(2)}, u32[]{:S(2)}) collective-permute-start(bf16[32,1024]{1,0:T(8,128)(2,1)S(1)} %get-tuple-element.51), channel_id=1, source_target_pairs={{0,2},{1,3},{2,0},{3,1},{4,6},{5,7},{6,4},{7,5},{8,10},{9,11},{10,... | collective-permute-start | bytes 196616 | tf_op jit(solution)/shard_map/ppermute | solution.py:406
  35.7 2.9 %collective-permute-start.10 = (bf16[2,32,1024]{2,1,0:T(8,128)(2,1)S(1)}, bf16[2,32,1024]{2,1,0:T(8,128)(2,1)S(1)}, u32[]{:S(2)}, u32[]{:S(2)}) collective-permute-start(bf16[2,32,1024]{2,1,0:T(8,128)(2,1)S(1)} %get-tuple-element.86), channel_id=1, source_target_pairs={{0,8},{1,9},{2,10},{3,11},{4,12},{5,13},{6,14},{7,15},{8,0},{9,1},... | collective-permute-start | bytes 393224 | tf_op jit(solution)/shard_map/ppermute | solution.py:406
  38.6 2.4 %shard_map.65 = (bf16[256,1024]{1,0:T(8,128)(2,1)S(1)}, bf16[256,1024]{1,0:T(8,128)(2,1)S(1)}, bf16[256,1024]{1,0:T(8,128)(2,1)S(1)}, bf16[256,1024]{1,0:T(8,128)(2,1)S(1)}) custom-call(s32[5]{0:T(128)S(1)} %stack.56.at, bf16[2,64,8192]{2,1,0:T(8,128)(2,1)} %tokens.5, bf16[64,4096]{1,0:T(8,128)(2,1)S(1)} %collective-permute-done.mine, ...), custom_call_target="tpu_custom_call" | custom-call | tf_op jit(solution)/shard_map/pallas_call | solution.py:160
  41.1 2.4 %collective-permute-done.10 = bf16[2,32,1024]{2,1,0:T(8,128)(2,1)S(1)} collective-permute-done((bf16[2,32,1024]{2,1,0:T(8,128)(2,1)S(1)}, bf16[2,32,1024]{2,1,0:T(8,128)(2,1)S(1)}, u32[]{:S(2)}, u32[]{:S(2)}) %collective-permute-start.10) | collective-permute-done | bytes 131104 | tf_op jit(solution)/shard_map/ppermute | solution.py:406
  45.2 4.3 %collective-permute-done.11 = bf16[2,32,1024]{2,1,0:T(8,128)(2,1)S(1)} collective-permute-done((bf16[2,32,1024]{2,1,0:T(8,128)(2,1)S(1)}, bf16[2,32,1024]{2,1,0:T(8,128)(2,1)S(1)}, u32[]{:S(2)}, u32[]{:S(2)}) %collective-permute-start.11) | collective-permute-done | bytes 131104 | tf_op jit(solution)/shard_map/ppermute | solution.py:406
  51.6 2.6 %collective-permute-start.4 = (bf16[256,1024]{1,0:T(8,128)(2,1)S(1)}, bf16[256,1024]{1,0:T(8,128)(2,1)S(1)}, u32[]{:S(2)}, u32[]{:S(2)}) collective-permute-start(bf16[256,1024]{1,0:T(8,128)(2,1)S(1)} %get-tuple-element.48), channel_id=1, source_target_pairs={{0,12},{1,13},{2,14},{3,15},{4,0},{5,1},{6,2},{7,3},{8,4},{9,5},{1... | collective-permute-start | bytes 1572872 | tf_op jit(solution)/shard_map/ppermute | solution.py:406
  56.4 2.5 %collective-permute-start.14 = (bf16[4,2,32,1024]{3,2,1,0:T(8,128)(2,1)S(1)}, bf16[4,2,32,1024]{3,2,1,0:T(8,128)(2,1)S(1)}, u32[]{:S(2)}, u32[]{:S(2)}) collective-permute-start(bf16[4,2,32,1024]{3,2,1,0:T(8,128)(2,1)S(1)} %pad_maximum_fusion.n0), channel_id=1, source_target_pairs={{0,3},{1,0},{2,1},{3,2},{4,7},{5,4},{6,5},{7,6},{8,11},{9,8},{10,9... | collective-permute-start | bytes 1572872 | tf_op jit(solution)/shard_map/ppermute | solution.py:406
  59.0 7.0 %collective-permute-done.3.refs_2_ = bf16[256,1024]{1,0:T(8,128)(2,1)S(1)} collective-permute-done((bf16[256,1024]{1,0:T(8,128)(2,1)S(1)}, bf16[256,1024]{1,0:T(8,128)(2,1)S(1)}, u32[]{:S(2)}, u32[]{:S(2)}) %collective-permute-start.3) | collective-permute-done | bytes 524320 | tf_op jit(solution)/shard_map/ppermute | solution.py:406
  65.9 9.4 %collective-permute-done.4.refs_3_ = bf16[256,1024]{1,0:T(8,128)(2,1)S(1)} collective-permute-done((bf16[256,1024]{1,0:T(8,128)(2,1)S(1)}, bf16[256,1024]{1,0:T(8,128)(2,1)S(1)}, u32[]{:S(2)}, u32[]{:S(2)}) %collective-permute-start.4) | collective-permute-done | bytes 524320 | tf_op jit(solution)/shard_map/ppermute | solution.py:406
  77.2 3.6 %collective-permute-start.26 = (bf16[128,1024]{1,0:T(8,128)(2,1)S(1)}, bf16[128,1024]{1,0:T(8,128)(2,1)S(1)}, u32[]{:S(2)}, u32[]{:S(2)}) collective-permute-start(bf16[128,1024]{1,0:T(8,128)(2,1)S(1)} %get-tuple-element.61), channel_id=1, source_target_pairs={{0,12},{1,13},{2,14},{3,15},{4,0},{5,1},{6,2},{7,3},{8,4},{9,5},{1... | collective-permute-start | bytes 786440 | tf_op jit(solution)/shard_map/ppermute | solution.py:406
  84.5 2.4 %collective-permute-start.22 = (bf16[128,1024]{1,0:T(8,128)(2,1)S(1)}, bf16[128,1024]{1,0:T(8,128)(2,1)S(1)}, u32[]{:S(2)}, u32[]{:S(2)}) collective-permute-start(bf16[128,1024]{1,0:T(8,128)(2,1)S(1)} %get-tuple-element.55), channel_id=1, source_target_pairs={{0,12},{1,13},{2,14},{3,15},{4,0},{5,1},{6,2},{7,3},{8,4},{9,5},{1... | collective-permute-start | bytes 786440 | tf_op jit(solution)/shard_map/ppermute | solution.py:406
  88.7 2.7 %collective-permute-done.28.m3 = bf16[128,1024]{1,0:T(8,128)(2,1)S(1)} collective-permute-done((bf16[128,1024]{1,0:T(8,128)(2,1)S(1)}, bf16[128,1024]{1,0:T(8,128)(2,1)S(1)}, u32[]{:S(2)}, u32[]{:S(2)}) %collective-permute-start.28) | collective-permute-done | bytes 262176 | tf_op jit(solution)/shard_map/ppermute | solution.py:406
  95.5 6.9 %collective-permute-done.24.m3 = bf16[128,1024]{1,0:T(8,128)(2,1)S(1)} collective-permute-done((bf16[128,1024]{1,0:T(8,128)(2,1)S(1)}, bf16[128,1024]{1,0:T(8,128)(2,1)S(1)}, u32[]{:S(2)}, u32[]{:S(2)}) %collective-permute-start.24) | collective-permute-done | bytes 262176 | tf_op jit(solution)/shard_map/ppermute | solution.py:406
  111.3 5.5 %collective-permute-start.31 = (bf16[64,1024]{1,0:T(8,128)(2,1)S(1)}, bf16[64,1024]{1,0:T(8,128)(2,1)S(1)}, u32[]{:S(2)}, u32[]{:S(2)}) collective-permute-start(bf16[64,1024]{1,0:T(8,128)(2,1)S(1)} %get-tuple-element.69), channel_id=1, source_target_pairs={{0,64},{1,65},{2,66},{3,67},{4,68},{5,69},{6,70},{7,71},{8,72},{9,... | collective-permute-start | bytes 393224 | tf_op jit(solution)/shard_map/ppermute | solution.py:406
  116.8 3.0 %collective-permute-done.31.c_in = bf16[64,1024]{1,0:T(8,128)(2,1)S(1)} collective-permute-done((bf16[64,1024]{1,0:T(8,128)(2,1)S(1)}, bf16[64,1024]{1,0:T(8,128)(2,1)S(1)}, u32[]{:S(2)}, u32[]{:S(2)}) %collective-permute-start.31) | collective-permute-done | bytes 131104 | tf_op jit(solution)/shard_map/ppermute | solution.py:406
  119.8 3.9 %shard_map.76 = (f32[2,64,1024]{2,1,0:T(8,128)S(1)}, f32[2,64,1024]{2,1,0:T(8,128)S(1)}, f32[2,64,128]{2,1,0:T(8,128)S(1)}, bf16[64,512]{1,0:T(8,128)(2,1)S(1)},...) custom-call(s32[5]{0:T(128)S(1)} %stack.56.at, ...), custom_call_target="tpu_custom_call" | custom-call | tf_op jit(solution)/shard_map/pallas_call | solution.py:375
  127.1 6.5 %collective-permute-done.38.g_in = bf16[64,1024]{1,0:T(8,128)(2,1)S(1)} collective-permute-done((bf16[64,1024]{1,0:T(8,128)(2,1)S(1)}, bf16[64,1024]{1,0:T(8,128)(2,1)S(1)}, u32[]{:S(2)}, u32[]{:S(2)}) %collective-permute-start.38) | collective-permute-done | bytes 131104 | tf_op jit(solution)/shard_map/ppermute | solution.py:406
  136.8 3.4 %collective-permute-start.36 = (bf16[2,128,512]{2,1,0:T(8,128)(2,1)S(1)}, bf16[2,128,512]{2,1,0:T(8,128)(2,1)S(1)}, u32[]{:S(2)}, u32[]{:S(2)}) collective-permute-start(bf16[2,128,512]{2,1,0:T(8,128)(2,1)S(1)} %pad_maximum_fusion.1.refs_4_), channel_id=1, source_target_pairs={{0,8},{1,9},{2,10},{3,11},{4,12},{5,13},{6,14},{7,15},{8,0},{9,1},... | collective-permute-start | bytes 786440 | tf_op jit(solution)/shard_map/ppermute | solution.py:406
  144.5 2.7 %collective-permute-start.46 = (bf16[128,1024]{1,0:T(8,128)(2,1)S(1)}, bf16[128,1024]{1,0:T(8,128)(2,1)S(1)}, u32[]{:S(2)}, u32[]{:S(2)}) collective-permute-start(bf16[128,1024]{1,0:T(8,128)(2,1)S(1)} %constant_dynamic-update-slice_fusion.2.refs_4_), channel_id=1, source_target_pairs={{0,8},{1,9},{2,10},{3,11},{4,12},{5,13},{6,14},{7,15},{8,0},{9,1},... | collective-permute-start | bytes 786440 | tf_op jit(solution)/shard_map/ppermute | solution.py:406
  155.9 2.8 %collective-permute-done.41.refs_2_ = bf16[128,1024]{1,0:T(8,128)(2,1)S(1)} collective-permute-done((bf16[128,1024]{1,0:T(8,128)(2,1)S(1)}, bf16[128,1024]{1,0:T(8,128)(2,1)S(1)}, u32[]{:S(2)}, u32[]{:S(2)}) %collective-permute-start.41) | collective-permute-done | bytes 262176 | tf_op jit(solution)/shard_map/ppermute | solution.py:406
  164.4 2.5 %collective-permute-start.50 = (bf16[256,1024]{1,0:T(8,128)(2,1)S(1)}, bf16[256,1024]{1,0:T(8,128)(2,1)S(1)}, u32[]{:S(2)}, u32[]{:S(2)}) collective-permute-start(bf16[256,1024]{1,0:T(8,128)(2,1)S(1)} %get-tuple-element.84), channel_id=1, source_target_pairs={{0,3},{1,0},{2,1},{3,2},{4,7},{5,4},{6,5},{7,6},{8,11},{9,8},{10,9... | collective-permute-start | bytes 1572872 | tf_op jit(solution)/shard_map/ppermute | solution.py:406
  169.1 4.9 %collective-permute-done.48.refs_1_ = bf16[256,1024]{1,0:T(8,128)(2,1)S(1)} collective-permute-done((bf16[256,1024]{1,0:T(8,128)(2,1)S(1)}, bf16[256,1024]{1,0:T(8,128)(2,1)S(1)}, u32[]{:S(2)}, u32[]{:S(2)}) %collective-permute-start.48) | collective-permute-done | bytes 524320 | tf_op jit(solution)/shard_map/ppermute | solution.py:406
  174.1 5.2 %collective-permute-done.50.refs_3_ = bf16[256,1024]{1,0:T(8,128)(2,1)S(1)} collective-permute-done((bf16[256,1024]{1,0:T(8,128)(2,1)S(1)}, bf16[256,1024]{1,0:T(8,128)(2,1)S(1)}, u32[]{:S(2)}, u32[]{:S(2)}) %collective-permute-start.50) | collective-permute-done | bytes 524320 | tf_op jit(solution)/shard_map/ppermute | solution.py:406
  (119 shorter events, 78.0 us)
Async XLA Ops:
  1.7 14.1 %collective-permute-start = (bf16[64,4096]{1,0:T(8,128)(2,1)S(1)}, bf16[64,4096]{1,0:T(8,128)(2,1)S(1)}, u32[]{:S(2)}, u32[]{:S(2)}) collective-permute-start(bf16[64,4096]{1,0:T(8,128)(2,1)S(1)} %shard_map.64), channel_id=1, source_target_pairs={{0,16},{1,17},{2,18},{3,19},{4,20},{5,21},{6,22},{7,23},{8,24},{9,... | collective-permute-start | bytes 1572872 | tf_op jit(solution)/shard_map/ppermute | solution.py:406
  15.7 20.0 %collective-permute-start.1 = (bf16[64,4096]{1,0:T(8,128)(2,1)S(1)}, bf16[64,4096]{1,0:T(8,128)(2,1)S(1)}, u32[]{:S(2)}, u32[]{:S(2)}) collective-permute-start(bf16[64,4096]{1,0:T(8,128)(2,1)S(1)} %collective-permute-done.mine), channel_id=1, source_target_pairs={{0,32},{1,33},{2,34},{3,35},{4,36},{5,37},{6,38},{7,39},{8,40},{9,... | collective-permute-start | bytes 1572872 | tf_op jit(solution)/shard_map/ppermute | solution.py:406
  27.9 23.7 %collective-permute-start.19 = (bf16[256,1024]{1,0:T(8,128)(2,1)S(1)}, bf16[256,1024]{1,0:T(8,128)(2,1)S(1)}, u32[]{:S(2)}, u32[]{:S(2)}) collective-permute-start(bf16[256,1024]{1,0:T(8,128)(2,1)S(1)} %get-tuple-element.53.refs_4_), channel_id=1, source_target_pairs={{0,1},{1,2},{2,3},{3,0},{4,5},{5,6},{6,7},{7,4},{8,9},{9,10},{10,1... | collective-permute-start | bytes 1572872 | tf_op jit(solution)/shard_map/ppermute | solution.py:406
  30.4 10.6 %collective-permute-start.9 = (bf16[2,32,1024]{2,1,0:T(8,128)(2,1)S(1)}, bf16[2,32,1024]{2,1,0:T(8,128)(2,1)S(1)}, u32[]{:S(2)}, u32[]{:S(2)}) collective-permute-start(bf16[2,32,1024]{2,1,0:T(8,128)(2,1)S(1)} %get-tuple-element.86), channel_id=1, source_target_pairs={{0,4},{1,5},{2,6},{3,7},{4,8},{5,9},{6,10},{7,11},{8,12},{9,13},{1... | collective-permute-start | bytes 393224 | tf_op jit(solution)/shard_map/ppermute | solution.py:406
  32.1 22.2 %collective-permute-start.20 = (bf16[256,1024]{1,0:T(8,128)(2,1)S(1)}, bf16[256,1024]{1,0:T(8,128)(2,1)S(1)}, u32[]{:S(2)}, u32[]{:S(2)}) collective-permute-start(bf16[256,1024]{1,0:T(8,128)(2,1)S(1)} %get-tuple-element.53.refs_4_), channel_id=1, source_target_pairs={{0,2},{1,3},{2,0},{3,1},{4,6},{5,7},{6,4},{7,5},{8,10},{9,11},{10,... | collective-permute-start | bytes 1572872 | tf_op jit(solution)/shard_map/ppermute | solution.py:406
  34.3 20.3 %collective-permute-start.21 = (bf16[256,1024]{1,0:T(8,128)(2,1)S(1)}, bf16[256,1024]{1,0:T(8,128)(2,1)S(1)}, u32[]{:S(2)}, u32[]{:S(2)}) collective-permute-start(bf16[256,1024]{1,0:T(8,128)(2,1)S(1)} %get-tuple-element.53.refs_4_), channel_id=1, source_target_pairs={{0,3},{1,0},{2,1},{3,2},{4,7},{5,4},{6,5},{7,6},{8,11},{9,8},{10,9... | collective-permute-start | bytes 1572872 | tf_op jit(solution)/shard_map/ppermute | solution.py:406
  41.1 15.4 %collective-permute-start.2 = (bf16[256,1024]{1,0:T(8,128)(2,1)S(1)}, bf16[256,1024]{1,0:T(8,128)(2,1)S(1)}, u32[]{:S(2)}, u32[]{:S(2)}) collective-permute-start(bf16[256,1024]{1,0:T(8,128)(2,1)S(1)} %get-tuple-element.46), channel_id=1, source_target_pairs={{0,4},{1,5},{2,6},{3,7},{4,8},{5,9},{6,10},{7,11},{8,12},{9,13},{1... | collective-permute-start | bytes 1572872 | tf_op jit(solution)/shard_map/ppermute | solution.py:406
  49.5 16.4 %collective-permute-start.3 = (bf16[256,1024]{1,0:T(8,128)(2,1)S(1)}, bf16[256,1024]{1,0:T(8,128)(2,1)S(1)}, u32[]{:S(2)}, u32[]{:S(2)}) collective-permute-start(bf16[256,1024]{1,0:T(8,128)(2,1)S(1)} %get-tuple-element.47), channel_id=1, source_target_pairs={{0,8},{1,9},{2,10},{3,11},{4,12},{5,13},{6,14},{7,15},{8,0},{9,1},... | collective-permute-start | bytes 1572872 | tf_op jit(solution)/shard_map/ppermute | solution.py:406
  51.6 23.8 %collective-permute-start.4 = (bf16[256,1024]{1,0:T(8,128)(2,1)S(1)}, bf16[256,1024]{1,0:T(8,128)(2,1)S(1)}, u32[]{:S(2)}, u32[]{:S(2)}) collective-permute-start(bf16[256,1024]{1,0:T(8,128)(2,1)S(1)} %get-tuple-element.48), channel_id=1, source_target_pairs={{0,12},{1,13},{2,14},{3,15},{4,0},{5,1},{6,2},{7,3},{8,4},{9,5},{1... | collective-permute-start | bytes 1572872 | tf_op jit(solution)/shard_map/ppermute | solution.py:406
  54.3 29.3 %collective-permute-start.12 = (bf16[4,2,32,1024]{3,2,1,0:T(8,128)(2,1)S(1)}, bf16[4,2,32,1024]{3,2,1,0:T(8,128)(2,1)S(1)}, u32[]{:S(2)}, u32[]{:S(2)}) collective-permute-start(bf16[4,2,32,1024]{3,2,1,0:T(8,128)(2,1)S(1)} %pad_maximum_fusion.n0), channel_id=1, source_target_pairs={{0,1},{1,2},{2,3},{3,0},{4,5},{5,6},{6,7},{7,4},{8,9},{9,10},{10,1... | collective-permute-start | bytes 1572872 | tf_op jit(solution)/shard_map/ppermute | solution.py:406
  54.6 29.9 %collective-permute-start.13 = (bf16[4,2,32,1024]{3,2,1,0:T(8,128)(2,1)S(1)}, bf16[4,2,32,1024]{3,2,1,0:T(8,128)(2,1)S(1)}, u32[]{:S(2)}, u32[]{:S(2)}) collective-permute-start(bf16[4,2,32,1024]{3,2,1,0:T(8,128)(2,1)S(1)} %pad_maximum_fusion.n0), channel_id=1, source_target_pairs={{0,2},{1,3},{2,0},{3,1},{4,6},{5,7},{6,4},{7,5},{8,10},{9,11},{10,... | collective-permute-start | bytes 1572872 | tf_op jit(solution)/shard_map/ppermute | solution.py:406
  56.4 30.5 %collective-permute-start.14 = (bf16[4,2,32,1024]{3,2,1,0:T(8,128)(2,1)S(1)}, bf16[4,2,32,1024]{3,2,1,0:T(8,128)(2,1)S(1)}, u32[]{:S(2)}, u32[]{:S(2)}) collective-permute-start(bf16[4,2,32,1024]{3,2,1,0:T(8,128)(2,1)S(1)} %pad_maximum_fusion.n0), channel_id=1, source_target_pairs={{0,3},{1,0},{2,1},{3,2},{4,7},{5,4},{6,5},{7,6},{8,11},{9,8},{10,9... | collective-permute-start | bytes 1572872 | tf_op jit(solution)/shard_map/ppermute | solution.py:406
  77.2 11.0 %collective-permute-start.26 = (bf16[128,1024]{1,0:T(8,128)(2,1)S(1)}, bf16[128,1024]{1,0:T(8,128)(2,1)S(1)}, u32[]{:S(2)}, u32[]{:S(2)}) collective-permute-start(bf16[128,1024]{1,0:T(8,128)(2,1)S(1)} %get-tuple-element.61), channel_id=1, source_target_pairs={{0,12},{1,13},{2,14},{3,15},{4,0},{5,1},{6,2},{7,3},{8,4},{9,5},{1... | collective-permute-start | bytes 786440 | tf_op jit(solution)/shard_map/ppermute | solution.py:406
  88.2 15.9 %collective-permute-start.15 = (bf16[4,2,32,1024]{3,2,1,0:T(8,128)(2,1)S(1)}, bf16[4,2,32,1024]{3,2,1,0:T(8,128)(2,1)S(1)}, u32[]{:S(2)}, u32[]{:S(2)}) collective-permute-start(bf16[4,2,32,1024]{3,2,1,0:T(8,128)(2,1)S(1)} %pad_maximum_fusion.n0), channel_id=1, source_target_pairs={{0,32},{1,33},{2,34},{3,35},{4,36},{5,37},{6,38},{7,39},{8,40},{9,... | collective-permute-start | bytes 1572872 | tf_op jit(solution)/shard_map/ppermute | solution.py:406
  88.6 15.6 %collective-permute-start.16 = (bf16[4,2,32,1024]{3,2,1,0:T(8,128)(2,1)S(1)}, bf16[4,2,32,1024]{3,2,1,0:T(8,128)(2,1)S(1)}, u32[]{:S(2)}, u32[]{:S(2)}) collective-permute-start(bf16[4,2,32,1024]{3,2,1,0:T(8,128)(2,1)S(1)} %collective-permute-done.12.n1), channel_id=1, source_target_pairs={{0,32},{1,33},{2,34},{3,35},{4,36},{5,37},{6,38},{7,39},{8,40},{9,... | collective-permute-start | bytes 1572872 | tf_op jit(solution)/shard_map/ppermute | solution.py:406
  91.4 15.1 %collective-permute-start.17 = (bf16[4,2,32,1024]{3,2,1,0:T(8,128)(2,1)S(1)}, bf16[4,2,32,1024]{3,2,1,0:T(8,128)(2,1)S(1)}, u32[]{:S(2)}, u32[]{:S(2)}) collective-permute-start(bf16[4,2,32,1024]{3,2,1,0:T(8,128)(2,1)S(1)} %collective-permute-done.13.n2), channel_id=1, source_target_pairs={{0,32},{1,33},{2,34},{3,35},{4,36},{5,37},{6,38},{7,39},{8,40},{9,... | collective-permute-start | bytes 1572872 | tf_op jit(solution)/shard_map/ppermute | solution.py:406
  93.7 12.9 %collective-permute-start.18 = (bf16[4,2,32,1024]{3,2,1,0:T(8,128)(2,1)S(1)}, bf16[4,2,32,1024]{3,2,1,0:T(8,128)(2,1)S(1)}, u32[]{:S(2)}, u32[]{:S(2)}) collective-permute-start(bf16[4,2,32,1024]{3,2,1,0:T(8,128)(2,1)S(1)} %collective-permute-done.14.n3), channel_id=1, source_target_pairs={{0,32},{1,33},{2,34},{3,35},{4,36},{5,37},{6,38},{7,39},{8,40},{9,... | collective-permute-start | bytes 1572872 | tf_op jit(solution)/shard_map/ppermute | solution.py:406
  125.1 11.1 %collective-permute-start.33 = (bf16[64,512]{1,0:T(8,128)(2,1)S(1)}, bf16[64,512]{1,0:T(8,128)(2,1)S(1)}, u32[]{:S(2)}, u32[]{:S(2)}) collective-permute-start(bf16[64,512]{1,0:T(8,128)(2,1)S(1)} %get-tuple-element.73), channel_id=1, source_target_pairs={{0,16},{1,17},{2,18},{3,19},{4,20},{5,21},{6,22},{7,23},{8,24},{9,... | collective-permute-start | bytes 196616 | tf_op jit(solution)/shard_map/ppermute | solution.py:406
  136.4 10.9 %collective-permute-start.35 = (bf16[2,128,512]{2,1,0:T(8,128)(2,1)S(1)}, bf16[2,128,512]{2,1,0:T(8,128)(2,1)S(1)}, u32[]{:S(2)}, u32[]{:S(2)}) collective-permute-start(bf16[2,128,512]{2,1,0:T(8,128)(2,1)S(1)} %pad_maximum_fusion.1.refs_4_), channel_id=1, source_target_pairs={{0,4},{1,5},{2,6},{3,7},{4,8},{5,9},{6,10},{7,11},{8,12},{9,13},{1... | collective-permute-start | bytes 786440 | tf_op jit(solution)/shard_map/ppermute | solution.py:406
  136.8 10.6 %collective-permute-start.36 = (bf16[2,128,512]{2,1,0:T(8,128)(2,1)S(1)}, bf16[2,128,512]{2,1,0:T(8,128)(2,1)S(1)}, u32[]{:S(2)}, u32[]{:S(2)}) collective-permute-start(bf16[2,128,512]{2,1,0:T(8,128)(2,1)S(1)} %pad_maximum_fusion.1.refs_4_), channel_id=1, source_target_pairs={{0,8},{1,9},{2,10},{3,11},{4,12},{5,13},{6,14},{7,15},{8,0},{9,1},... | collective-permute-start | bytes 786440 | tf_op jit(solution)/shard_map/ppermute | solution.py:406
  150.2 10.3 %collective-permute-start.42 = (bf16[128,1024]{1,0:T(8,128)(2,1)S(1)}, bf16[128,1024]{1,0:T(8,128)(2,1)S(1)}, u32[]{:S(2)}, u32[]{:S(2)}) collective-permute-start(bf16[128,1024]{1,0:T(8,128)(2,1)S(1)} %constant_dynamic-update-slice_fusion.refs_0_), channel_id=1, source_target_pairs={{0,12},{1,13},{2,14},{3,15},{4,0},{5,1},{6,2},{7,3},{8,4},{9,5},{1... | collective-permute-start | bytes 786440 | tf_op jit(solution)/shard_map/ppermute | solution.py:406
  163.6 10.5 %collective-permute-start.48 = (bf16[256,1024]{1,0:T(8,128)(2,1)S(1)}, bf16[256,1024]{1,0:T(8,128)(2,1)S(1)}, u32[]{:S(2)}, u32[]{:S(2)}) collective-permute-start(bf16[256,1024]{1,0:T(8,128)(2,1)S(1)} %get-tuple-element.82), channel_id=1, source_target_pairs={{0,1},{1,2},{2,3},{3,0},{4,5},{5,6},{6,7},{7,4},{8,9},{9,10},{10,1... | collective-permute-start | bytes 1572872 | tf_op jit(solution)/shard_map/ppermute | solution.py:406
  164.4 14.8 %collective-permute-start.50 = (bf16[256,1024]{1,0:T(8,128)(2,1)S(1)}, bf16[256,1024]{1,0:T(8,128)(2,1)S(1)}, u32[]{:S(2)}, u32[]{:S(2)}) collective-permute-start(bf16[256,1024]{1,0:T(8,128)(2,1)S(1)} %get-tuple-element.84), channel_id=1, source_target_pairs={{0,3},{1,0},{2,1},{3,2},{4,7},{5,4},{6,5},{7,6},{8,11},{9,8},{10,9... | collective-permute-start | bytes 1572872 | tf_op jit(solution)/shard_map/ppermute | solution.py:406
  166.9 13.7 %collective-permute-start.49 = (bf16[256,1024]{1,0:T(8,128)(2,1)S(1)}, bf16[256,1024]{1,0:T(8,128)(2,1)S(1)}, u32[]{:S(2)}, u32[]{:S(2)}) collective-permute-start(bf16[256,1024]{1,0:T(8,128)(2,1)S(1)} %get-tuple-element.83), channel_id=1, source_target_pairs={{0,2},{1,3},{2,0},{3,1},{4,6},{5,7},{6,4},{7,5},{8,10},{9,11},{10,... | collective-permute-start | bytes 1572872 | tf_op jit(solution)/shard_map/ppermute | solution.py:406
  (32 other events, 283.4 us)

commit v3 on v2

--- a/solution.py
+++ b/solution.py
@@ -48,13 +48,19 @@
     return [e * inverse for e in expo]
 
 
+def gain_column(index, gain, rows):
+    row = gain[:, pl.ds(pl.multiple_of(index * rows, rows), rows)].astype(F32)
+    return jnp.broadcast_to(row, (8, rows)).T[:, :1]
+
+
 def mask_kernel(at, logits, noise, weight, gain, scaled, q0, q1, q2, q3, rows):
+    column = gain_column(at[1], gain, weight.shape[0])
     for i, s in enumerate(tiles(weight.shape[1])):
         p = pattern_probs(logits, noise, s)
         for r in range(4):
             kept = [p[k] for k in range(6) if r in KEEPS[k]]
             rows.at[i][pl.ds(r, kept[0].shape[0], stride=4), :] = kept[0] + kept[1] + kept[2]
-        value = weight[:, s].astype(F32) * rows[i] * gain[...]
+        value = weight[:, s].astype(F32) * rows[i] * column
         scaled[:, s] = value.astype(BF)
         rows[i] = value
         quarter = q0.shape[0]
@@ -75,33 +81,49 @@
     )(at, logits, noise, weight, gain)
 
 
-def final_kernel(logits, noise, weight, gain, *refs):
-    parts, out, rows = refs[:-2], refs[-2], refs[-1]
-    tile = rows.shape[2]
-    where = [(j, at) for j in range(len(parts) // 4) for at in range(0, parts[j * 4].shape[1], tile)]
-    for i, (j, at) in enumerate(where):
-        s, inner = slice(i * tile, (i + 1) * tile), slice(at, at + tile)
-        mine = parts[j * 4 : j * 4 + 4]
-        total = (mine[0][:, inner].astype(F32) + mine[1][:, inner].astype(F32)) + (
-            mine[2][:, inner].astype(F32) + mine[3][:, inner].astype(F32)
+def ready_kernel(at, logits, noise, weight, gain, probs, ready):
+    column = gain_column(at[1], gain, weight.shape[0]) * (1.0 / sharpness_divisor)
+    for s in tiles(weight.shape[1]):
+        for k, p in enumerate(pattern_probs(logits, noise, s)):
+            probs[k, :, s] = p
+        ready[:, s] = weight[:, s].astype(F32) * column
+
+
+def final_kernel(probs, ready, *refs):
+    parts, out, rows, done, sems = refs[:-4], *refs[-4:]
+    copies = []
+    for i, s in enumerate(tiles(ready.shape[1])):
+        total = (parts[0][:, s].astype(F32) + parts[1][:, s].astype(F32)) + (
+            parts[2][:, s].astype(F32) + parts[3][:, s].astype(F32)
         )
-        rows[i] = total * gain[...] * weight[:, s].astype(F32) * (1.0 / sharpness_divisor)
-        d = [rows.at[i][pl.ds(r, logits.shape[1], stride=4), :] for r in range(4)]
-        p = pattern_probs(logits, noise, s)
+        rows[i] = total * ready[:, s]
+        d = [rows.at[i][pl.ds(r, probs.shape[1], stride=4), :] for r in range(4)]
+        p = [probs[k, :, s] for k in range(6)]
         dprob = [d[a] + d[b] for a, b in KEEPS]
         mean = p[0] * dprob[0]
         for k in range(1, 6):
             mean = mean + p[k] * dprob[k]
         for k in range(6):
-            out[k, :, s] = (p[k] * (dprob[k] - mean)).astype(BF)
-
-
-def logit_gradient(logits, noise, weight, gain, parts):
+            done[i, k] = (p[k] * (dprob[k] - mean)).astype(BF)
+        copies.append(pltpu.make_async_copy(done.at[i], out.at[:, :, s], sems.at[i]))
+        copies[-1].start()
+    for copy in copies:
+        copy.wait()
+
+
+def logit_gradient(probs, ready, parts):
+    count = len(tiles(ready.shape[1]))
+    tile = ready.shape[1] // count
     return call(
         final_kernel,
-        shape(logits.shape, BF),
-        scratch_shapes=[by_tile(*weight.shape, most=weight.shape[1] // 8)],
-    )(logits, noise, weight, gain, *parts)
+        shape(probs.shape, BF),
+        out_specs=pl.BlockSpec(memory_space=pl.ANY),
+        scratch_shapes=[
+            by_tile(*ready.shape),
+            pltpu.VMEM((count, *probs.shape[:2], tile), BF),
+            pltpu.SemaphoreType.DMA((count,)),
+        ],
+    )(probs, ready, *parts)
 
 
 def run_copies(copies, sems):
@@ -161,7 +183,7 @@
         blocks_kernel,
         (shape((4 * rows, width // 8), BF),) * 4,
         in_specs=[pl.BlockSpec(memory_space=pltpu.SMEM), pl.BlockSpec(memory_space=HBM), block, block],
-        out_specs=(block,) * 4,
+        out_specs=(pl.BlockSpec(memory_space=pltpu.VMEM),) * 4,
         scratch_shapes=[pltpu.SemaphoreType.DMA((64,))],
     )(at, tokens, mine, other)
 
@@ -459,19 +481,21 @@
     first = co == 0
     at = jnp.stack([zl, jnp.where(first, y, x), jnp.where(first, x, y), co, zh])
     weight = value_weight[0]
-    gain = lax.dynamic_slice_in_dim(norm_gain[0].astype(F32), own * part, part, 0)[:, None]
     wide32 = shape((rows, kv), F32)
     half = shape((rows, kv), BF)
 
     stream = stream_in if INTERPRET else pltpu.with_memory_space_constraint(stream_in, HBM)
     far = far_half(at, stream)
     far = to_z(far)
-    scaled, *quarters = masked_weights(x.reshape(1), mask_logits[0], gumbel_noise[0], weight, gain)
+    scaled, *quarters = masked_weights(jnp.stack([x, own]), mask_logits[0], gumbel_noise[0], weight, norm_gain)
     blocks = [to_h(scaled, k) for k in range(4)]
     quarters = [along_x(quarters[k], k) for k in range(4)]
     swapped = to_core(far)
     tokens = token_blocks(at, stream, far, swapped)
     tokens = [to_g(tokens[k], k) for k in range(4)]
+    probs, ready = call(
+        ready_kernel, (shape(mask_logits[0].shape, F32), shape(weight.shape, F32)), **small(4)
+    )(jnp.stack([x, own]), mask_logits[0], gumbel_noise[0], weight, norm_gain)
     short = call(short_kernel, shape(quarters[0].shape, BF))(*quarters)
     short = jnp.stack([short, to_z(short)])
     short = jnp.stack([to_g(short, k) for k in range(4)])
@@ -524,7 +548,7 @@
     t1, t3 = call(functools.partial(wgrad_kernel, (1, 3)), [block] * 2, **small(2))(at, turned, right)
     t1, t3 = to_h(t1, 1), to_h(t3, 3)
     (t0,) = call(functools.partial(wgrad_kernel, (0,)), [block], **small(2))(at, turned, right)
-    return logit_gradient(mask_logits[0], gumbel_noise[0], weight, gain, [t0, t1, t2, t3])[None]
+    return logit_gradient(probs, ready, [t0, t1, t2, t3])[None]
 
 
 def solution(mesh):

time: 183 us -> 183 us (level)
  transfers between devices with their start and end apart: 51 -> 51, of which waited for: 28 -> 28; matrix products, arithmetic and copies ran while one was open for 1% -> 0% of each run, Pallas kernels for 7% -> 9%
where the time goes in v3:
time: 183 us
  waiting for transfers between devices  85.1 us (47%)
  starting transfers between devices  69.2 us (38%)
  Pallas kernels  27.5 us (15%)
    ppermute x51, waiting for transfers between devices, move(): return lax.ppermute(v, AXES, pairs)  85.1 us
    ppermute x51, starting transfers between devices, move(): return lax.ppermute(v, AXES, pairs)  69.2 us
    pallas_call x3, Pallas kernels, chain_call(): call(kernel, out, in_specs=[pl.BlockSpec(memory_space=pltpu.SMEM)] + [pl....  6.79 us
  transfers between devices with their start and end apart: 51, of which 28 were waited for; matrix products, arithmetic and copies ran while one was open for 0% of the time, Pallas kernels for 9%

profile of v3, /device:TPU:0, one launch (start us, length us, event | category | flops | bytes accessed | tf_op | source)
XLA Modules:
  0.0 182.7 jit_solution(15450004911711132060)
XLA Ops:
  3.8 11.9 %collective-permute-done.mine = bf16[64,4096]{1,0:T(8,128)(2,1)S(1)} collective-permute-done((bf16[64,4096]{1,0:T(8,128)(2,1)S(1)}, bf16[64,4096]{1,0:T(8,128)(2,1)S(1)}, u32[]{:S(2)}, u32[]{:S(2)}) %collective-permute-start) | collective-permute-done | bytes 524320 | tf_op jit(solution)/shard_map/ppermute | solution.py:428
  19.0 2.7 %collective-permute-start.6 = (bf16[32,1024]{1,0:T(8,128)(2,1)S(1)}, bf16[32,1024]{1,0:T(8,128)(2,1)S(1)}, u32[]{:S(2)}, u32[]{:S(2)}) collective-permute-start(bf16[32,1024]{1,0:T(8,128)(2,1)S(1)} %get-tuple-element.55), channel_id=1, source_target_pairs={{0,2},{1,3},{2,0},{3,1},{4,6},{5,7},{6,4},{7,5},{8,10},{9,11},{10,... | collective-permute-start | bytes 196616 | tf_op jit(solution)/shard_map/ppermute | solution.py:428
  35.7 2.9 %collective-permute-start.10 = (bf16[2,32,1024]{2,1,0:T(8,128)(2,1)S(1)}, bf16[2,32,1024]{2,1,0:T(8,128)(2,1)S(1)}, u32[]{:S(2)}, u32[]{:S(2)}) collective-permute-start(bf16[2,32,1024]{2,1,0:T(8,128)(2,1)S(1)} %get-tuple-element.90), channel_id=1, source_target_pairs={{0,8},{1,9},{2,10},{3,11},{4,12},{5,13},{6,14},{7,15},{8,0},{9,1},... | collective-permute-start | bytes 393224 | tf_op jit(solution)/shard_map/ppermute | solution.py:428
  38.6 2.4 %shard_map.66 = (bf16[256,1024]{1,0:T(8,128)(2,1)S(1)}, bf16[256,1024]{1,0:T(8,128)(2,1)S(1)}, bf16[256,1024]{1,0:T(8,128)(2,1)S(1)}, bf16[256,1024]{1,0:T(8,128)(2,1)S(1)}) custom-call(s32[5]{0:T(128)S(1)} %stack.71.at, bf16[2,64,8192]{2,1,0:T(8,128)(2,1)} %tokens.5, bf16[64,4096]{1,0:T(8,128)(2,1)S(1)} %collective-permute-done.mine, ...), custom_call_target="tpu_custom_call" | custom-call | tf_op jit(solution)/shard_map/pallas_call | solution.py:182
  41.1 2.4 %collective-permute-done.10 = bf16[2,32,1024]{2,1,0:T(8,128)(2,1)S(1)} collective-permute-done((bf16[2,32,1024]{2,1,0:T(8,128)(2,1)S(1)}, bf16[2,32,1024]{2,1,0:T(8,128)(2,1)S(1)}, u32[]{:S(2)}, u32[]{:S(2)}) %collective-permute-start.10) | collective-permute-done | bytes 131104 | tf_op jit(solution)/shard_map/ppermute | solution.py:428
  45.2 4.3 %collective-permute-done.11 = bf16[2,32,1024]{2,1,0:T(8,128)(2,1)S(1)} collective-permute-done((bf16[2,32,1024]{2,1,0:T(8,128)(2,1)S(1)}, bf16[2,32,1024]{2,1,0:T(8,128)(2,1)S(1)}, u32[]{:S(2)}, u32[]{:S(2)}) %collective-permute-start.11) | collective-permute-done | bytes 131104 | tf_op jit(solution)/shard_map/ppermute | solution.py:428
  51.6 2.6 %collective-permute-start.4 = (bf16[256,1024]{1,0:T(8,128)(2,1)S(1)}, bf16[256,1024]{1,0:T(8,128)(2,1)S(1)}, u32[]{:S(2)}, u32[]{:S(2)}) collective-permute-start(bf16[256,1024]{1,0:T(8,128)(2,1)S(1)} %get-tuple-element.52), channel_id=1, source_target_pairs={{0,12},{1,13},{2,14},{3,15},{4,0},{5,1},{6,2},{7,3},{8,4},{9,5},{1... | collective-permute-start | bytes 1572872 | tf_op jit(solution)/shard_map/ppermute | solution.py:428
  56.4 2.5 %collective-permute-start.14 = (bf16[4,2,32,1024]{3,2,1,0:T(8,128)(2,1)S(1)}, bf16[4,2,32,1024]{3,2,1,0:T(8,128)(2,1)S(1)}, u32[]{:S(2)}, u32[]{:S(2)}) collective-permute-start(bf16[4,2,32,1024]{3,2,1,0:T(8,128)(2,1)S(1)} %pad_maximum_fusion.n0), channel_id=1, source_target_pairs={{0,3},{1,0},{2,1},{3,2},{4,7},{5,4},{6,5},{7,6},{8,11},{9,8},{10,9... | collective-permute-start | bytes 1572872 | tf_op jit(solution)/shard_map/ppermute | solution.py:428
  58.9 7.0 %collective-permute-done.3.refs_2_ = bf16[256,1024]{1,0:T(8,128)(2,1)S(1)} collective-permute-done((bf16[256,1024]{1,0:T(8,128)(2,1)S(1)}, bf16[256,1024]{1,0:T(8,128)(2,1)S(1)}, u32[]{:S(2)}, u32[]{:S(2)}) %collective-permute-start.3) | collective-permute-done | bytes 524320 | tf_op jit(solution)/shard_map/ppermute | solution.py:428
  65.9 9.4 %collective-permute-done.4.refs_3_ = bf16[256,1024]{1,0:T(8,128)(2,1)S(1)} collective-permute-done((bf16[256,1024]{1,0:T(8,128)(2,1)S(1)}, bf16[256,1024]{1,0:T(8,128)(2,1)S(1)}, u32[]{:S(2)}, u32[]{:S(2)}) %collective-permute-start.4) | collective-permute-done | bytes 524320 | tf_op jit(solution)/shard_map/ppermute | solution.py:428
  77.1 3.6 %collective-permute-start.26 = (bf16[128,1024]{1,0:T(8,128)(2,1)S(1)}, bf16[128,1024]{1,0:T(8,128)(2,1)S(1)}, u32[]{:S(2)}, u32[]{:S(2)}) collective-permute-start(bf16[128,1024]{1,0:T(8,128)(2,1)S(1)} %get-tuple-element.65), channel_id=1, source_target_pairs={{0,12},{1,13},{2,14},{3,15},{4,0},{5,1},{6,2},{7,3},{8,4},{9,5},{1... | collective-permute-start | bytes 786440 | tf_op jit(solution)/shard_map/ppermute | solution.py:428
  84.5 2.4 %collective-permute-start.22 = (bf16[128,1024]{1,0:T(8,128)(2,1)S(1)}, bf16[128,1024]{1,0:T(8,128)(2,1)S(1)}, u32[]{:S(2)}, u32[]{:S(2)}) collective-permute-start(bf16[128,1024]{1,0:T(8,128)(2,1)S(1)} %get-tuple-element.59), channel_id=1, source_target_pairs={{0,12},{1,13},{2,14},{3,15},{4,0},{5,1},{6,2},{7,3},{8,4},{9,5},{1... | collective-permute-start | bytes 786440 | tf_op jit(solution)/shard_map/ppermute | solution.py:428
  88.7 2.7 %collective-permute-done.28.m3 = bf16[128,1024]{1,0:T(8,128)(2,1)S(1)} collective-permute-done((bf16[128,1024]{1,0:T(8,128)(2,1)S(1)}, bf16[128,1024]{1,0:T(8,128)(2,1)S(1)}, u32[]{:S(2)}, u32[]{:S(2)}) %collective-permute-start.28) | collective-permute-done | bytes 262176 | tf_op jit(solution)/shard_map/ppermute | solution.py:428
  95.5 6.9 %collective-permute-done.24.m3 = bf16[128,1024]{1,0:T(8,128)(2,1)S(1)} collective-permute-done((bf16[128,1024]{1,0:T(8,128)(2,1)S(1)}, bf16[128,1024]{1,0:T(8,128)(2,1)S(1)}, u32[]{:S(2)}, u32[]{:S(2)}) %collective-permute-start.24) | collective-permute-done | bytes 262176 | tf_op jit(solution)/shard_map/ppermute | solution.py:428
  111.3 5.5 %collective-permute-start.31 = (bf16[64,1024]{1,0:T(8,128)(2,1)S(1)}, bf16[64,1024]{1,0:T(8,128)(2,1)S(1)}, u32[]{:S(2)}, u32[]{:S(2)}) collective-permute-start(bf16[64,1024]{1,0:T(8,128)(2,1)S(1)} %get-tuple-element.73), channel_id=1, source_target_pairs={{0,64},{1,65},{2,66},{3,67},{4,68},{5,69},{6,70},{7,71},{8,72},{9,... | collective-permute-start | bytes 393224 | tf_op jit(solution)/shard_map/ppermute | solution.py:428
  116.8 3.0 %collective-permute-done.31.c_in = bf16[64,1024]{1,0:T(8,128)(2,1)S(1)} collective-permute-done((bf16[64,1024]{1,0:T(8,128)(2,1)S(1)}, bf16[64,1024]{1,0:T(8,128)(2,1)S(1)}, u32[]{:S(2)}, u32[]{:S(2)}) %collective-permute-start.31) | collective-permute-done | bytes 131104 | tf_op jit(solution)/shard_map/ppermute | solution.py:428
  119.8 3.9 %shard_map.77 = (f32[2,64,1024]{2,1,0:T(8,128)S(1)}, f32[2,64,1024]{2,1,0:T(8,128)S(1)}, f32[2,64,128]{2,1,0:T(8,128)S(1)}, bf16[64,512]{1,0:T(8,128)(2,1)S(1)},...) custom-call(s32[5]{0:T(128)S(1)} %stack.71.at, ...), custom_call_target="tpu_custom_call" | custom-call | tf_op jit(solution)/shard_map/pallas_call | solution.py:397
  127.0 6.5 %collective-permute-done.38.g_in = bf16[64,1024]{1,0:T(8,128)(2,1)S(1)} collective-permute-done((bf16[64,1024]{1,0:T(8,128)(2,1)S(1)}, bf16[64,1024]{1,0:T(8,128)(2,1)S(1)}, u32[]{:S(2)}, u32[]{:S(2)}) %collective-permute-start.38) | collective-permute-done | bytes 131104 | tf_op jit(solution)/shard_map/ppermute | solution.py:428
  136.8 3.3 %collective-permute-start.36 = (bf16[2,128,512]{2,1,0:T(8,128)(2,1)S(1)}, bf16[2,128,512]{2,1,0:T(8,128)(2,1)S(1)}, u32[]{:S(2)}, u32[]{:S(2)}) collective-permute-start(bf16[2,128,512]{2,1,0:T(8,128)(2,1)S(1)} %pad_maximum_fusion.1.refs_4_), channel_id=1, source_target_pairs={{0,8},{1,9},{2,10},{3,11},{4,12},{5,13},{6,14},{7,15},{8,0},{9,1},... | collective-permute-start | bytes 786440 | tf_op jit(solution)/shard_map/ppermute | solution.py:428
  144.5 2.7 %collective-permute-start.46 = (bf16[128,1024]{1,0:T(8,128)(2,1)S(1)}, bf16[128,1024]{1,0:T(8,128)(2,1)S(1)}, u32[]{:S(2)}, u32[]{:S(2)}) collective-permute-start(bf16[128,1024]{1,0:T(8,128)(2,1)S(1)} %constant_dynamic-update-slice_fusion.2.refs_4_), channel_id=1, source_target_pairs={{0,8},{1,9},{2,10},{3,11},{4,12},{5,13},{6,14},{7,15},{8,0},{9,1},... | collective-permute-start | bytes 786440 | tf_op jit(solution)/shard_map/ppermute | solution.py:428
  155.9 2.8 %collective-permute-done.41.refs_2_ = bf16[128,1024]{1,0:T(8,128)(2,1)S(1)} collective-permute-done((bf16[128,1024]{1,0:T(8,128)(2,1)S(1)}, bf16[128,1024]{1,0:T(8,128)(2,1)S(1)}, u32[]{:S(2)}, u32[]{:S(2)}) %collective-permute-start.41) | collective-permute-done | bytes 262176 | tf_op jit(solution)/shard_map/ppermute | solution.py:428
  164.4 2.5 %collective-permute-start.50 = (bf16[256,1024]{1,0:T(8,128)(2,1)S(1)}, bf16[256,1024]{1,0:T(8,128)(2,1)S(1)}, u32[]{:S(2)}, u32[]{:S(2)}) collective-permute-start(bf16[256,1024]{1,0:T(8,128)(2,1)S(1)} %get-tuple-element.88), channel_id=1, source_target_pairs={{0,3},{1,0},{2,1},{3,2},{4,7},{5,4},{6,5},{7,6},{8,11},{9,8},{10,9... | collective-permute-start | bytes 1572872 | tf_op jit(solution)/shard_map/ppermute | solution.py:428
  170.4 3.6 %collective-permute-done.48.refs_1_ = bf16[256,1024]{1,0:T(8,128)(2,1)S(1)} collective-permute-done((bf16[256,1024]{1,0:T(8,128)(2,1)S(1)}, bf16[256,1024]{1,0:T(8,128)(2,1)S(1)}, u32[]{:S(2)}, u32[]{:S(2)}) %collective-permute-start.48) | collective-permute-done | bytes 524320 | tf_op jit(solution)/shard_map/ppermute | solution.py:428
  174.1 5.2 %collective-permute-done.50.refs_3_ = bf16[256,1024]{1,0:T(8,128)(2,1)S(1)} collective-permute-done((bf16[256,1024]{1,0:T(8,128)(2,1)S(1)}, bf16[256,1024]{1,0:T(8,128)(2,1)S(1)}, u32[]{:S(2)}, u32[]{:S(2)}) %collective-permute-start.50) | collective-permute-done | bytes 524320 | tf_op jit(solution)/shard_map/ppermute | solution.py:428
  (121 shorter events, 79.2 us)
Async XLA Ops:
  1.7 14.1 %collective-permute-start = (bf16[64,4096]{1,0:T(8,128)(2,1)S(1)}, bf16[64,4096]{1,0:T(8,128)(2,1)S(1)}, u32[]{:S(2)}, u32[]{:S(2)}) collective-permute-start(bf16[64,4096]{1,0:T(8,128)(2,1)S(1)} %shard_map.65), channel_id=1, source_target_pairs={{0,16},{1,17},{2,18},{3,19},{4,20},{5,21},{6,22},{7,23},{8,24},{9,... | collective-permute-start | bytes 1572872 | tf_op jit(solution)/shard_map/ppermute | solution.py:428
  15.8 19.9 %collective-permute-start.1 = (bf16[64,4096]{1,0:T(8,128)(2,1)S(1)}, bf16[64,4096]{1,0:T(8,128)(2,1)S(1)}, u32[]{:S(2)}, u32[]{:S(2)}) collective-permute-start(bf16[64,4096]{1,0:T(8,128)(2,1)S(1)} %collective-permute-done.mine), channel_id=1, source_target_pairs={{0,32},{1,33},{2,34},{3,35},{4,36},{5,37},{6,38},{7,39},{8,40},{9,... | collective-permute-start | bytes 1572872 | tf_op jit(solution)/shard_map/ppermute | solution.py:428
  27.9 23.7 %collective-permute-start.19 = (bf16[256,1024]{1,0:T(8,128)(2,1)S(1)}, bf16[256,1024]{1,0:T(8,128)(2,1)S(1)}, u32[]{:S(2)}, u32[]{:S(2)}) collective-permute-start(bf16[256,1024]{1,0:T(8,128)(2,1)S(1)} %get-tuple-element.57.refs_4_), channel_id=1, source_target_pairs={{0,1},{1,2},{2,3},{3,0},{4,5},{5,6},{6,7},{7,4},{8,9},{9,10},{10,1... | collective-permute-start | bytes 1572872 | tf_op jit(solution)/shard_map/ppermute | solution.py:428
  30.4 10.6 %collective-permute-start.9 = (bf16[2,32,1024]{2,1,0:T(8,128)(2,1)S(1)}, bf16[2,32,1024]{2,1,0:T(8,128)(2,1)S(1)}, u32[]{:S(2)}, u32[]{:S(2)}) collective-permute-start(bf16[2,32,1024]{2,1,0:T(8,128)(2,1)S(1)} %get-tuple-element.90), channel_id=1, source_target_pairs={{0,4},{1,5},{2,6},{3,7},{4,8},{5,9},{6,10},{7,11},{8,12},{9,13},{1... | collective-permute-start | bytes 393224 | tf_op jit(solution)/shard_map/ppermute | solution.py:428
  32.1 22.2 %collective-permute-start.20 = (bf16[256,1024]{1,0:T(8,128)(2,1)S(1)}, bf16[256,1024]{1,0:T(8,128)(2,1)S(1)}, u32[]{:S(2)}, u32[]{:S(2)}) collective-permute-start(bf16[256,1024]{1,0:T(8,128)(2,1)S(1)} %get-tuple-element.57.refs_4_), channel_id=1, source_target_pairs={{0,2},{1,3},{2,0},{3,1},{4,6},{5,7},{6,4},{7,5},{8,10},{9,11},{10,... | collective-permute-start | bytes 1572872 | tf_op jit(solution)/shard_map/ppermute | solution.py:428
  34.3 20.3 %collective-permute-start.21 = (bf16[256,1024]{1,0:T(8,128)(2,1)S(1)}, bf16[256,1024]{1,0:T(8,128)(2,1)S(1)}, u32[]{:S(2)}, u32[]{:S(2)}) collective-permute-start(bf16[256,1024]{1,0:T(8,128)(2,1)S(1)} %get-tuple-element.57.refs_4_), channel_id=1, source_target_pairs={{0,3},{1,0},{2,1},{3,2},{4,7},{5,4},{6,5},{7,6},{8,11},{9,8},{10,9... | collective-permute-start | bytes 1572872 | tf_op jit(solution)/shard_map/ppermute | solution.py:428
  41.0 15.4 %collective-permute-start.2 = (bf16[256,1024]{1,0:T(8,128)(2,1)S(1)}, bf16[256,1024]{1,0:T(8,128)(2,1)S(1)}, u32[]{:S(2)}, u32[]{:S(2)}) collective-permute-start(bf16[256,1024]{1,0:T(8,128)(2,1)S(1)} %get-tuple-element.50), channel_id=1, source_target_pairs={{0,4},{1,5},{2,6},{3,7},{4,8},{5,9},{6,10},{7,11},{8,12},{9,13},{1... | collective-permute-start | bytes 1572872 | tf_op jit(solution)/shard_map/ppermute | solution.py:428
  49.5 16.4 %collective-permute-start.3 = (bf16[256,1024]{1,0:T(8,128)(2,1)S(1)}, bf16[256,1024]{1,0:T(8,128)(2,1)S(1)}, u32[]{:S(2)}, u32[]{:S(2)}) collective-permute-start(bf16[256,1024]{1,0:T(8,128)(2,1)S(1)} %get-tuple-element.51), channel_id=1, source_target_pairs={{0,8},{1,9},{2,10},{3,11},{4,12},{5,13},{6,14},{7,15},{8,0},{9,1},... | collective-permute-start | bytes 1572872 | tf_op jit(solution)/shard_map/ppermute | solution.py:428
  51.6 23.8 %collective-permute-start.4 = (bf16[256,1024]{1,0:T(8,128)(2,1)S(1)}, bf16[256,1024]{1,0:T(8,128)(2,1)S(1)}, u32[]{:S(2)}, u32[]{:S(2)}) collective-permute-start(bf16[256,1024]{1,0:T(8,128)(2,1)S(1)} %get-tuple-element.52), channel_id=1, source_target_pairs={{0,12},{1,13},{2,14},{3,15},{4,0},{5,1},{6,2},{7,3},{8,4},{9,5},{1... | collective-permute-start | bytes 1572872 | tf_op jit(solution)/shard_map/ppermute | solution.py:428
  54.3 29.3 %collective-permute-start.12 = (bf16[4,2,32,1024]{3,2,1,0:T(8,128)(2,1)S(1)}, bf16[4,2,32,1024]{3,2,1,0:T(8,128)(2,1)S(1)}, u32[]{:S(2)}, u32[]{:S(2)}) collective-permute-start(bf16[4,2,32,1024]{3,2,1,0:T(8,128)(2,1)S(1)} %pad_maximum_fusion.n0), channel_id=1, source_target_pairs={{0,1},{1,2},{2,3},{3,0},{4,5},{5,6},{6,7},{7,4},{8,9},{9,10},{10,1... | collective-permute-start | bytes 1572872 | tf_op jit(solution)/shard_map/ppermute | solution.py:428
  54.6 29.9 %collective-permute-start.13 = (bf16[4,2,32,1024]{3,2,1,0:T(8,128)(2,1)S(1)}, bf16[4,2,32,1024]{3,2,1,0:T(8,128)(2,1)S(1)}, u32[]{:S(2)}, u32[]{:S(2)}) collective-permute-start(bf16[4,2,32,1024]{3,2,1,0:T(8,128)(2,1)S(1)} %pad_maximum_fusion.n0), channel_id=1, source_target_pairs={{0,2},{1,3},{2,0},{3,1},{4,6},{5,7},{6,4},{7,5},{8,10},{9,11},{10,... | collective-permute-start | bytes 1572872 | tf_op jit(solution)/shard_map/ppermute | solution.py:428
  56.4 30.5 %collective-permute-start.14 = (bf16[4,2,32,1024]{3,2,1,0:T(8,128)(2,1)S(1)}, bf16[4,2,32,1024]{3,2,1,0:T(8,128)(2,1)S(1)}, u32[]{:S(2)}, u32[]{:S(2)}) collective-permute-start(bf16[4,2,32,1024]{3,2,1,0:T(8,128)(2,1)S(1)} %pad_maximum_fusion.n0), channel_id=1, source_target_pairs={{0,3},{1,0},{2,1},{3,2},{4,7},{5,4},{6,5},{7,6},{8,11},{9,8},{10,9... | collective-permute-start | bytes 1572872 | tf_op jit(solution)/shard_map/ppermute | solution.py:428
  77.1 11.0 %collective-permute-start.26 = (bf16[128,1024]{1,0:T(8,128)(2,1)S(1)}, bf16[128,1024]{1,0:T(8,128)(2,1)S(1)}, u32[]{:S(2)}, u32[]{:S(2)}) collective-permute-start(bf16[128,1024]{1,0:T(8,128)(2,1)S(1)} %get-tuple-element.65), channel_id=1, source_target_pairs={{0,12},{1,13},{2,14},{3,15},{4,0},{5,1},{6,2},{7,3},{8,4},{9,5},{1... | collective-permute-start | bytes 786440 | tf_op jit(solution)/shard_map/ppermute | solution.py:428
  88.2 15.9 %collective-permute-start.15 = (bf16[4,2,32,1024]{3,2,1,0:T(8,128)(2,1)S(1)}, bf16[4,2,32,1024]{3,2,1,0:T(8,128)(2,1)S(1)}, u32[]{:S(2)}, u32[]{:S(2)}) collective-permute-start(bf16[4,2,32,1024]{3,2,1,0:T(8,128)(2,1)S(1)} %pad_maximum_fusion.n0), channel_id=1, source_target_pairs={{0,32},{1,33},{2,34},{3,35},{4,36},{5,37},{6,38},{7,39},{8,40},{9,... | collective-permute-start | bytes 1572872 | tf_op jit(solution)/shard_map/ppermute | solution.py:428
  88.6 15.6 %collective-permute-start.16 = (bf16[4,2,32,1024]{3,2,1,0:T(8,128)(2,1)S(1)}, bf16[4,2,32,1024]{3,2,1,0:T(8,128)(2,1)S(1)}, u32[]{:S(2)}, u32[]{:S(2)}) collective-permute-start(bf16[4,2,32,1024]{3,2,1,0:T(8,128)(2,1)S(1)} %collective-permute-done.12.n1), channel_id=1, source_target_pairs={{0,32},{1,33},{2,34},{3,35},{4,36},{5,37},{6,38},{7,39},{8,40},{9,... | collective-permute-start | bytes 1572872 | tf_op jit(solution)/shard_map/ppermute | solution.py:428
  91.4 15.1 %collective-permute-start.17 = (bf16[4,2,32,1024]{3,2,1,0:T(8,128)(2,1)S(1)}, bf16[4,2,32,1024]{3,2,1,0:T(8,128)(2,1)S(1)}, u32[]{:S(2)}, u32[]{:S(2)}) collective-permute-start(bf16[4,2,32,1024]{3,2,1,0:T(8,128)(2,1)S(1)} %collective-permute-done.13.n2), channel_id=1, source_target_pairs={{0,32},{1,33},{2,34},{3,35},{4,36},{5,37},{6,38},{7,39},{8,40},{9,... | collective-permute-start | bytes 1572872 | tf_op jit(solution)/shard_map/ppermute | solution.py:428
  93.6 12.9 %collective-permute-start.18 = (bf16[4,2,32,1024]{3,2,1,0:T(8,128)(2,1)S(1)}, bf16[4,2,32,1024]{3,2,1,0:T(8,128)(2,1)S(1)}, u32[]{:S(2)}, u32[]{:S(2)}) collective-permute-start(bf16[4,2,32,1024]{3,2,1,0:T(8,128)(2,1)S(1)} %collective-permute-done.14.n3), channel_id=1, source_target_pairs={{0,32},{1,33},{2,34},{3,35},{4,36},{5,37},{6,38},{7,39},{8,40},{9,... | collective-permute-start | bytes 1572872 | tf_op jit(solution)/shard_map/ppermute | solution.py:428
  125.1 11.1 %collective-permute-start.33 = (bf16[64,512]{1,0:T(8,128)(2,1)S(1)}, bf16[64,512]{1,0:T(8,128)(2,1)S(1)}, u32[]{:S(2)}, u32[]{:S(2)}) collective-permute-start(bf16[64,512]{1,0:T(8,128)(2,1)S(1)} %get-tuple-element.77), channel_id=1, source_target_pairs={{0,16},{1,17},{2,18},{3,19},{4,20},{5,21},{6,22},{7,23},{8,24},{9,... | collective-permute-start | bytes 196616 | tf_op jit(solution)/shard_map/ppermute | solution.py:428
  136.4 10.9 %collective-permute-start.35 = (bf16[2,128,512]{2,1,0:T(8,128)(2,1)S(1)}, bf16[2,128,512]{2,1,0:T(8,128)(2,1)S(1)}, u32[]{:S(2)}, u32[]{:S(2)}) collective-permute-start(bf16[2,128,512]{2,1,0:T(8,128)(2,1)S(1)} %pad_maximum_fusion.1.refs_4_), channel_id=1, source_target_pairs={{0,4},{1,5},{2,6},{3,7},{4,8},{5,9},{6,10},{7,11},{8,12},{9,13},{1... | collective-permute-start | bytes 786440 | tf_op jit(solution)/shard_map/ppermute | solution.py:428
  136.8 10.6 %collective-permute-start.36 = (bf16[2,128,512]{2,1,0:T(8,128)(2,1)S(1)}, bf16[2,128,512]{2,1,0:T(8,128)(2,1)S(1)}, u32[]{:S(2)}, u32[]{:S(2)}) collective-permute-start(bf16[2,128,512]{2,1,0:T(8,128)(2,1)S(1)} %pad_maximum_fusion.1.refs_4_), channel_id=1, source_target_pairs={{0,8},{1,9},{2,10},{3,11},{4,12},{5,13},{6,14},{7,15},{8,0},{9,1},... | collective-permute-start | bytes 786440 | tf_op jit(solution)/shard_map/ppermute | solution.py:428
  150.2 10.3 %collective-permute-start.42 = (bf16[128,1024]{1,0:T(8,128)(2,1)S(1)}, bf16[128,1024]{1,0:T(8,128)(2,1)S(1)}, u32[]{:S(2)}, u32[]{:S(2)}) collective-permute-start(bf16[128,1024]{1,0:T(8,128)(2,1)S(1)} %constant_dynamic-update-slice_fusion.refs_0_), channel_id=1, source_target_pairs={{0,12},{1,13},{2,14},{3,15},{4,0},{5,1},{6,2},{7,3},{8,4},{9,5},{1... | collective-permute-start | bytes 786440 | tf_op jit(solution)/shard_map/ppermute | solution.py:428
  163.6 10.5 %collective-permute-start.48 = (bf16[256,1024]{1,0:T(8,128)(2,1)S(1)}, bf16[256,1024]{1,0:T(8,128)(2,1)S(1)}, u32[]{:S(2)}, u32[]{:S(2)}) collective-permute-start(bf16[256,1024]{1,0:T(8,128)(2,1)S(1)} %get-tuple-element.86), channel_id=1, source_target_pairs={{0,1},{1,2},{2,3},{3,0},{4,5},{5,6},{6,7},{7,4},{8,9},{9,10},{10,1... | collective-permute-start | bytes 1572872 | tf_op jit(solution)/shard_map/ppermute | solution.py:428
  164.4 14.8 %collective-permute-start.50 = (bf16[256,1024]{1,0:T(8,128)(2,1)S(1)}, bf16[256,1024]{1,0:T(8,128)(2,1)S(1)}, u32[]{:S(2)}, u32[]{:S(2)}) collective-permute-start(bf16[256,1024]{1,0:T(8,128)(2,1)S(1)} %get-tuple-element.88), channel_id=1, source_target_pairs={{0,3},{1,0},{2,1},{3,2},{4,7},{5,4},{6,5},{7,6},{8,11},{9,8},{10,9... | collective-permute-start | bytes 1572872 | tf_op jit(solution)/shard_map/ppermute | solution.py:428
  166.9 13.7 %collective-permute-start.49 = (bf16[256,1024]{1,0:T(8,128)(2,1)S(1)}, bf16[256,1024]{1,0:T(8,128)(2,1)S(1)}, u32[]{:S(2)}, u32[]{:S(2)}) collective-permute-start(bf16[256,1024]{1,0:T(8,128)(2,1)S(1)} %get-tuple-element.87), channel_id=1, source_target_pairs={{0,2},{1,3},{2,0},{3,1},{4,6},{5,7},{6,4},{7,5},{8,10},{9,11},{10,... | collective-permute-start | bytes 1572872 | tf_op jit(solution)/shard_map/ppermute | solution.py:428
  (33 other events, 297.0 us)

commit v4 on v3

--- a/solution.py
+++ b/solution.py
@@ -339,9 +339,14 @@
     c_out[...] = (c + scale_of(sums, spread[...], repeat, width) * value).astype(BF)
 
 
-def lower_of(width, at, layer, own, other, acc, g, sums, sigma, value):
+def pre_kernel(at, own, other, g4, du, acc):
+    du[...] = by_layer(at[3], 1, own, other, acc, g4[...].astype(BF), BEHIND)
+
+
+def lower_of(width, at, layer, own, other, acc, g, sums, sigma, value, du=None):
     vg = g.astype(BF)
-    du = by_layer(at[3], layer, own, other, acc, vg, BEHIND)
+    if du is None:
+        du = by_layer(at[3], layer, own, other, acc, vg, BEHIND)
     dot = jnp.sum(vg.astype(F32) * value, -1, keepdims=True) * (1.0 / width)
     return g + sigma * du - sigma * sigma * dot * sums
 
@@ -352,7 +357,7 @@
 
 
 def turn_kernel(
-    repeat, width, at, own, other, u, y0, spread, c_in, g4,
+    repeat, width, at, own, other, u, y0, spread, c_in, g4, du,
     value, sums, sigma, keep, give, far_keep, far_give, g_out, acc,
 ):
     c = c_in[...]
@@ -375,7 +380,7 @@
         there[...] = jnp.where(low, c[:, half:], c[:, :half]).astype(BF)
     g = g4[...]
     for layer in (1, 0):
-        g = lower_of(width, at, layer, own, other, acc, g, sums[layer], sigma[layer][:, :1], value[layer])
+        g = lower_of(width, at, layer, own, other, acc, g, sums[layer], sigma[layer][:, :1], value[layer], du[...] if layer else None)
     g_out[...] = g.astype(BF)
 
 
@@ -522,11 +527,12 @@
         at, n, n_other, mine, theirs, far_mine, far_theirs, y0, spread,
     )
     c_in = up(c)
+    du = chain_call(pre_kernel, wide32, at, n, n_other, g4)
     quarter = shape((rows, kv // 2), BF)
     value, sums, sigma, keep, give, far_keep, far_give, g = chain_call(
         functools.partial(turn_kernel, repeat, width),
         (two, two, shape((2, rows, head), F32)) + (quarter,) * 4 + (half,),
-        at, n, n_other, u, y0, spread, c_in, g4,
+        at, n, n_other, u, y0, spread, c_in, g4, du,
     )
     g_in = down(g)
     cs = jnp.stack([

time: 183 us -> 182 us (level)
    pallas_call x3 -> x4, Pallas kernels: 6.79 us -> 7.31 us  [chain_call(): call(kernel, out, in_specs=[pl.BlockSpec(memory_space=pltpu.SMEM)] + [pl....]
where the time goes in v4:
time: 182 us
  waiting for transfers between devices  83.7 us (46%)
  starting transfers between devices  69.2 us (38%)
  Pallas kernels  28.1 us (15%)
    ppermute x51, waiting for transfers between devices, move(): return lax.ppermute(v, AXES, pairs)  83.7 us
    ppermute x51, starting transfers between devices, move(): return lax.ppermute(v, AXES, pairs)  69.2 us
    pallas_call x4, Pallas kernels, chain_call(): call(kernel, out, in_specs=[pl.BlockSpec(memory_space=pltpu.SMEM)] + [pl....  7.31 us
  transfers between devices with their start and end apart: 51, of which 28 were waited for; matrix products, arithmetic and copies ran while one was open for 0% of the time, Pallas kernels for 9%

profile of v4, /device:TPU:0, one launch (start us, length us, event | category | flops | bytes accessed | tf_op | source)
XLA Modules:
  0.0 181.9 jit_solution(7146220929303265872)
XLA Ops:
  3.8 11.9 %collective-permute-done.mine = bf16[64,4096]{1,0:T(8,128)(2,1)S(1)} collective-permute-done((bf16[64,4096]{1,0:T(8,128)(2,1)S(1)}, bf16[64,4096]{1,0:T(8,128)(2,1)S(1)}, u32[]{:S(2)}, u32[]{:S(2)}) %collective-permute-start) | collective-permute-done | bytes 524320 | tf_op jit(solution)/shard_map/ppermute | solution.py:433
  19.0 2.7 %collective-permute-start.6 = (bf16[32,1024]{1,0:T(8,128)(2,1)S(1)}, bf16[32,1024]{1,0:T(8,128)(2,1)S(1)}, u32[]{:S(2)}, u32[]{:S(2)}) collective-permute-start(bf16[32,1024]{1,0:T(8,128)(2,1)S(1)} %get-tuple-element.55), channel_id=1, source_target_pairs={{0,2},{1,3},{2,0},{3,1},{4,6},{5,7},{6,4},{7,5},{8,10},{9,11},{10,... | collective-permute-start | bytes 196616 | tf_op jit(solution)/shard_map/ppermute | solution.py:433
  23.2 2.4 %collective-permute-done.6.q2 = bf16[32,1024]{1,0:T(8,128)(2,1)S(1)} collective-permute-done((bf16[32,1024]{1,0:T(8,128)(2,1)S(1)}, bf16[32,1024]{1,0:T(8,128)(2,1)S(1)}, u32[]{:S(2)}, u32[]{:S(2)}) %collective-permute-start.6) | collective-permute-done | bytes 65568 | tf_op jit(solution)/shard_map/ppermute | solution.py:433
  35.7 2.9 %collective-permute-start.10 = (bf16[2,32,1024]{2,1,0:T(8,128)(2,1)S(1)}, bf16[2,32,1024]{2,1,0:T(8,128)(2,1)S(1)}, u32[]{:S(2)}, u32[]{:S(2)}) collective-permute-start(bf16[2,32,1024]{2,1,0:T(8,128)(2,1)S(1)} %get-tuple-element.90), channel_id=1, source_target_pairs={{0,8},{1,9},{2,10},{3,11},{4,12},{5,13},{6,14},{7,15},{8,0},{9,1},... | collective-permute-start | bytes 393224 | tf_op jit(solution)/shard_map/ppermute | solution.py:433
  38.6 2.4 %shard_map.66 = (bf16[256,1024]{1,0:T(8,128)(2,1)S(1)}, bf16[256,1024]{1,0:T(8,128)(2,1)S(1)}, bf16[256,1024]{1,0:T(8,128)(2,1)S(1)}, bf16[256,1024]{1,0:T(8,128)(2,1)S(1)}) custom-call(s32[5]{0:T(128)S(1)} %stack.71.at, bf16[2,64,8192]{2,1,0:T(8,128)(2,1)} %tokens.5, bf16[64,4096]{1,0:T(8,128)(2,1)S(1)} %collective-permute-done.mine, ...), custom_call_target="tpu_custom_call" | custom-call | tf_op jit(solution)/shard_map/pallas_call | solution.py:182
  41.1 2.4 %collective-permute-done.10 = bf16[2,32,1024]{2,1,0:T(8,128)(2,1)S(1)} collective-permute-done((bf16[2,32,1024]{2,1,0:T(8,128)(2,1)S(1)}, bf16[2,32,1024]{2,1,0:T(8,128)(2,1)S(1)}, u32[]{:S(2)}, u32[]{:S(2)}) %collective-permute-start.10) | collective-permute-done | bytes 131104 | tf_op jit(solution)/shard_map/ppermute | solution.py:433
  45.2 4.3 %collective-permute-done.11 = bf16[2,32,1024]{2,1,0:T(8,128)(2,1)S(1)} collective-permute-done((bf16[2,32,1024]{2,1,0:T(8,128)(2,1)S(1)}, bf16[2,32,1024]{2,1,0:T(8,128)(2,1)S(1)}, u32[]{:S(2)}, u32[]{:S(2)}) %collective-permute-start.11) | collective-permute-done | bytes 131104 | tf_op jit(solution)/shard_map/ppermute | solution.py:433
  51.6 2.6 %collective-permute-start.4 = (bf16[256,1024]{1,0:T(8,128)(2,1)S(1)}, bf16[256,1024]{1,0:T(8,128)(2,1)S(1)}, u32[]{:S(2)}, u32[]{:S(2)}) collective-permute-start(bf16[256,1024]{1,0:T(8,128)(2,1)S(1)} %get-tuple-element.52), channel_id=1, source_target_pairs={{0,12},{1,13},{2,14},{3,15},{4,0},{5,1},{6,2},{7,3},{8,4},{9,5},{1... | collective-permute-start | bytes 1572872 | tf_op jit(solution)/shard_map/ppermute | solution.py:433
  56.4 2.5 %collective-permute-start.14 = (bf16[4,2,32,1024]{3,2,1,0:T(8,128)(2,1)S(1)}, bf16[4,2,32,1024]{3,2,1,0:T(8,128)(2,1)S(1)}, u32[]{:S(2)}, u32[]{:S(2)}) collective-permute-start(bf16[4,2,32,1024]{3,2,1,0:T(8,128)(2,1)S(1)} %pad_maximum_fusion.n0), channel_id=1, source_target_pairs={{0,3},{1,0},{2,1},{3,2},{4,7},{5,4},{6,5},{7,6},{8,11},{9,8},{10,9... | collective-permute-start | bytes 1572872 | tf_op jit(solution)/shard_map/ppermute | solution.py:433
  58.9 7.0 %collective-permute-done.3.refs_2_ = bf16[256,1024]{1,0:T(8,128)(2,1)S(1)} collective-permute-done((bf16[256,1024]{1,0:T(8,128)(2,1)S(1)}, bf16[256,1024]{1,0:T(8,128)(2,1)S(1)}, u32[]{:S(2)}, u32[]{:S(2)}) %collective-permute-start.3) | collective-permute-done | bytes 524320 | tf_op jit(solution)/shard_map/ppermute | solution.py:433
  65.9 9.4 %collective-permute-done.4.refs_3_ = bf16[256,1024]{1,0:T(8,128)(2,1)S(1)} collective-permute-done((bf16[256,1024]{1,0:T(8,128)(2,1)S(1)}, bf16[256,1024]{1,0:T(8,128)(2,1)S(1)}, u32[]{:S(2)}, u32[]{:S(2)}) %collective-permute-start.4) | collective-permute-done | bytes 524320 | tf_op jit(solution)/shard_map/ppermute | solution.py:433
  77.1 3.6 %collective-permute-start.26 = (bf16[128,1024]{1,0:T(8,128)(2,1)S(1)}, bf16[128,1024]{1,0:T(8,128)(2,1)S(1)}, u32[]{:S(2)}, u32[]{:S(2)}) collective-permute-start(bf16[128,1024]{1,0:T(8,128)(2,1)S(1)} %get-tuple-element.65), channel_id=1, source_target_pairs={{0,12},{1,13},{2,14},{3,15},{4,0},{5,1},{6,2},{7,3},{8,4},{9,5},{1... | collective-permute-start | bytes 786440 | tf_op jit(solution)/shard_map/ppermute | solution.py:433
  84.5 2.4 %collective-permute-start.22 = (bf16[128,1024]{1,0:T(8,128)(2,1)S(1)}, bf16[128,1024]{1,0:T(8,128)(2,1)S(1)}, u32[]{:S(2)}, u32[]{:S(2)}) collective-permute-start(bf16[128,1024]{1,0:T(8,128)(2,1)S(1)} %get-tuple-element.59), channel_id=1, source_target_pairs={{0,12},{1,13},{2,14},{3,15},{4,0},{5,1},{6,2},{7,3},{8,4},{9,5},{1... | collective-permute-start | bytes 786440 | tf_op jit(solution)/shard_map/ppermute | solution.py:433
  88.7 2.7 %collective-permute-done.28.m3 = bf16[128,1024]{1,0:T(8,128)(2,1)S(1)} collective-permute-done((bf16[128,1024]{1,0:T(8,128)(2,1)S(1)}, bf16[128,1024]{1,0:T(8,128)(2,1)S(1)}, u32[]{:S(2)}, u32[]{:S(2)}) %collective-permute-start.28) | collective-permute-done | bytes 262176 | tf_op jit(solution)/shard_map/ppermute | solution.py:433
  95.5 6.9 %collective-permute-done.24.m3 = bf16[128,1024]{1,0:T(8,128)(2,1)S(1)} collective-permute-done((bf16[128,1024]{1,0:T(8,128)(2,1)S(1)}, bf16[128,1024]{1,0:T(8,128)(2,1)S(1)}, u32[]{:S(2)}, u32[]{:S(2)}) %collective-permute-start.24) | collective-permute-done | bytes 262176 | tf_op jit(solution)/shard_map/ppermute | solution.py:433
  111.3 5.5 %collective-permute-start.31 = (bf16[64,1024]{1,0:T(8,128)(2,1)S(1)}, bf16[64,1024]{1,0:T(8,128)(2,1)S(1)}, u32[]{:S(2)}, u32[]{:S(2)}) collective-permute-start(bf16[64,1024]{1,0:T(8,128)(2,1)S(1)} %get-tuple-element.73), channel_id=1, source_target_pairs={{0,64},{1,65},{2,66},{3,67},{4,68},{5,69},{6,70},{7,71},{8,72},{9,... | collective-permute-start | bytes 393224 | tf_op jit(solution)/shard_map/ppermute | solution.py:433
  119.8 3.1 %shard_map.78 = (f32[2,64,1024]{2,1,0:T(8,128)S(1)}, f32[2,64,1024]{2,1,0:T(8,128)S(1)}, f32[2,64,128]{2,1,0:T(8,128)S(1)}, bf16[64,512]{1,0:T(8,128)(2,1)S(1)},...) custom-call(s32[5]{0:T(128)S(1)} %stack.71.at, ...), custom_call_target="tpu_custom_call" | custom-call | tf_op jit(solution)/shard_map/pallas_call | solution.py:402
  126.2 6.5 %collective-permute-done.38.g_in = bf16[64,1024]{1,0:T(8,128)(2,1)S(1)} collective-permute-done((bf16[64,1024]{1,0:T(8,128)(2,1)S(1)}, bf16[64,1024]{1,0:T(8,128)(2,1)S(1)}, u32[]{:S(2)}, u32[]{:S(2)}) %collective-permute-start.38) | collective-permute-done | bytes 131104 | tf_op jit(solution)/shard_map/ppermute | solution.py:433
  136.0 3.4 %collective-permute-start.36 = (bf16[2,128,512]{2,1,0:T(8,128)(2,1)S(1)}, bf16[2,128,512]{2,1,0:T(8,128)(2,1)S(1)}, u32[]{:S(2)}, u32[]{:S(2)}) collective-permute-start(bf16[2,128,512]{2,1,0:T(8,128)(2,1)S(1)} %pad_maximum_fusion.1.refs_4_), channel_id=1, source_target_pairs={{0,8},{1,9},{2,10},{3,11},{4,12},{5,13},{6,14},{7,15},{8,0},{9,1},... | collective-permute-start | bytes 786440 | tf_op jit(solution)/shard_map/ppermute | solution.py:433
  143.7 2.7 %collective-permute-start.46 = (bf16[128,1024]{1,0:T(8,128)(2,1)S(1)}, bf16[128,1024]{1,0:T(8,128)(2,1)S(1)}, u32[]{:S(2)}, u32[]{:S(2)}) collective-permute-start(bf16[128,1024]{1,0:T(8,128)(2,1)S(1)} %constant_dynamic-update-slice_fusion.2.refs_4_), channel_id=1, source_target_pairs={{0,8},{1,9},{2,10},{3,11},{4,12},{5,13},{6,14},{7,15},{8,0},{9,1},... | collective-permute-start | bytes 786440 | tf_op jit(solution)/shard_map/ppermute | solution.py:433
  155.0 2.8 %collective-permute-done.41.refs_2_ = bf16[128,1024]{1,0:T(8,128)(2,1)S(1)} collective-permute-done((bf16[128,1024]{1,0:T(8,128)(2,1)S(1)}, bf16[128,1024]{1,0:T(8,128)(2,1)S(1)}, u32[]{:S(2)}, u32[]{:S(2)}) %collective-permute-start.41) | collective-permute-done | bytes 262176 | tf_op jit(solution)/shard_map/ppermute | solution.py:433
  163.6 2.5 %collective-permute-start.50 = (bf16[256,1024]{1,0:T(8,128)(2,1)S(1)}, bf16[256,1024]{1,0:T(8,128)(2,1)S(1)}, u32[]{:S(2)}, u32[]{:S(2)}) collective-permute-start(bf16[256,1024]{1,0:T(8,128)(2,1)S(1)} %get-tuple-element.88), channel_id=1, source_target_pairs={{0,3},{1,0},{2,1},{3,2},{4,7},{5,4},{6,5},{7,6},{8,11},{9,8},{10,9... | collective-permute-start | bytes 1572872 | tf_op jit(solution)/shard_map/ppermute | solution.py:433
  169.6 3.6 %collective-permute-done.48.refs_1_ = bf16[256,1024]{1,0:T(8,128)(2,1)S(1)} collective-permute-done((bf16[256,1024]{1,0:T(8,128)(2,1)S(1)}, bf16[256,1024]{1,0:T(8,128)(2,1)S(1)}, u32[]{:S(2)}, u32[]{:S(2)}) %collective-permute-start.48) | collective-permute-done | bytes 524320 | tf_op jit(solution)/shard_map/ppermute | solution.py:433
  173.3 5.2 %collective-permute-done.50.refs_3_ = bf16[256,1024]{1,0:T(8,128)(2,1)S(1)} collective-permute-done((bf16[256,1024]{1,0:T(8,128)(2,1)S(1)}, bf16[256,1024]{1,0:T(8,128)(2,1)S(1)}, u32[]{:S(2)}, u32[]{:S(2)}) %collective-permute-start.50) | collective-permute-done | bytes 524320 | tf_op jit(solution)/shard_map/ppermute | solution.py:433
  (122 shorter events, 79.7 us)
Async XLA Ops:
  1.7 14.1 %collective-permute-start = (bf16[64,4096]{1,0:T(8,128)(2,1)S(1)}, bf16[64,4096]{1,0:T(8,128)(2,1)S(1)}, u32[]{:S(2)}, u32[]{:S(2)}) collective-permute-start(bf16[64,4096]{1,0:T(8,128)(2,1)S(1)} %shard_map.65), channel_id=1, source_target_pairs={{0,16},{1,17},{2,18},{3,19},{4,20},{5,21},{6,22},{7,23},{8,24},{9,... | collective-permute-start | bytes 1572872 | tf_op jit(solution)/shard_map/ppermute | solution.py:433
  15.8 19.9 %collective-permute-start.1 = (bf16[64,4096]{1,0:T(8,128)(2,1)S(1)}, bf16[64,4096]{1,0:T(8,128)(2,1)S(1)}, u32[]{:S(2)}, u32[]{:S(2)}) collective-permute-start(bf16[64,4096]{1,0:T(8,128)(2,1)S(1)} %collective-permute-done.mine), channel_id=1, source_target_pairs={{0,32},{1,33},{2,34},{3,35},{4,36},{5,37},{6,38},{7,39},{8,40},{9,... | collective-permute-start | bytes 1572872 | tf_op jit(solution)/shard_map/ppermute | solution.py:433
  27.9 23.7 %collective-permute-start.19 = (bf16[256,1024]{1,0:T(8,128)(2,1)S(1)}, bf16[256,1024]{1,0:T(8,128)(2,1)S(1)}, u32[]{:S(2)}, u32[]{:S(2)}) collective-permute-start(bf16[256,1024]{1,0:T(8,128)(2,1)S(1)} %get-tuple-element.57.refs_4_), channel_id=1, source_target_pairs={{0,1},{1,2},{2,3},{3,0},{4,5},{5,6},{6,7},{7,4},{8,9},{9,10},{10,1... | collective-permute-start | bytes 1572872 | tf_op jit(solution)/shard_map/ppermute | solution.py:433
  30.4 10.6 %collective-permute-start.9 = (bf16[2,32,1024]{2,1,0:T(8,128)(2,1)S(1)}, bf16[2,32,1024]{2,1,0:T(8,128)(2,1)S(1)}, u32[]{:S(2)}, u32[]{:S(2)}) collective-permute-start(bf16[2,32,1024]{2,1,0:T(8,128)(2,1)S(1)} %get-tuple-element.90), channel_id=1, source_target_pairs={{0,4},{1,5},{2,6},{3,7},{4,8},{5,9},{6,10},{7,11},{8,12},{9,13},{1... | collective-permute-start | bytes 393224 | tf_op jit(solution)/shard_map/ppermute | solution.py:433
  32.1 22.2 %collective-permute-start.20 = (bf16[256,1024]{1,0:T(8,128)(2,1)S(1)}, bf16[256,1024]{1,0:T(8,128)(2,1)S(1)}, u32[]{:S(2)}, u32[]{:S(2)}) collective-permute-start(bf16[256,1024]{1,0:T(8,128)(2,1)S(1)} %get-tuple-element.57.refs_4_), channel_id=1, source_target_pairs={{0,2},{1,3},{2,0},{3,1},{4,6},{5,7},{6,4},{7,5},{8,10},{9,11},{10,... | collective-permute-start | bytes 1572872 | tf_op jit(solution)/shard_map/ppermute | solution.py:433
  34.3 20.3 %collective-permute-start.21 = (bf16[256,1024]{1,0:T(8,128)(2,1)S(1)}, bf16[256,1024]{1,0:T(8,128)(2,1)S(1)}, u32[]{:S(2)}, u32[]{:S(2)}) collective-permute-start(bf16[256,1024]{1,0:T(8,128)(2,1)S(1)} %get-tuple-element.57.refs_4_), channel_id=1, source_target_pairs={{0,3},{1,0},{2,1},{3,2},{4,7},{5,4},{6,5},{7,6},{8,11},{9,8},{10,9... | collective-permute-start | bytes 1572872 | tf_op jit(solution)/shard_map/ppermute | solution.py:433
  41.0 15.4 %collective-permute-start.2 = (bf16[256,1024]{1,0:T(8,128)(2,1)S(1)}, bf16[256,1024]{1,0:T(8,128)(2,1)S(1)}, u32[]{:S(2)}, u32[]{:S(2)}) collective-permute-start(bf16[256,1024]{1,0:T(8,128)(2,1)S(1)} %get-tuple-element.50), channel_id=1, source_target_pairs={{0,4},{1,5},{2,6},{3,7},{4,8},{5,9},{6,10},{7,11},{8,12},{9,13},{1... | collective-permute-start | bytes 1572872 | tf_op jit(solution)/shard_map/ppermute | solution.py:433
  49.5 16.4 %collective-permute-start.3 = (bf16[256,1024]{1,0:T(8,128)(2,1)S(1)}, bf16[256,1024]{1,0:T(8,128)(2,1)S(1)}, u32[]{:S(2)}, u32[]{:S(2)}) collective-permute-start(bf16[256,1024]{1,0:T(8,128)(2,1)S(1)} %get-tuple-element.51), channel_id=1, source_target_pairs={{0,8},{1,9},{2,10},{3,11},{4,12},{5,13},{6,14},{7,15},{8,0},{9,1},... | collective-permute-start | bytes 1572872 | tf_op jit(solution)/shard_map/ppermute | solution.py:433
  51.6 23.8 %collective-permute-start.4 = (bf16[256,1024]{1,0:T(8,128)(2,1)S(1)}, bf16[256,1024]{1,0:T(8,128)(2,1)S(1)}, u32[]{:S(2)}, u32[]{:S(2)}) collective-permute-start(bf16[256,1024]{1,0:T(8,128)(2,1)S(1)} %get-tuple-element.52), channel_id=1, source_target_pairs={{0,12},{1,13},{2,14},{3,15},{4,0},{5,1},{6,2},{7,3},{8,4},{9,5},{1... | collective-permute-start | bytes 1572872 | tf_op jit(solution)/shard_map/ppermute | solution.py:433
  54.3 29.3 %collective-permute-start.12 = (bf16[4,2,32,1024]{3,2,1,0:T(8,128)(2,1)S(1)}, bf16[4,2,32,1024]{3,2,1,0:T(8,128)(2,1)S(1)}, u32[]{:S(2)}, u32[]{:S(2)}) collective-permute-start(bf16[4,2,32,1024]{3,2,1,0:T(8,128)(2,1)S(1)} %pad_maximum_fusion.n0), channel_id=1, source_target_pairs={{0,1},{1,2},{2,3},{3,0},{4,5},{5,6},{6,7},{7,4},{8,9},{9,10},{10,1... | collective-permute-start | bytes 1572872 | tf_op jit(solution)/shard_map/ppermute | solution.py:433
  54.6 29.9 %collective-permute-start.13 = (bf16[4,2,32,1024]{3,2,1,0:T(8,128)(2,1)S(1)}, bf16[4,2,32,1024]{3,2,1,0:T(8,128)(2,1)S(1)}, u32[]{:S(2)}, u32[]{:S(2)}) collective-permute-start(bf16[4,2,32,1024]{3,2,1,0:T(8,128)(2,1)S(1)} %pad_maximum_fusion.n0), channel_id=1, source_target_pairs={{0,2},{1,3},{2,0},{3,1},{4,6},{5,7},{6,4},{7,5},{8,10},{9,11},{10,... | collective-permute-start | bytes 1572872 | tf_op jit(solution)/shard_map/ppermute | solution.py:433
  56.4 30.5 %collective-permute-start.14 = (bf16[4,2,32,1024]{3,2,1,0:T(8,128)(2,1)S(1)}, bf16[4,2,32,1024]{3,2,1,0:T(8,128)(2,1)S(1)}, u32[]{:S(2)}, u32[]{:S(2)}) collective-permute-start(bf16[4,2,32,1024]{3,2,1,0:T(8,128)(2,1)S(1)} %pad_maximum_fusion.n0), channel_id=1, source_target_pairs={{0,3},{1,0},{2,1},{3,2},{4,7},{5,4},{6,5},{7,6},{8,11},{9,8},{10,9... | collective-permute-start | bytes 1572872 | tf_op jit(solution)/shard_map/ppermute | solution.py:433
  77.1 11.0 %collective-permute-start.26 = (bf16[128,1024]{1,0:T(8,128)(2,1)S(1)}, bf16[128,1024]{1,0:T(8,128)(2,1)S(1)}, u32[]{:S(2)}, u32[]{:S(2)}) collective-permute-start(bf16[128,1024]{1,0:T(8,128)(2,1)S(1)} %get-tuple-element.65), channel_id=1, source_target_pairs={{0,12},{1,13},{2,14},{3,15},{4,0},{5,1},{6,2},{7,3},{8,4},{9,5},{1... | collective-permute-start | bytes 786440 | tf_op jit(solution)/shard_map/ppermute | solution.py:433
  88.2 15.9 %collective-permute-start.15 = (bf16[4,2,32,1024]{3,2,1,0:T(8,128)(2,1)S(1)}, bf16[4,2,32,1024]{3,2,1,0:T(8,128)(2,1)S(1)}, u32[]{:S(2)}, u32[]{:S(2)}) collective-permute-start(bf16[4,2,32,1024]{3,2,1,0:T(8,128)(2,1)S(1)} %pad_maximum_fusion.n0), channel_id=1, source_target_pairs={{0,32},{1,33},{2,34},{3,35},{4,36},{5,37},{6,38},{7,39},{8,40},{9,... | collective-permute-start | bytes 1572872 | tf_op jit(solution)/shard_map/ppermute | solution.py:433
  88.6 15.6 %collective-permute-start.16 = (bf16[4,2,32,1024]{3,2,1,0:T(8,128)(2,1)S(1)}, bf16[4,2,32,1024]{3,2,1,0:T(8,128)(2,1)S(1)}, u32[]{:S(2)}, u32[]{:S(2)}) collective-permute-start(bf16[4,2,32,1024]{3,2,1,0:T(8,128)(2,1)S(1)} %collective-permute-done.12.n1), channel_id=1, source_target_pairs={{0,32},{1,33},{2,34},{3,35},{4,36},{5,37},{6,38},{7,39},{8,40},{9,... | collective-permute-start | bytes 1572872 | tf_op jit(solution)/shard_map/ppermute | solution.py:433
  91.4 15.1 %collective-permute-start.17 = (bf16[4,2,32,1024]{3,2,1,0:T(8,128)(2,1)S(1)}, bf16[4,2,32,1024]{3,2,1,0:T(8,128)(2,1)S(1)}, u32[]{:S(2)}, u32[]{:S(2)}) collective-permute-start(bf16[4,2,32,1024]{3,2,1,0:T(8,128)(2,1)S(1)} %collective-permute-done.13.n2), channel_id=1, source_target_pairs={{0,32},{1,33},{2,34},{3,35},{4,36},{5,37},{6,38},{7,39},{8,40},{9,... | collective-permute-start | bytes 1572872 | tf_op jit(solution)/shard_map/ppermute | solution.py:433
  93.6 12.9 %collective-permute-start.18 = (bf16[4,2,32,1024]{3,2,1,0:T(8,128)(2,1)S(1)}, bf16[4,2,32,1024]{3,2,1,0:T(8,128)(2,1)S(1)}, u32[]{:S(2)}, u32[]{:S(2)}) collective-permute-start(bf16[4,2,32,1024]{3,2,1,0:T(8,128)(2,1)S(1)} %collective-permute-done.14.n3), channel_id=1, source_target_pairs={{0,32},{1,33},{2,34},{3,35},{4,36},{5,37},{6,38},{7,39},{8,40},{9,... | collective-permute-start | bytes 1572872 | tf_op jit(solution)/shard_map/ppermute | solution.py:433
  124.3 11.1 %collective-permute-start.33 = (bf16[64,512]{1,0:T(8,128)(2,1)S(1)}, bf16[64,512]{1,0:T(8,128)(2,1)S(1)}, u32[]{:S(2)}, u32[]{:S(2)}) collective-permute-start(bf16[64,512]{1,0:T(8,128)(2,1)S(1)} %get-tuple-element.77), channel_id=1, source_target_pairs={{0,16},{1,17},{2,18},{3,19},{4,20},{5,21},{6,22},{7,23},{8,24},{9,... | collective-permute-start | bytes 196616 | tf_op jit(solution)/shard_map/ppermute | solution.py:433
  135.6 10.9 %collective-permute-start.35 = (bf16[2,128,512]{2,1,0:T(8,128)(2,1)S(1)}, bf16[2,128,512]{2,1,0:T(8,128)(2,1)S(1)}, u32[]{:S(2)}, u32[]{:S(2)}) collective-permute-start(bf16[2,128,512]{2,1,0:T(8,128)(2,1)S(1)} %pad_maximum_fusion.1.refs_4_), channel_id=1, source_target_pairs={{0,4},{1,5},{2,6},{3,7},{4,8},{5,9},{6,10},{7,11},{8,12},{9,13},{1... | collective-permute-start | bytes 786440 | tf_op jit(solution)/shard_map/ppermute | solution.py:433
  136.0 10.6 %collective-permute-start.36 = (bf16[2,128,512]{2,1,0:T(8,128)(2,1)S(1)}, bf16[2,128,512]{2,1,0:T(8,128)(2,1)S(1)}, u32[]{:S(2)}, u32[]{:S(2)}) collective-permute-start(bf16[2,128,512]{2,1,0:T(8,128)(2,1)S(1)} %pad_maximum_fusion.1.refs_4_), channel_id=1, source_target_pairs={{0,8},{1,9},{2,10},{3,11},{4,12},{5,13},{6,14},{7,15},{8,0},{9,1},... | collective-permute-start | bytes 786440 | tf_op jit(solution)/shard_map/ppermute | solution.py:433
  149.4 10.3 %collective-permute-start.42 = (bf16[128,1024]{1,0:T(8,128)(2,1)S(1)}, bf16[128,1024]{1,0:T(8,128)(2,1)S(1)}, u32[]{:S(2)}, u32[]{:S(2)}) collective-permute-start(bf16[128,1024]{1,0:T(8,128)(2,1)S(1)} %constant_dynamic-update-slice_fusion.refs_0_), channel_id=1, source_target_pairs={{0,12},{1,13},{2,14},{3,15},{4,0},{5,1},{6,2},{7,3},{8,4},{9,5},{1... | collective-permute-start | bytes 786440 | tf_op jit(solution)/shard_map/ppermute | solution.py:433
  162.8 10.5 %collective-permute-start.48 = (bf16[256,1024]{1,0:T(8,128)(2,1)S(1)}, bf16[256,1024]{1,0:T(8,128)(2,1)S(1)}, u32[]{:S(2)}, u32[]{:S(2)}) collective-permute-start(bf16[256,1024]{1,0:T(8,128)(2,1)S(1)} %get-tuple-element.86), channel_id=1, source_target_pairs={{0,1},{1,2},{2,3},{3,0},{4,5},{5,6},{6,7},{7,4},{8,9},{9,10},{10,1... | collective-permute-start | bytes 1572872 | tf_op jit(solution)/shard_map/ppermute | solution.py:433
  163.6 14.8 %collective-permute-start.50 = (bf16[256,1024]{1,0:T(8,128)(2,1)S(1)}, bf16[256,1024]{1,0:T(8,128)(2,1)S(1)}, u32[]{:S(2)}, u32[]{:S(2)}) collective-permute-start(bf16[256,1024]{1,0:T(8,128)(2,1)S(1)} %get-tuple-element.88), channel_id=1, source_target_pairs={{0,3},{1,0},{2,1},{3,2},{4,7},{5,4},{6,5},{7,6},{8,11},{9,8},{10,9... | collective-permute-start | bytes 1572872 | tf_op jit(solution)/shard_map/ppermute | solution.py:433
  166.1 13.7 %collective-permute-start.49 = (bf16[256,1024]{1,0:T(8,128)(2,1)S(1)}, bf16[256,1024]{1,0:T(8,128)(2,1)S(1)}, u32[]{:S(2)}, u32[]{:S(2)}) collective-permute-start(bf16[256,1024]{1,0:T(8,128)(2,1)S(1)} %get-tuple-element.87), channel_id=1, source_target_pairs={{0,2},{1,3},{2,0},{3,1},{4,6},{5,7},{6,4},{7,5},{8,10},{9,11},{10,... | collective-permute-start | bytes 1572872 | tf_op jit(solution)/shard_map/ppermute | solution.py:433
  (33 other events, 297.0 us)
